TPU v7x, 512 devices: a whole 4x4x16 slice. The times are simulated.
512 devices in a mesh: box: 32 (over x, y, core), dir: 16 (over z).
Axes of the slice: x: 4, y: 4, z: 16, core: 2. Of those that a mesh axis runs over, the one named last changes fastest.
Arguments:
- outgoing: float32 [2048, 8, 2048], P(('box', 'dir')), may hold values from -6 to 6
- fine_slot: int32 [2048], P('box'), may hold values from 0 to 2047, as said below
- translator: float32 [316, 2, 8192], P(None, None, 'dir'), may hold values from -0.4 to 0.4
- list_partner: int32 [256, 189], replicated, may hold values from 0 to 255
- list_kind: int32 [256, 189], replicated, may hold values from 0 to 315
- list_count: int32 [256], replicated, may hold values from 63 to 189, as said below
Outputs:
- fine_incoming: float32 [2048, 8, 2048], P(('box', 'dir'))
Inputs may be any that keep to these rules, and one draw needn't show every extreme that they name: `fine_slot`: the fine boxes 8 * 8 * g to 8 * 8 * (g + 1) - 1 carry each of the values 8 * 8 * g to 8 * 8 * (g + 1) - 1 exactly once, so every parent has its 8 children, one in each octant, within that group. Slots from list_count[p] on are ignored.
All inputs are finite; a program needn't handle non-finite values.
Results may differ from a plain program's by a relative error of at most 0.0003.
Values sent between devices are 32-bit elements; how exact they have to be, the bound alone decides.
No kernel may reach another device: no remote copies, remote signals or barrier semaphores. Data moves between devices by JAX's collectives and lax.ppermute only.
A program may use at most 64 MiB of HBM per device.

v0:
```python
import jax
import jax.numpy as jnp
from jax import lax
from jax.sharding import PartitionSpec as P

TF = 32
PF = 64
TP = 64
PP = 128


wave_shift = 5.0
highest = lax.Precision.HIGHEST


def theta_table(fine_count, coarse_count):
    fine_angle = (jnp.arange(fine_count, dtype=jnp.float32) + 0.5) * (jnp.pi / fine_count)
    coarse_angle = (jnp.arange(coarse_count, dtype=jnp.float32) + 0.5) * (jnp.pi / coarse_count)
    orders = jnp.arange(1, fine_count, dtype=jnp.float32)
    products = jnp.cos(coarse_angle[:, None, None] * orders) * jnp.cos(
        fine_angle[None, :, None] * orders
    )
    return (1.0 + 2.0 * jnp.sum(products, axis=2)) / fine_count


def phi_table(fine_count, coarse_count):
    fine_angle = jnp.arange(fine_count, dtype=jnp.float32) * (2.0 * jnp.pi / fine_count)
    coarse_angle = jnp.arange(coarse_count, dtype=jnp.float32) * (2.0 * jnp.pi / coarse_count)
    offset = coarse_angle[:, None] - fine_angle[None, :]
    orders = jnp.arange(1, fine_count // 2, dtype=jnp.float32)
    series = jnp.sum(jnp.cos(offset[:, :, None] * orders), axis=2)
    return (1.0 + 2.0 * series + jnp.cos(offset * (fine_count // 2))) / fine_count


def octant_phase(octant, first_theta, theta_count, coarse_theta, coarse_phi):
    theta_index = first_theta + jnp.arange(theta_count, dtype=jnp.int32)
    polar = (theta_index.astype(jnp.float32) + 0.5) * (jnp.pi / coarse_theta)
    azimuth = jnp.arange(coarse_phi, dtype=jnp.float32) * (2.0 * jnp.pi / coarse_phi)
    along_x = jnp.sin(polar)[:, None] * jnp.cos(azimuth)[None, :]
    along_y = jnp.sin(polar)[:, None] * jnp.sin(azimuth)[None, :]
    along_z = jnp.cos(polar)[:, None] + 0.0 * azimuth[None, :]
    sign_x = (2 * (octant % 2) - 1).astype(jnp.float32)
    sign_y = (2 * (octant // 2 % 2) - 1).astype(jnp.float32)
    sign_z = (2 * (octant // 4) - 1).astype(jnp.float32)
    phase_angle = wave_shift * (
        sign_x[:, None, None] * along_x[None]
        + sign_y[:, None, None] * along_y[None]
        + sign_z[:, None, None] * along_z[None]
    )
    return (jnp.cos(phase_angle), jnp.sin(phase_angle))


def translate(sources, kernel_table, partner, kind, count):
    targets, length = partner.shape
    source_rows, _, excite, lanes = sources.shape
    kinds = kernel_table.shape[0]
    blocks = 7
    block_width = length // blocks
    flat_sources = sources.reshape(source_rows, 2 * excite * lanes)
    flat_kernel = kernel_table.reshape(kinds, 2 * lanes)
    source_ids = jnp.arange(source_rows, dtype=jnp.int32)
    kind_ids = jnp.arange(kinds, dtype=jnp.int32)

    def add_block(block_step, running):
        begin_at = block_step * block_width
        near_rows = lax.dynamic_slice_in_dim(partner, begin_at, block_width, 1)
        kind_rows = lax.dynamic_slice_in_dim(kind, begin_at, block_width, 1)
        position = begin_at + jnp.arange(block_width, dtype=jnp.int32)
        alive_mask = (position[None, :] < count[:, None]).astype(jnp.float32)
        select_source = (
            (near_rows[:, :, None] == source_ids)
            .astype(jnp.float32)
            .reshape(targets * block_width, source_rows)
        )
        select_kind = (
            (kind_rows[:, :, None] == kind_ids).astype(jnp.float32) * alive_mask[:, :, None]
        ).reshape(targets * block_width, kinds)
        picked = jnp.dot(
            select_source, flat_sources, precision=highest, preferred_element_type=jnp.float32
        )
        picked = picked.reshape(targets, block_width, 2, excite, lanes)
        factor = jnp.dot(
            select_kind, flat_kernel, precision=highest, preferred_element_type=jnp.float32
        )
        factor = factor.reshape(targets, block_width, 2, 1, lanes)
        along_real = factor[:, :, 0]
        along_imag = factor[:, :, 1]
        real_part = picked[:, :, 0]
        imag_part = picked[:, :, 1]
        new_real = jnp.sum(along_real * real_part - along_imag * imag_part, axis=1)
        new_imag = jnp.sum(along_real * imag_part + along_imag * real_part, axis=1)
        return running + jnp.stack([new_real, new_imag], axis=1)

    initial = jnp.zeros((targets, 2, excite, lanes), jnp.float32)
    return lax.fori_loop(0, blocks, add_block, initial)


def body(outgoing, fine_slot, translator, list_partner, list_kind, list_count):
    dir_count = lax.axis_size("dir")
    box_index = lax.axis_index("box")
    dir_index = lax.axis_index("dir")
    channels = outgoing.shape[1]
    excite = channels // 2
    fine_here = outgoing.shape[0]
    row_boxes = fine_slot.shape[0]
    parents_here = row_boxes // 8
    theta_here = TP // dir_count
    dirs_here = translator.shape[2]
    up_theta = theta_table(TF, TP)
    up_phi = phi_table(PF, PP)
    octant = fine_slot % 8
    local_parent = fine_slot // 8 % parents_here
    onehot = (local_parent[None, :] == jnp.arange(parents_here, dtype=jnp.int32)[:, None]).astype(
        jnp.float32
    )
    cos_table, sin_table = octant_phase(octant, dir_index * theta_here, theta_here, TP, PP)
    cos_table = cos_table[:, :, None, :]
    sin_table = sin_table[:, :, None, :]
    pattern = outgoing.reshape(fine_here, channels, TF, PF)
    raised = jnp.einsum("ut,fctp->fcup", up_theta, pattern, precision=highest)
    raised = jnp.einsum("qp,fcup->fucq", up_phi, raised, precision=highest)
    spread = lax.all_to_all(raised, "dir", split_axis=1, concat_axis=0, tiled=True)
    real_part = spread[:, :, :excite]
    imag_part = spread[:, :, excite:]
    shifted = jnp.concatenate(
        [
            real_part * cos_table + imag_part * sin_table,
            imag_part * cos_table - real_part * sin_table,
        ],
        axis=2,
    )
    parent_out = jnp.einsum("pf,fucq->pcuq", onehot, shifted, precision=highest)
    parent_out = parent_out.reshape(parents_here, channels, dirs_here)
    everyone = lax.all_gather(parent_out, "box", axis=0, tiled=True)
    everyone = everyone.reshape(everyone.shape[0], 2, excite, dirs_here)
    first_parent = box_index * parents_here
    mine_partner = lax.dynamic_slice_in_dim(list_partner, first_parent, parents_here, 0)
    mine_kind = lax.dynamic_slice_in_dim(list_kind, first_parent, parents_here, 0)
    mine_count = lax.dynamic_slice_in_dim(list_count, first_parent, parents_here, 0)
    incoming = translate(everyone, translator, mine_partner, mine_kind, mine_count)
    incoming = incoming.reshape(parents_here, channels, dirs_here)
    fields = incoming.reshape(parents_here, channels, theta_here, PP)
    spread_back = jnp.einsum("pf,pcuq->fucq", onehot, fields, precision=highest)
    real_part = spread_back[:, :, :excite]
    imag_part = spread_back[:, :, excite:]
    shifted_back = jnp.concatenate(
        [
            real_part * cos_table - imag_part * sin_table,
            imag_part * cos_table + real_part * sin_table,
        ],
        axis=2,
    )
    arrived_back = lax.all_to_all(shifted_back, "dir", split_axis=0, concat_axis=1, tiled=True)
    arrived_back = jnp.einsum("qp,fucq->fucp", up_phi, arrived_back, precision=highest) * (PF / PP)
    result = jnp.einsum("ut,fucp->fctp", up_theta, arrived_back, precision=highest) * (TF / TP)
    return result.reshape(fine_here, channels, TF * PF)


def solution(mesh):
    placed = (P(("box", "dir"), None, None), P("box"), P(None, None, "dir"), P(), P(), P())
    return jax.shard_map(
        body, mesh=mesh, in_specs=placed, out_specs=P(("box", "dir"), None, None), check_vma=False
    )
```

profile of v0, /device:TPU:32, one launch (start us, length us, event | category | flops | bytes accessed | tf_op | source)
XLA Modules:
  0.0 271.5 jit_solution(12876599583716240283)
XLA Ops:
  6.7 3.3 %cosine_reduce_fusion = f32[128,64]{0,1:T(8,128)S(1)} fusion(f32[31]{0:T(128)S(1)} %iota_add_fusion.1, f32[128,64]{0,1:T(8,128)S(1)} %broadcast_subtract_fusion), kind=kLoop, calls=%fused_computation.39 | loop fusion | flops 499712 | bytes 65660 | tf_op jit(solution)/shard_map/reduce_sum | solution.py:31
  12.7 1.2 convolution_bitcast_fusion.3
  13.9 1.6 copy.57
  15.4 15.2 %all-to-all-start = ((f32[4,64,8,128]{3,2,0,1:T(8,128)}), f32[4,64,8,128]{3,2,0,1:T(8,128)S(1)}, u32[]{:S(2)}, u32[]{:S(2)}) async-start(f32[4,64,8,128]{3,2,0,1:T(8,128)} %copy.57), calls=%async_computation | async-start | bytes 2097152 | tf_op jit(solution)/shard_map/all_to_all | solution.py:122
  31.8 48.2 %all-to-all-done = f32[4,64,8,128]{3,2,0,1:T(8,128)S(1)} async-done(((f32[4,64,8,128]{3,2,0,1:T(8,128)}), f32[4,64,8,128]{3,2,0,1:T(8,128)S(1)}, u32[]{:S(2)}, u32[]{:S(2)}) %all-to-all-start) | async-done | bytes 1048608 | tf_op jit(solution)/shard_map/all_to_all | solution.py:122
  82.8 57.8 %all-gather.2.cloned.1.call-done = f32[256,8,512]{2,1,0:T(8,128)} async-done(((f32[8,8,512]{2,1,0:T(8,128)}), f32[256,8,512]{2,1,0:T(8,128)}) %all-gather.2.cloned.1.call-update) | async-done | bytes 4194320 | tf_op jit(solution)/shard_map/all_gather | solution.py:134
  140.6 5.2 %copy.73 = f32[256,8,512]{0,2,1:T(8,128)} copy(f32[256,8,512]{2,1,0:T(8,128)} %all-gather.2.cloned.1.call-done) | data formatting | bytes 8388608
  145.8 49.8 %while.14 = (s32[]{:T(128)}, f32[8,2,4,512]{3,2,1,0:T(4,128)S(1)}, s32[8,189]{1,0:T(8,128)S(1)}, s32[8]{0:T(128)S(1)}, f32[316,1024]{1,0:T(8,128)S(1)}, /*index=...) while((s32[]{:T(128)}, f32[8,2,4,512]{3,2,1,0:T(4,128)S(1)}, ...), condition=%wide.region_5.6_spmd.clone, body=%wide.region_2.5_spmd.clone.sunk | while | flops 3560435456 | bytes 36003004 | solution.py:95
  147.1 2.0 convolution_bitcast_fusion.6
  149.3 2.5 fusion.80
  154.2 2.0 convolution_bitcast_fusion.6
  156.4 2.5 fusion.80
  161.3 2.0 convolution_bitcast_fusion.6
  163.5 2.5 fusion.80
  168.4 2.0 convolution_bitcast_fusion.6
  170.6 2.5 fusion.80
  175.5 2.0 convolution_bitcast_fusion.6
  177.7 2.5 fusion.80
  182.6 2.0 convolution_bitcast_fusion.6
  184.8 2.5 fusion.80
  189.8 2.0 convolution_bitcast_fusion.6
  191.9 2.5 fusion.80
  197.2 64.6 %all_to_all.36 = f32[64,4,8,128]{3,2,1,0:T(8,128)S(1)} all-to-all(f32[64,4,8,128]{3,2,1,0:T(8,128)S(1)} %copy.63), channel_id=1, replica_groups=mesh['box'=32,'dir'=16] {'dir'}, dimensions={0} | all-to-all | bytes 2097152 | tf_op jit(solution)/shard_map/all_to_all | solution.py:153
  261.9 1.2 convolution_multiply_fusion
  (113 shorter events, 27.8 us)
Async XLA Ops:
  13.8 17.1 %copy-start.4 = (s32[64]{0:T(128)S(1)}, s32[64]{0:T(128)}, u32[]{:S(2)}) copy-start(s32[64]{0:T(128)} %param.9) | copy-start | bytes 772
  15.4 64.5 %all-to-all-start = ((f32[4,64,8,128]{3,2,0,1:T(8,128)}), f32[4,64,8,128]{3,2,0,1:T(8,128)S(1)}, u32[]{:S(2)}, u32[]{:S(2)}) async-start(f32[4,64,8,128]{3,2,0,1:T(8,128)} %copy.57), calls=%async_computation | async-start | bytes 2097152 | tf_op jit(solution)/shard_map/all_to_all | solution.py:122
  30.7 109.9 %all-gather.2.cloned.1.call-start = ((), (), s32[]{:S(2)}) async-start(), calls=%async_computation.2 | async-start | bytes 4325376 | tf_op jit(solution)/shard_map/all_gather | solution.py:134
  80.2 1.4 copy-start.2
  80.3 1.4 copy-start.3
  80.3 1.7 copy-start.5
  80.3 1.7 copy-start.1
  147.1 2.2 copy-start
  154.2 2.2 copy-start
  161.3 2.2 copy-start
  168.4 2.2 copy-start
  175.5 2.2 copy-start
  182.6 2.2 copy-start
  189.8 2.2 copy-start
Sparse Core Ops, SparseCore 0:
  81.8 58.7 all-gather.1
where the time goes:
time: 272 us; the launch traced here: 271 us
  waiting for transfers between devices  106 us (39%)
  blocking collectives  64.6 us (24%)
  matrix products  36.3 us (13%)
  local copies, waits for them, and re-layouts  21.3 us (8%)
  starting transfers between devices  15.4 us (6%)
  other arithmetic  13.7 us (5%)
  between operations  13.7 us (5%)
    all_to_all x1, blocking collectives, body(): lax.all_to_all(shifted_back, 'dir', split_axis=0, concat_axis=1, tiled=True)  64.6 us
    all_gather x1, waiting for transfers between devices, body(): everyone = lax.all_gather(parent_out, 'box', axis=0, tiled=True)  57.8 us
    all_to_all x1, waiting for transfers between devices, body(): lax.all_to_all(raised, 'dir', split_axis=1, concat_axis=0, tiled=True)  48.2 us
    dot_general x7, matrix products, add_block(): jnp.dot(select_source, flat_sources, precision=highest, preferred_element...  17.4 us
    all_to_all x1, starting transfers between devices, body(): lax.all_to_all(raised, 'dir', split_axis=1, concat_axis=0, tiled=True)  15.2 us
    dot_general x7, matrix products, add_block(): jnp.dot(select_kind, flat_kernel, precision=highest, preferred_element_ty...  13.8 us
    another operation x7, local copies, waits for them, and re-layouts  7.69 us
    reduce_sum x7, other arithmetic, add_block(): new_real = jnp.sum(along_real * real_part - along_imag * imag_part, axis=1)  7.42 us
  transfers between devices with their start and end apart: 2, of which 2 were waited for; matrix products, arithmetic and copies ran while one was open for 1% of the time, Pallas kernels for 0%

commit v1 on v0

v1 whole, which is shorter than its diff:
```python
import numpy as np

import jax
import jax.numpy as jnp
from jax import lax
from jax.experimental import pallas as pl
from jax.experimental.pallas import tpu as pltpu
from jax.sharding import PartitionSpec as P

TF = 32
PF = 64
TP = 64
PP = 128
LANES = 128
SLOTS = 256
KINDS = 384
TARGETS = 64
SOURCES = 256
CHUNK = 64

wave_shift = 5.0
f32 = jnp.float32
bf16 = jnp.bfloat16


def theta_matrix():
    a = (np.arange(TP) + 0.5) * np.pi / TP
    b = (np.arange(TF) + 0.5) * np.pi / TF
    m = np.arange(1, TF)
    series = np.cos(a[:, None, None] * m) * np.cos(b[None, :, None] * m)
    return (1.0 + 2.0 * series.sum(2)) / TF


def phi_matrix():
    e = 2 * np.pi * (np.arange(PP)[:, None] / PP - np.arange(PF)[None, :] / PF)
    k = np.arange(1, PF // 2)
    series = np.cos(e[:, :, None] * k).sum(2)
    return (1.0 + 2.0 * series + np.cos(e * (PF // 2))) / PF


def pair_table(matrix):
    n_out, n_in = matrix.shape
    m = matrix.reshape(n_out // 2, 2, n_in // 2, 2).transpose(0, 2, 1, 3)
    same = np.stack([m[:, :, 0, 0], m[:, :, 1, 1]], -1)
    cross = np.stack([m[:, :, 1, 0], m[:, :, 0, 1]], -1)
    table = np.repeat(np.stack([same, cross], 2), PF, axis=3)
    return table.reshape(n_out // 2, n_in, LANES).astype(np.float32)


def split(x):
    high = x.astype(bf16)
    return high, (x - high.astype(f32)).astype(bf16)


def split_constant(x):
    high = np.asarray(x, np.float32).astype(jnp.bfloat16)
    low = (np.asarray(x, np.float32) - high.astype(np.float32)).astype(jnp.bfloat16)
    return np.stack([high, low])


def swap_halves(x):
    return pltpu.roll(x, PF, x.ndim - 1)


def theta_up_kernel(x_ref, c_ref, o_ref):
    def step(z, carry):
        for part in range(2):
            j = 2 * z + part
            same = [jnp.zeros((8, LANES), f32) for _ in range(4)]
            cross = [jnp.zeros((8, LANES), f32) for _ in range(4)]
            for i in range(TF // 2):
                cs = c_ref[j, pl.ds(2 * i, 1), :]
                cx = c_ref[j, pl.ds(2 * i + 1, 1), :]
                for f in range(4):
                    v = x_ref[f, :, pl.ds(i * LANES, LANES)]
                    same[f] = same[f] + cs * v
                    cross[f] = cross[f] + cx * v
            for f in range(4):
                o_ref[z, f, :, pl.ds(part * LANES, LANES)] = same[f] + swap_halves(cross[f])
        return carry

    lax.fori_loop(0, 16, step, 0)


def theta_down_kernel(y_ref, c_ref, o_ref):
    for j in range(TF // 2):
        zero = jnp.zeros((8, LANES), f32)

        def step(z, carry):
            same, cross = list(carry[:4]), list(carry[4:])
            for part in range(2):
                i = 2 * z + part
                cs = c_ref[j, pl.ds(2 * i, 1), :]
                cx = c_ref[j, pl.ds(2 * i + 1, 1), :]
                for f in range(4):
                    v = y_ref[z, f, :, pl.ds(part * LANES, LANES)]
                    same[f] = same[f] + cs * v
                    cross[f] = cross[f] + cx * v
            return (*same, *cross)

        done = lax.fori_loop(0, 16, step, (zero,) * 8, unroll=True)
        for f in range(4):
            o_ref[f, :, pl.ds(j * LANES, LANES)] = done[f] + swap_halves(done[4 + f])


def channel_sign():
    row = lax.broadcasted_iota(jnp.int32, (8, 4 * LANES), 0)
    return jnp.where(row < 4, 1.0, -1.0).astype(f32)


def gather_kernel(slot_ref, x_ref, w_ref, cos_ref, sin_ref, after_ref, o_ref, raised_ref, parent_ref, inv_ref):
    for i in range(64):
        inv_ref[slot_ref[i] % 64] = i
    for j in range(2):
        high, low = split(x_ref[:, :, :, pl.ds(j * LANES, LANES)].reshape(512, LANES))
        wh, wl = w_ref[0], w_ref[1]
        part = (
            jnp.dot(high, wh, preferred_element_type=f32)
            + jnp.dot(low, wh, preferred_element_type=f32)
            + jnp.dot(high, wl, preferred_element_type=f32)
        )
        raised_ref[:, :, pl.ds(j * 256, 256)] = part.reshape(64, 8, 256)
    sign = channel_sign()

    def step(p, carry):
        plain = jnp.zeros((8, 512), f32)
        turned = jnp.zeros((8, 512), f32)
        for o in range(8):
            v = raised_ref[inv_ref[p * 8 + o]]
            plain = plain + v * cos_ref[pl.ds(o, 1), :]
            turned = turned + v * sin_ref[pl.ds(o, 1), :]
        parent_ref[p] = plain + sign * pltpu.roll(turned, 4, 0)
        return carry

    lax.fori_loop(0, 8, step, 0)
    low_half = lax.broadcasted_iota(jnp.int32, (8, LANES), 1) < PF
    for j in range(4):
        for block in range(4):
            a = parent_ref[j, :, pl.ds(block * LANES, LANES)]
            b = parent_ref[j + 4, :, pl.ds(block * LANES, LANES)]
            even = jnp.where(low_half, a, swap_halves(b))
            odd = jnp.where(low_half, swap_halves(a), b)
            for group in range(4):
                o_ref[group * 8 + 2 * block, j] = even
                o_ref[group * 8 + 2 * block + 1, j] = odd


def matrix_kernel(partner_ref, kind_ref, table_ref, o_ref, both_ref):
    @pl.when(pl.program_id(0) == 0)
    def _():
        high, low = split(table_ref[...])
        both_ref[:LANES] = high
        both_ref[LANES:] = low

    slot_kind = lax.broadcasted_iota(jnp.int32, (KINDS, SLOTS), 0)
    slot_source = lax.broadcasted_iota(jnp.int32, (SOURCES, SLOTS), 0)
    table = both_ref[...]

    def step(p, carry):
        pick_kind = jnp.where(slot_kind == kind_ref[pl.ds(p, 1), :], 1.0, 0.0).astype(bf16)
        pick_source = jnp.where(slot_source == partner_ref[pl.ds(p, 1), :], 1.0, 0.0).astype(bf16)
        rows = jnp.dot(table, pick_kind, preferred_element_type=f32).astype(bf16)
        both = lax.dot_general(
            pick_source, rows, (((1,), (1,)), ((), ())), preferred_element_type=f32
        )
        o_ref[p] = both[:, :LANES] + both[:, LANES:]
        return carry

    lax.fori_loop(0, 8, step, 0)


def translate_kernel(s_ref, m_ref, o_ref, wide_ref):
    low_half = lax.broadcasted_iota(jnp.int32, (8, LANES), 1) < PF

    @pl.when(pl.program_id(0) == 0)
    def _():
        def spread(b, carry):
            for j in range(4):
                v = s_ref[b, j]
                r = swap_halves(v)
                wide_ref[b * 8 + j] = jnp.where(low_half, v, r)
                wide_ref[b * 8 + j + 4] = jnp.where(low_half, r, v)
            return carry

        lax.fori_loop(0, 32, spread, 0)

    def step(q, sums):
        sums = list(sums)
        for k in range(8):
            s = q * 8 + k
            v = wide_ref[s]
            for p in range(8):
                sums[p] = sums[p] + m_ref[p, pl.ds(s, 1), :] * v
        return tuple(sums)

    sums = lax.fori_loop(0, SOURCES // 8, step, (jnp.zeros((8, LANES), f32),) * 8)
    row = lax.broadcasted_iota(jnp.int32, (8, LANES), 0)
    sign = jnp.where(row < 4, -1.0, 1.0).astype(f32)
    whole = [a + sign * pltpu.roll(swap_halves(a), 4, 0) for a in sums]
    for j in range(4):
        o_ref[0, j] = jnp.where(low_half, whole[j], swap_halves(whole[j + 4]))


def scatter_kernel(slot_ref, x_ref, w_ref, cos_ref, sin_ref, o_ref, plain_ref, turned_ref, child_ref):
    low_half = lax.broadcasted_iota(jnp.int32, (8, LANES), 1) < PF
    for block in range(4):
        for j in range(4):
            a = x_ref[2 * block, j]
            b = x_ref[2 * block + 1, j]
            first = jnp.where(low_half, a, swap_halves(b))
            second = jnp.where(low_half, swap_halves(a), b)
            plain_ref[j, :, pl.ds(block * LANES, LANES)] = first
            plain_ref[j + 4, :, pl.ds(block * LANES, LANES)] = second
    sign = channel_sign()
    for p in range(8):
        turned_ref[p] = -sign * pltpu.roll(plain_ref[p], 4, 0)

    def step(f, carry):
        s = slot_ref[f] % 64
        p = s // 8
        o = s % 8
        child_ref[f] = (
            plain_ref[p] * cos_ref[pl.ds(o, 1), :] + turned_ref[p] * sin_ref[pl.ds(o, 1), :]
        )
        return carry

    lax.fori_loop(0, 64, step, 0, unroll=4)
    for j in range(2):
        high, low = split(child_ref[:, :, pl.ds(j * 256, 256)].reshape(512, 256))
        wh, wl = w_ref[0], w_ref[1]
        part = (
            jnp.dot(high, wh, preferred_element_type=f32)
            + jnp.dot(low, wh, preferred_element_type=f32)
            + jnp.dot(high, wl, preferred_element_type=f32)
        )
        o_ref[:, :, :, pl.ds(j * LANES, LANES)] = part.reshape(16, 4, 8, LANES)


def phase_tables(dir_index):
    theta_here = TP // 16
    theta_index = dir_index * theta_here + jnp.arange(theta_here, dtype=jnp.int32)
    polar = (theta_index.astype(f32) + 0.5) * (jnp.pi / TP)
    azimuth = jnp.arange(PP, dtype=f32) * (2.0 * jnp.pi / PP)
    along_x = (jnp.sin(polar)[:, None] * jnp.cos(azimuth)[None, :]).reshape(1, 512)
    along_y = (jnp.sin(polar)[:, None] * jnp.sin(azimuth)[None, :]).reshape(1, 512)
    along_z = (jnp.cos(polar)[:, None] + 0.0 * azimuth[None, :]).reshape(1, 512)
    octant = jnp.arange(8, dtype=jnp.int32)[:, None]
    sign_x = (2 * (octant % 2) - 1).astype(f32)
    sign_y = (2 * (octant // 2 % 2) - 1).astype(f32)
    sign_z = (2 * (octant // 4) - 1).astype(f32)
    angle = wave_shift * (sign_x * along_x + sign_y * along_y + sign_z * along_z)
    return jnp.cos(angle), jnp.sin(angle)


vmem = pl.BlockSpec(memory_space=pltpu.VMEM)
smem = pl.BlockSpec(memory_space=pltpu.SMEM)


def shape(*dims):
    return jax.ShapeDtypeStruct(dims, f32)


def body(outgoing, fine_slot, translator, list_partner, list_kind, list_count):
    box_index = lax.axis_index("box")
    dir_index = lax.axis_index("dir")
    chunk = box_index % 8
    group = box_index // 8

    theta = theta_matrix()
    up = jnp.asarray(pair_table(theta))
    down = jnp.asarray(pair_table(theta.T * (TF / TP)))
    phi = phi_matrix()
    phi_up = jnp.asarray(split_constant(np.kron(np.eye(2), phi.T)))
    phi_down = jnp.asarray(split_constant(np.kron(np.eye(2), phi) * (PF / PP)))

    sent = pl.pallas_call(
        theta_up_kernel, out_shape=shape(16, 4, 8, 256), in_specs=[vmem, vmem], out_specs=vmem
    )(outgoing, up)
    spread = lax.all_to_all(sent, "dir", split_axis=0, concat_axis=0, tiled=True)

    rows = lax.dynamic_slice_in_dim(list_partner, group * TARGETS, TARGETS, 0)
    kinds = lax.dynamic_slice_in_dim(list_kind, group * TARGETS, TARGETS, 0)
    count = lax.dynamic_slice_in_dim(list_count, group * TARGETS, TARGETS, 0)
    length = rows.shape[1]
    live = jnp.arange(length, dtype=jnp.int32)[None, :] < count[:, None]
    pad = ((0, 0), (0, SLOTS - length))
    rows = jnp.pad(jnp.where(live, rows, -1), pad, constant_values=-1)
    kinds = jnp.pad(kinds, pad, constant_values=-1)
    table = lax.dynamic_slice_in_dim(translator, chunk * CHUNK, CHUNK, 2)
    table = table.reshape(table.shape[0], LANES).T
    table = jnp.pad(table, ((0, 0), (0, KINDS - table.shape[1])))
    matrix = pl.pallas_call(
        matrix_kernel,
        grid=(TARGETS // 8,),
        in_specs=[
            pl.BlockSpec((8, SLOTS), lambda i: (i, 0)),
            pl.BlockSpec((8, SLOTS), lambda i: (i, 0)),
            pl.BlockSpec((LANES, KINDS), lambda i: (0, 0)),
        ],
        out_specs=pl.BlockSpec((8, SOURCES, LANES), lambda i: (i, 0, 0)),
        out_shape=shape(TARGETS, SOURCES, LANES),
        scratch_shapes=[pltpu.VMEM((256, KINDS), bf16)],
    )(rows, kinds, table)
    cos_table, sin_table = phase_tables(dir_index)

    packed = pl.pallas_call(
        gather_kernel,
        out_shape=shape(32, 4, 8, LANES),
        in_specs=[smem, vmem, vmem, vmem, vmem, pl.BlockSpec(memory_space=pl.ANY)],
        out_specs=vmem,
        scratch_shapes=[
            pltpu.VMEM((64, 8, 512), f32),
            pltpu.VMEM((8, 8, 512), f32),
            pltpu.SMEM((64,), jnp.int32),
        ],
    )(fine_slot, spread, phi_up, cos_table, sin_table, matrix)
    everyone = lax.all_to_all(packed, "box", split_axis=0, concat_axis=0, tiled=True)
    incoming = pl.pallas_call(
        translate_kernel,
        grid=(TARGETS // 8,),
        in_specs=[
            pl.BlockSpec((32, 4, 8, LANES), lambda i: (0, 0, 0, 0)),
            pl.BlockSpec((8, SOURCES, LANES), lambda i: (i, 0, 0)),
        ],
        out_specs=pl.BlockSpec((1, 4, 8, LANES), lambda i: (i, 0, 0, 0)),
        out_shape=shape(8, 4, 8, LANES),
        scratch_shapes=[pltpu.VMEM((SOURCES, 8, LANES), f32)],
    )(everyone, matrix)
    groups = [[8 * g + k for k in range(8)] for g in range(4)]
    fields = lax.all_to_all(
        incoming, "box", split_axis=0, concat_axis=0, axis_index_groups=groups, tiled=True
    )
    lowered = pl.pallas_call(
        scatter_kernel,
        out_shape=shape(16, 4, 8, 256),
        in_specs=[smem, vmem, vmem, vmem, vmem],
        out_specs=vmem,
        scratch_shapes=[
            pltpu.VMEM((8, 8, 512), f32),
            pltpu.VMEM((8, 8, 512), f32),
            pltpu.VMEM((64, 8, 512), f32),
        ],
    )(fine_slot, fields, phi_down, cos_table, sin_table)
    back = lax.all_to_all(lowered, "dir", split_axis=0, concat_axis=0, tiled=True)
    return pl.pallas_call(
        theta_down_kernel, out_shape=shape(4, 8, TF * PF), in_specs=[vmem, vmem], out_specs=vmem
    )(back, down)


def solution(mesh):
    placed = (P(("box", "dir"), None, None), P("box"), P(None, None, "dir"), P(), P(), P())
    return jax.shard_map(
        body, mesh=mesh, in_specs=placed, out_specs=P(("box", "dir"), None, None), check_vma=False
    )
```

time: 272 us -> 144 us (0.53)
  waiting for transfers between devices: 106 us -> 0.01 us
  Pallas kernels: 0 us -> 54 us
  matrix products: 36.3 us -> 0 us
  local copies, waits for them, and re-layouts: 21.3 us -> 3.72 us
  between operations: 13.7 us -> 0.07 us
  other arithmetic: 13.7 us -> 1.1 us
  blocking collectives: 64.6 us -> 68.7 us
    all_gather x1 -> x0, waiting for transfers between devices: 57.8 us -> none  [body(): everyone = lax.all_gather(parent_out, 'box', axis=0, tiled=True)]
    pallas_call x0 -> x6, Pallas kernels: none -> 54 us  [the longest x1 28.2 us: body(): pl.pallas_call(matrix_kernel, grid=(TARGETS // 8,), in_specs=[pl.BlockSpe...]
    all_to_all x1, waiting for transfers between devices: 48.2 us -> 0.01 us  [body(): lax.all_to_all(sent, 'dir', split_axis=0, concat_axis=0, tiled=True)]
    dot_general x20 -> x0, matrix products: 36.3 us -> none  [the longest x7 17.4 us: add_block(): jnp.dot(select_source, flat_sources, precision=highest, preferred_element...]
    reduce_sum x9 -> x0, other arithmetic: 11 us -> none  [the longest x7 7.42 us: add_block(): new_real = jnp.sum(along_real * real_part - along_imag * imag_part, axis=1)]
    another operation x8 -> x0, local copies, waits for them, and re-layouts: 7.77 us -> none
    unnamed x15 -> x12, local copies, waits for them, and re-layouts: 6.12 us -> 1.01 us
    all_to_all x1 -> x3, blocking collectives: 64.6 us -> 68.7 us  [the longest x1 40.1 us: body(): lax.all_to_all(lowered, 'dir', split_axis=0, concat_axis=0, tiled=True)]
  transfers between devices with their start and end apart: 2 -> 1, of which waited for: 2 -> 0; matrix products, arithmetic and copies ran while one was open for 1% -> 3% of each run, Pallas kernels for 0% -> 20%
where the time goes in v1:
time: 144 us; the launch traced here: 143 us
  blocking collectives  68.7 us (48%)
  Pallas kernels  54 us (38%)
  starting transfers between devices  15.2 us (11%)
  local copies, waits for them, and re-layouts  3.72 us (3%)
    all_to_all x1, blocking collectives, body(): lax.all_to_all(lowered, 'dir', split_axis=0, concat_axis=0, tiled=True)  40.1 us
    pallas_call x1, Pallas kernels, body(): pl.pallas_call(matrix_kernel, grid=(TARGETS // 8,), in_specs=[pl.BlockSpe...  28.2 us
    all_to_all x1, blocking collectives, body(): lax.all_to_all(packed, 'box', split_axis=0, concat_axis=0, tiled=True)  18.5 us
    all_to_all x1, starting transfers between devices, body(): lax.all_to_all(sent, 'dir', split_axis=0, concat_axis=0, tiled=True)  15.2 us
    pallas_call x1, Pallas kernels, body(): pl.pallas_call(translate_kernel, grid=(TARGETS // 8,), in_specs=[pl.Block...  12.4 us
    all_to_all x1, blocking collectives, body(): lax.all_to_all(incoming, 'box', split_axis=0, concat_axis=0, axis_index_g...  10.1 us
    pallas_call x1, Pallas kernels, body(): pl.pallas_call(theta_up_kernel, out_shape=shape(16, 4, 8, 256), in_specs=...  3.91 us
    pallas_call x1, Pallas kernels, body(): pl.pallas_call(scatter_kernel, out_shape=shape(16, 4, 8, 256), in_specs=[...  3.29 us
  transfers between devices with their start and end apart: 1, of which 0 were waited for; matrix products, arithmetic and copies ran while one was open for 3% of the time, Pallas kernels for 20%

profile of v1, /device:TPU:32, one launch (start us, length us, event | category | flops | bytes accessed | tf_op | source)
XLA Modules:
  0.0 142.8 jit_solution(2270602930662983708)
XLA Ops:
  0.0 3.9 %shard_map.100 = f32[16,4,8,256]{3,2,1,0:T(8,128)} custom-call(f32[4,8,2048]{2,1,0:T(8,128)} %x_ref.1, f32[32,32,128]{2,1,0:T(8,128)} %constant.110.clone.c_ref), custom_call_target="tpu_custom_call" | custom-call | tf_op jit(solution)/shard_map/pallas_call | solution.py:276
  3.9 15.2 %all-to-all-start = ((f32[16,4,8,256]{3,2,1,0:T(8,128)}), f32[16,4,8,256]{3,2,1,0:T(8,128)S(1)}, u32[]{:S(2)}, u32[]{:S(2)}) async-start(f32[16,4,8,256]{3,2,1,0:T(8,128)} %shard_map.100), calls=%async_computation | async-start | bytes 1048576 | tf_op jit(solution)/shard_map/all_to_all | solution.py:279
  19.1 0.1 dynamic_slice.12
  19.2 0.1 constant_dynamic-slice_fusion.1
  19.3 0.1 copy.15
  19.4 0.6 pad.12.kind_ref
  20.1 0.1 copy.14
  20.2 0.1 fusion
  20.2 0.6 pad.11.partner_ref
  20.9 0.4 constant_dynamic-slice_fusion
  21.3 0.2 copy.13
  21.4 0.7 pad.13.table_ref
  22.1 28.2 %shard_map.101.after_ref.m_ref = f32[64,256,128]{2,1,0:T(8,128)} custom-call(s32[64,256]{1,0:T(8,128)} %pad.11.partner_ref, s32[64,256]{1,0:T(8,128)} %pad.12.kind_ref, f32[128,384]{1,0:T(8,128)} %pad.13.table_ref), custom_call_target="tpu_custom_call" | custom-call | tf_op jit(solution)/shard_map/pallas_call | solution.py:292
  50.5 0.1 add_bitcast_fusion
  50.6 0.1 multiply_bitcast_fusion.1
  50.6 0.8 fusion.1
  51.4 0.8 copy-done.1
  52.2 2.9 %shard_map.102 = f32[32,4,8,128]{3,2,1,0:T(8,128)} custom-call(s32[64]{0:T(128)} %slot_ref.3, f32[16,4,8,256]{3,2,1,0:T(8,128)} %copy-done.1, bf16[2,128,256]{2,1,0:T(8,128)(2,1)} %constant.112.clone.w_ref, f32[8,512]{1,0:T(8,128)} %get-tuple-element.6.cos_ref, f32[8,512]{1,0:T(8,128)} %get-tuple-element.5.sin_ref, f32[64,256,128]{2,1,0:T(8,128)} %shard_map.101.after_ref.m_ref), custom_call_target="tpu_custom_call" | custom-call | tf_op jit(solution)/shard_map/pallas_call | solution.py:306
  55.1 18.5 %all_to_all.20.s_ref = f32[32,4,8,128]{3,2,1,0:T(8,128)} all-to-all(f32[32,4,8,128]{3,2,1,0:T(8,128)} %shard_map.102), channel_id=1, replica_groups=mesh['box'=32,'dir'=16] {'box'}, dimensions={0} | all-to-all | bytes 1048576 | tf_op jit(solution)/shard_map/all_to_all | solution.py:317
  73.6 12.4 %shard_map.103 = f32[8,4,8,128]{3,2,1,0:T(8,128)} custom-call(f32[32,4,8,128]{3,2,1,0:T(8,128)} %all_to_all.20.s_ref, f32[64,256,128]{2,1,0:T(8,128)} %shard_map.101.after_ref.m_ref), custom_call_target="tpu_custom_call" | custom-call | tf_op jit(solution)/shard_map/pallas_call | solution.py:318
  86.0 10.1 %all_to_all.21.x_ref = f32[8,4,8,128]{3,2,1,0:T(8,128)} all-to-all(f32[8,4,8,128]{3,2,1,0:T(8,128)} %shard_map.103), channel_id=1, replica_groups={{0,16,32,48,64,80,96,112},{128,144,160,176,192,208,224,240},{256,272,28..., dimensions={0} | all-to-all | bytes 262144 | tf_op jit(solution)/shard_map/all_to_all | solution.py:330
  96.1 3.3 %shard_map.104 = f32[16,4,8,256]{3,2,1,0:T(8,128)} custom-call(s32[64]{0:T(128)} %slot_ref.3, f32[8,4,8,128]{3,2,1,0:T(8,128)} %all_to_all.21.x_ref, bf16[2,256,128]{2,1,0:T(8,128)(2,1)} %constant.113.clone.w_ref, f32[8,512]{1,0:T(8,128)} %get-tuple-element.6.cos_ref, f32[8,512]{1,0:T(8,128)} %get-tuple-element.5.sin_ref), custom_call_target="tpu_custom_call" | custom-call | tf_op jit(solution)/shard_map/pallas_call | solution.py:333
  99.4 40.1 %all_to_all.22.y_ref = f32[16,4,8,256]{3,2,1,0:T(8,128)} all-to-all(f32[16,4,8,256]{3,2,1,0:T(8,128)} %shard_map.104), channel_id=1, replica_groups=mesh['box'=32,'dir'=16] {'dir'}, dimensions={0} | all-to-all | bytes 1048576 | tf_op jit(solution)/shard_map/all_to_all | solution.py:344
  139.5 3.2 %shard_map.105 = f32[4,8,2048]{2,1,0:T(8,128)} custom-call(f32[16,4,8,256]{3,2,1,0:T(8,128)} %all_to_all.22.y_ref, f32[16,64,128]{2,1,0:T(8,128)} %constant.111.clone.c_ref), custom_call_target="tpu_custom_call" | custom-call | tf_op jit(solution)/shard_map/pallas_call | solution.py:345
  (15 shorter events, 0.1 us)
Async XLA Ops:
  0.0 20.9 %copy-start = (f32[316,2,512]{2,1,0:T(2,128)S(1)}, f32[316,2,512]{2,1,0:T(2,128)}, u32[]{:S(2)}) copy-start(f32[316,2,512]{2,1,0:T(2,128)} %param.12) | copy-start | bytes 3883012
  0.0 19.1 %copy-start.4 = (s32[256]{0:T(256)S(1)}, s32[256]{0:T(256)}, u32[]{:S(2)}) copy-start(s32[256]{0:T(256)} %param.15) | copy-start | bytes 3076
  0.0 19.2 %copy-start.2 = (s32[256,189]{0,1:T(8,128)S(1)}, s32[256,189]{0,1:T(8,128)}, u32[]{:S(2)}) copy-start(s32[256,189]{0,1:T(8,128)} %param.14) | copy-start | bytes 580612
  0.0 19.2 %copy-start.3 = (s32[256,189]{0,1:T(8,128)S(1)}, s32[256,189]{0,1:T(8,128)}, u32[]{:S(2)}) copy-start(s32[256,189]{0,1:T(8,128)} %param.13) | copy-start | bytes 580612
  3.9 47.5 %all-to-all-start = ((f32[16,4,8,256]{3,2,1,0:T(8,128)}), f32[16,4,8,256]{3,2,1,0:T(8,128)S(1)}, u32[]{:S(2)}, u32[]{:S(2)}) async-start(f32[16,4,8,256]{3,2,1,0:T(8,128)} %shard_map.100), calls=%async_computation | async-start | bytes 1048576 | tf_op jit(solution)/shard_map/all_to_all | solution.py:279
  51.4 0.8 copy-start.1

commit v2 on v1

--- a/solution.py
+++ b/solution.py
@@ -198,7 +198,7 @@
     sign = jnp.where(row < 4, -1.0, 1.0).astype(f32)
     whole = [a + sign * pltpu.roll(swap_halves(a), 4, 0) for a in sums]
     for j in range(4):
-        o_ref[0, j] = jnp.where(low_half, whole[j], swap_halves(whole[j + 4]))
+        o_ref[pl.program_id(0), j] = jnp.where(low_half, whole[j], swap_halves(whole[j + 4]))
 
 
 def scatter_kernel(slot_ref, x_ref, w_ref, cos_ref, sin_ref, o_ref, plain_ref, turned_ref, child_ref):
@@ -260,6 +260,14 @@
     return jax.ShapeDtypeStruct(dims, f32)
 
 
+def near(*dims):
+    return pltpu.VMEM(dims, f32)
+
+
+def hold(x):
+    return pltpu.with_memory_space_constraint(x, pltpu.VMEM)
+
+
 def body(outgoing, fine_slot, translator, list_partner, list_kind, list_count):
     box_index = lax.axis_index("box")
     dir_index = lax.axis_index("dir")
@@ -274,7 +282,7 @@
     phi_down = jnp.asarray(split_constant(np.kron(np.eye(2), phi) * (PF / PP)))
 
     sent = pl.pallas_call(
-        theta_up_kernel, out_shape=shape(16, 4, 8, 256), in_specs=[vmem, vmem], out_specs=vmem
+        theta_up_kernel, out_shape=near(16, 4, 8, 256), in_specs=[vmem, vmem], out_specs=vmem
     )(outgoing, up)
     spread = lax.all_to_all(sent, "dir", split_axis=0, concat_axis=0, tiled=True)
 
@@ -305,7 +313,7 @@
 
     packed = pl.pallas_call(
         gather_kernel,
-        out_shape=shape(32, 4, 8, LANES),
+        out_shape=near(32, 4, 8, LANES),
         in_specs=[smem, vmem, vmem, vmem, vmem, pl.BlockSpec(memory_space=pl.ANY)],
         out_specs=vmem,
         scratch_shapes=[
@@ -313,26 +321,26 @@
             pltpu.VMEM((8, 8, 512), f32),
             pltpu.SMEM((64,), jnp.int32),
         ],
-    )(fine_slot, spread, phi_up, cos_table, sin_table, matrix)
+    )(fine_slot, hold(spread), phi_up, cos_table, sin_table, matrix)
     everyone = lax.all_to_all(packed, "box", split_axis=0, concat_axis=0, tiled=True)
     incoming = pl.pallas_call(
         translate_kernel,
         grid=(TARGETS // 8,),
         in_specs=[
-            pl.BlockSpec((32, 4, 8, LANES), lambda i: (0, 0, 0, 0)),
+            vmem,
             pl.BlockSpec((8, SOURCES, LANES), lambda i: (i, 0, 0)),
         ],
-        out_specs=pl.BlockSpec((1, 4, 8, LANES), lambda i: (i, 0, 0, 0)),
-        out_shape=shape(8, 4, 8, LANES),
+        out_specs=vmem,
+        out_shape=near(8, 4, 8, LANES),
         scratch_shapes=[pltpu.VMEM((SOURCES, 8, LANES), f32)],
-    )(everyone, matrix)
+    )(hold(everyone), matrix)
     groups = [[8 * g + k for k in range(8)] for g in range(4)]
     fields = lax.all_to_all(
         incoming, "box", split_axis=0, concat_axis=0, axis_index_groups=groups, tiled=True
     )
     lowered = pl.pallas_call(
         scatter_kernel,
-        out_shape=shape(16, 4, 8, 256),
+        out_shape=near(16, 4, 8, 256),
         in_specs=[smem, vmem, vmem, vmem, vmem],
         out_specs=vmem,
         scratch_shapes=[
@@ -340,11 +348,11 @@
             pltpu.VMEM((8, 8, 512), f32),
             pltpu.VMEM((64, 8, 512), f32),
         ],
-    )(fine_slot, fields, phi_down, cos_table, sin_table)
+    )(fine_slot, hold(fields), phi_down, cos_table, sin_table)
     back = lax.all_to_all(lowered, "dir", split_axis=0, concat_axis=0, tiled=True)
     return pl.pallas_call(
         theta_down_kernel, out_shape=shape(4, 8, TF * PF), in_specs=[vmem, vmem], out_specs=vmem
-    )(back, down)
+    )(hold(back), down)
 
 
 def solution(mesh):

time: 144 us -> 138 us (0.958)
  Pallas kernels: 54 us -> 51.2 us
  blocking collectives: 68.7 us -> 67.1 us
    pallas_call x4, Pallas kernels: 22.5 us -> 19.8 us  [the longest x1 11.6 us: body(): pl.pallas_call(translate_kernel, grid=(TARGETS // 8,), in_specs=[vmem, pl...]
  transfers between devices with their start and end apart: 1 -> 1, of which waited for: 0 -> 0; matrix products, arithmetic and copies ran while one was open for 3% -> 3% of each run, Pallas kernels for 20% -> 21%
where the time goes in v2:
time: 138 us; the launch traced here: 137 us
  blocking collectives  67.1 us (49%)
  Pallas kernels  51.2 us (37%)
  starting transfers between devices  15.2 us (11%)
  local copies, waits for them, and re-layouts  2.86 us (2%)
    all_to_all x1, blocking collectives, body(): lax.all_to_all(lowered, 'dir', split_axis=0, concat_axis=0, tiled=True)  40 us
    pallas_call x1, Pallas kernels, body(): pl.pallas_call(matrix_kernel, grid=(TARGETS // 8,), in_specs=[pl.BlockSpe...  28.2 us
    all_to_all x1, blocking collectives, body(): lax.all_to_all(packed, 'box', split_axis=0, concat_axis=0, tiled=True)  18 us
    all_to_all x1, starting transfers between devices, body(): lax.all_to_all(sent, 'dir', split_axis=0, concat_axis=0, tiled=True)  15.2 us
    pallas_call x1, Pallas kernels, body(): pl.pallas_call(translate_kernel, grid=(TARGETS // 8,), in_specs=[vmem, pl...  11.6 us
    all_to_all x1, blocking collectives, body(): lax.all_to_all(incoming, 'box', split_axis=0, concat_axis=0, axis_index_g...  9.05 us
    pallas_call x1, Pallas kernels, body(): pl.pallas_call(theta_up_kernel, out_shape=near(16, 4, 8, 256), in_specs=[...  3.91 us
    pallas_call x1, Pallas kernels, body(): pl.pallas_call(theta_down_kernel, out_shape=shape(4, 8, TF * PF), in_spec...  3.09 us
  transfers between devices with their start and end apart: 1, of which 0 were waited for; matrix products, arithmetic and copies ran while one was open for 3% of the time, Pallas kernels for 21%

profile of v2, /device:TPU:32, one launch (start us, length us, event | category | flops | bytes accessed | tf_op | source)
XLA Modules:
  0.0 137.5 jit_solution(8207834712504536702)
XLA Ops:
  0.0 3.9 %shard_map.100 = f32[16,4,8,256]{3,2,1,0:T(8,128)} custom-call(f32[4,8,2048]{2,1,0:T(8,128)} %x_ref.1, f32[32,32,128]{2,1,0:T(8,128)} %constant.110.clone.c_ref), custom_call_target="tpu_custom_call" | custom-call | tf_op jit(solution)/shard_map/pallas_call | solution.py:284
  3.9 15.2 %all-to-all-start = ((f32[16,4,8,256]{3,2,1,0:T(8,128)}), f32[16,4,8,256]{3,2,1,0:T(8,128)S(1)}, u32[]{:S(2)}, u32[]{:S(2)}) async-start(f32[16,4,8,256]{3,2,1,0:T(8,128)} %shard_map.100), calls=%async_computation | async-start | bytes 1048576 | tf_op jit(solution)/shard_map/all_to_all | solution.py:287
  19.1 0.1 dynamic_slice.12
  19.2 0.1 constant_dynamic-slice_fusion.1
  19.3 0.1 copy.15
  19.4 0.6 pad.12.kind_ref
  20.1 0.1 copy.14
  20.2 0.1 fusion
  20.2 0.6 pad.11.partner_ref
  20.9 0.4 constant_dynamic-slice_fusion
  21.3 0.2 copy.13
  21.4 0.7 pad.13.table_ref
  22.1 28.2 %shard_map.101.after_ref.m_ref = f32[64,256,128]{2,1,0:T(8,128)} custom-call(s32[64,256]{1,0:T(8,128)} %pad.11.partner_ref, s32[64,256]{1,0:T(8,128)} %pad.12.kind_ref, f32[128,384]{1,0:T(8,128)} %pad.13.table_ref), custom_call_target="tpu_custom_call" | custom-call | tf_op jit(solution)/shard_map/pallas_call | solution.py:300
  50.5 0.1 add_bitcast_fusion
  50.6 0.1 multiply_bitcast_fusion.1
  50.6 0.8 fusion.1
  51.4 0.0 all-to-all-done.x_ref
  51.4 1.8 %shard_map.102 = f32[32,4,8,128]{3,2,1,0:T(8,128)S(1)} custom-call(s32[64]{0:T(128)} %slot_ref.3, f32[16,4,8,256]{3,2,1,0:T(8,128)S(1)} %all-to-all-done.x_ref, bf16[2,128,256]{2,1,0:T(8,128)(2,1)} %constant.112.clone.w_ref, f32[8,512]{1,0:T(8,128)} %get-tuple-element.6.cos_ref, f32[8,512]{1,0:T(8,128)} %get-tuple-element.5.sin_ref, ...), custom_call_target="tpu_custom_call" | custom-call | tf_op jit(solution)/shard_map/pallas_call | solution.py:314
  53.2 18.0 %all_to_all.20.s_ref = f32[32,4,8,128]{3,2,1,0:T(8,128)S(1)} all-to-all(f32[32,4,8,128]{3,2,1,0:T(8,128)S(1)} %shard_map.102), channel_id=1, replica_groups=mesh['box'=32,'dir'=16] {'box'}, dimensions={0} | all-to-all | bytes 1048576 | tf_op jit(solution)/shard_map/all_to_all | solution.py:325
  71.3 11.6 %shard_map.103 = f32[8,4,8,128]{3,2,1,0:T(8,128)S(1)} custom-call(f32[32,4,8,128]{3,2,1,0:T(8,128)S(1)} %all_to_all.20.s_ref, f32[64,256,128]{2,1,0:T(8,128)} %shard_map.101.after_ref.m_ref), custom_call_target="tpu_custom_call" | custom-call | tf_op jit(solution)/shard_map/pallas_call | solution.py:326
  82.9 9.1 %all_to_all.21.x_ref = f32[8,4,8,128]{3,2,1,0:T(8,128)S(1)} all-to-all(f32[8,4,8,128]{3,2,1,0:T(8,128)S(1)} %shard_map.103), channel_id=1, replica_groups={{0,16,32,48,64,80,96,112},{128,144,160,176,192,208,224,240},{256,272,28..., dimensions={0} | all-to-all | bytes 262144 | tf_op jit(solution)/shard_map/all_to_all | solution.py:338
  92.0 2.4 %shard_map.104 = f32[16,4,8,256]{3,2,1,0:T(8,128)S(1)} custom-call(s32[64]{0:T(128)} %slot_ref.3, f32[8,4,8,128]{3,2,1,0:T(8,128)S(1)} %all_to_all.21.x_ref, bf16[2,256,128]{2,1,0:T(8,128)(2,1)} %constant.113.clone.w_ref, f32[8,512]{1,0:T(8,128)} %get-tuple-element.6.cos_ref, f32[8,512]{1,0:T(8,128)} %get-tuple-element.5.sin_ref), custom_call_target="tpu_custom_call" | custom-call | tf_op jit(solution)/shard_map/pallas_call | solution.py:341
  94.4 40.0 %all_to_all.22.y_ref = f32[16,4,8,256]{3,2,1,0:T(8,128)S(1)} all-to-all(f32[16,4,8,256]{3,2,1,0:T(8,128)S(1)} %shard_map.104), channel_id=1, replica_groups=mesh['box'=32,'dir'=16] {'dir'}, dimensions={0} | all-to-all | bytes 1048576 | tf_op jit(solution)/shard_map/all_to_all | solution.py:352
  134.4 3.1 %shard_map.105 = f32[4,8,2048]{2,1,0:T(8,128)} custom-call(f32[16,4,8,256]{3,2,1,0:T(8,128)S(1)} %all_to_all.22.y_ref, f32[16,64,128]{2,1,0:T(8,128)} %constant.111.clone.c_ref), custom_call_target="tpu_custom_call" | custom-call | tf_op jit(solution)/shard_map/pallas_call | solution.py:353
  (13 shorter events, 0.1 us)
Async XLA Ops:
  0.0 20.9 %copy-start = (f32[316,2,512]{2,1,0:T(2,128)S(1)}, f32[316,2,512]{2,1,0:T(2,128)}, u32[]{:S(2)}) copy-start(f32[316,2,512]{2,1,0:T(2,128)} %param.12) | copy-start | bytes 3883012
  0.0 19.1 %copy-start.3 = (s32[256]{0:T(256)S(1)}, s32[256]{0:T(256)}, u32[]{:S(2)}) copy-start(s32[256]{0:T(256)} %param.15) | copy-start | bytes 3076
  0.0 19.2 %copy-start.1 = (s32[256,189]{0,1:T(8,128)S(1)}, s32[256,189]{0,1:T(8,128)}, u32[]{:S(2)}) copy-start(s32[256,189]{0,1:T(8,128)} %param.14) | copy-start | bytes 580612
  0.0 19.2 %copy-start.2 = (s32[256,189]{0,1:T(8,128)S(1)}, s32[256,189]{0,1:T(8,128)}, u32[]{:S(2)}) copy-start(s32[256,189]{0,1:T(8,128)} %param.13) | copy-start | bytes 580612
  3.9 47.5 %all-to-all-start = ((f32[16,4,8,256]{3,2,1,0:T(8,128)}), f32[16,4,8,256]{3,2,1,0:T(8,128)S(1)}, u32[]{:S(2)}, u32[]{:S(2)}) async-start(f32[16,4,8,256]{3,2,1,0:T(8,128)} %shard_map.100), calls=%async_computation | async-start | bytes 1048576 | tf_op jit(solution)/shard_map/all_to_all | solution.py:287

commit v3 on v2

--- a/solution.py
+++ b/solution.py
@@ -12,7 +12,7 @@
 TP = 64
 PP = 128
 LANES = 128
-SLOTS = 256
+SLOTS = 192
 KINDS = 384
 TARGETS = 64
 SOURCES = 256
@@ -62,45 +62,63 @@
     return pltpu.roll(x, PF, x.ndim - 1)
 
 
-def theta_up_kernel(x_ref, c_ref, o_ref):
+def parity_table(matrix):
+    n_out, n_in = matrix.shape
+    top = matrix[: n_out // 2]
+    near, far = top[:, : n_in // 2], top[:, ::-1][:, : n_in // 2]
+    return np.concatenate([pair_table((near + far) / 2), pair_table((near - far) / 2)], 1)
+
+
+def theta_step(parity_ref, c_ref, j, count):
+    zero = jnp.zeros((8, LANES), f32)
+    sums = [[zero] * 4 for _ in range(4)]
+    for i in range(count):
+        for odd in range(2):
+            base = odd * 2 * count + 2 * i
+            cs = c_ref[j, pl.ds(base, 1), :]
+            cx = c_ref[j, pl.ds(base + 1, 1), :]
+            for f in range(4):
+                v = parity_ref[f, i, odd]
+                sums[2 * odd][f] = sums[2 * odd][f] + cs * v
+                sums[2 * odd + 1][f] = sums[2 * odd + 1][f] + cx * v
+    out = []
+    for f in range(4):
+        es, ex, os, ox = (sums[k][f] for k in range(4))
+        out.append(((es + os) + swap_halves(ex + ox), swap_halves(es - os) + (ex - ox)))
+    return out
+
+
+def theta_up_kernel(x_ref, c_ref, o_ref, parity_ref):
+    for f in range(4):
+        for i in range(8):
+            v = x_ref[f, :, pl.ds(i * LANES, LANES)]
+            w = swap_halves(x_ref[f, :, pl.ds((15 - i) * LANES, LANES)])
+            parity_ref[f, i, 0] = v + w
+            parity_ref[f, i, 1] = v - w
+
     def step(z, carry):
         for part in range(2):
-            j = 2 * z + part
-            same = [jnp.zeros((8, LANES), f32) for _ in range(4)]
-            cross = [jnp.zeros((8, LANES), f32) for _ in range(4)]
-            for i in range(TF // 2):
-                cs = c_ref[j, pl.ds(2 * i, 1), :]
-                cx = c_ref[j, pl.ds(2 * i + 1, 1), :]
-                for f in range(4):
-                    v = x_ref[f, :, pl.ds(i * LANES, LANES)]
-                    same[f] = same[f] + cs * v
-                    cross[f] = cross[f] + cx * v
+            out = theta_step(parity_ref, c_ref, 2 * z + part, 8)
             for f in range(4):
-                o_ref[z, f, :, pl.ds(part * LANES, LANES)] = same[f] + swap_halves(cross[f])
+                o_ref[z, f, :, pl.ds(part * LANES, LANES)] = out[f][0]
+                o_ref[15 - z, f, :, pl.ds((1 - part) * LANES, LANES)] = out[f][1]
         return carry
 
-    lax.fori_loop(0, 16, step, 0)
-
-
-def theta_down_kernel(y_ref, c_ref, o_ref):
-    for j in range(TF // 2):
-        zero = jnp.zeros((8, LANES), f32)
-
-        def step(z, carry):
-            same, cross = list(carry[:4]), list(carry[4:])
-            for part in range(2):
-                i = 2 * z + part
-                cs = c_ref[j, pl.ds(2 * i, 1), :]
-                cx = c_ref[j, pl.ds(2 * i + 1, 1), :]
-                for f in range(4):
-                    v = y_ref[z, f, :, pl.ds(part * LANES, LANES)]
-                    same[f] = same[f] + cs * v
-                    cross[f] = cross[f] + cx * v
-            return (*same, *cross)
-
-        done = lax.fori_loop(0, 16, step, (zero,) * 8, unroll=True)
+    lax.fori_loop(0, 8, step, 0)
+
+
+def theta_down_kernel(y_ref, c_ref, o_ref, parity_ref):
+    for f in range(4):
+        for i in range(16):
+            v = y_ref[i // 2, f, :, pl.ds(i % 2 * LANES, LANES)]
+            w = swap_halves(y_ref[15 - i // 2, f, :, pl.ds((1 - i % 2) * LANES, LANES)])
+            parity_ref[f, i, 0] = v + w
+            parity_ref[f, i, 1] = v - w
+    for j in range(8):
+        out = theta_step(parity_ref, c_ref, j, 16)
         for f in range(4):
-            o_ref[f, :, pl.ds(j * LANES, LANES)] = done[f] + swap_halves(done[4 + f])
+            o_ref[f, :, pl.ds(j * LANES, LANES)] = out[f][0]
+            o_ref[f, :, pl.ds((15 - j) * LANES, LANES)] = out[f][1]
 
 
 def channel_sign():
@@ -136,8 +154,8 @@
     low_half = lax.broadcasted_iota(jnp.int32, (8, LANES), 1) < PF
     for j in range(4):
         for block in range(4):
-            a = parent_ref[j, :, pl.ds(block * LANES, LANES)]
-            b = parent_ref[j + 4, :, pl.ds(block * LANES, LANES)]
+            a = parent_ref[2 * j, :, pl.ds(block * LANES, LANES)]
+            b = parent_ref[2 * j + 1, :, pl.ds(block * LANES, LANES)]
             even = jnp.where(low_half, a, swap_halves(b))
             odd = jnp.where(low_half, swap_halves(a), b)
             for group in range(4):
@@ -145,60 +163,99 @@
                 o_ref[group * 8 + 2 * block + 1, j] = odd
 
 
-def matrix_kernel(partner_ref, kind_ref, table_ref, o_ref, both_ref):
+def matrix_kernel(partner_ref, kind_ref, table_ref, o_ref, both_ref, picked_ref):
     @pl.when(pl.program_id(0) == 0)
     def _():
         high, low = split(table_ref[...])
-        both_ref[:LANES] = high
-        both_ref[LANES:] = low
-
-    slot_kind = lax.broadcasted_iota(jnp.int32, (KINDS, SLOTS), 0)
-    slot_source = lax.broadcasted_iota(jnp.int32, (SOURCES, SLOTS), 0)
-    table = both_ref[...]
-
-    def step(p, carry):
-        pick_kind = jnp.where(slot_kind == kind_ref[pl.ds(p, 1), :], 1.0, 0.0).astype(bf16)
-        pick_source = jnp.where(slot_source == partner_ref[pl.ds(p, 1), :], 1.0, 0.0).astype(bf16)
-        rows = jnp.dot(table, pick_kind, preferred_element_type=f32).astype(bf16)
-        both = lax.dot_general(
-            pick_source, rows, (((1,), (1,)), ((), ())), preferred_element_type=f32
-        )
+        both_ref[:, :LANES] = high
+        both_ref[:, LANES:] = low
+
+    lane_kind = lax.broadcasted_iota(jnp.int32, (SLOTS, KINDS), 1)
+    row_source = lax.broadcasted_iota(jnp.int32, (SOURCES, SLOTS), 0)
+    pick_kind = jnp.concatenate(
+        [
+            jnp.where(lane_kind == kind_ref[0, :, p : p + 1], 1.0, 0.0).astype(bf16)
+            for p in range(8)
+        ],
+        0,
+    )
+    picked_ref[...] = jnp.dot(pick_kind, both_ref[...], preferred_element_type=f32).astype(bf16)
+    for p in range(8):
+        pick_source = jnp.where(row_source == partner_ref[pl.ds(p, 1), :], 1.0, 0.0).astype(bf16)
+        rows = picked_ref[pl.ds(p * SLOTS, SLOTS), :]
+        both = jnp.dot(pick_source, rows, preferred_element_type=f32)
         o_ref[p] = both[:, :LANES] + both[:, LANES:]
-        return carry
-
-    lax.fori_loop(0, 8, step, 0)
-
-
-def translate_kernel(s_ref, m_ref, o_ref, wide_ref):
+
+
+def fold_rows(parts):
+    row = lax.broadcasted_iota(jnp.int32, (8, LANES), 0)
+    shift = 1
+    while len(parts) > 1:
+        first = (row & shift) == 0
+        parts = [
+            jnp.where(first, a, b) + pltpu.roll(jnp.where(first, b, a), shift, 0)
+            for a, b in zip(parts[0::2], parts[1::2])
+        ]
+        shift *= 2
+    return parts[0]
+
+
+def translate_kernel(s_ref, m_ref, o_ref, rows_ref, wide_ref):
     low_half = lax.broadcasted_iota(jnp.int32, (8, LANES), 1) < PF
+    top = lax.broadcasted_iota(jnp.int32, (8, LANES), 0) < 4
 
     @pl.when(pl.program_id(0) == 0)
     def _():
-        def spread(b, carry):
+        def pair(b, carry):
             for j in range(4):
                 v = s_ref[b, j]
-                r = swap_halves(v)
-                wide_ref[b * 8 + j] = jnp.where(low_half, v, r)
-                wide_ref[b * 8 + j + 4] = jnp.where(low_half, r, v)
+                w = swap_halves(pltpu.roll(v, 4, 0))
+                rows_ref[pl.ds(b * 32 + j * 8, 8), :] = jnp.where(low_half == top, v, w)
             return carry
 
+        lax.fori_loop(0, 32, pair, 0)
+
+        def spread(b, carry):
+            plain = [rows_ref[pl.ds(b * 32 + e, 8, stride=4), :] for e in range(4)]
+            both = [v + swap_halves(v) for v in plain]
+            for e in range(4):
+                wide_ref[b, e] = plain[e]
+            for h in range(2):
+                wide_ref[b, 4 + h] = jnp.where(low_half, both[2 * h], both[2 * h + 1])
+            return carry
+
         lax.fori_loop(0, 32, spread, 0)
 
-    def step(q, sums):
-        sums = list(sums)
-        for k in range(8):
-            s = q * 8 + k
-            v = wide_ref[s]
-            for p in range(8):
-                sums[p] = sums[p] + m_ref[p, pl.ds(s, 1), :] * v
-        return tuple(sums)
-
-    sums = lax.fori_loop(0, SOURCES // 8, step, (jnp.zeros((8, LANES), f32),) * 8)
-    row = lax.broadcasted_iota(jnp.int32, (8, LANES), 0)
-    sign = jnp.where(row < 4, -1.0, 1.0).astype(f32)
-    whole = [a + sign * pltpu.roll(swap_halves(a), 4, 0) for a in sums]
-    for j in range(4):
-        o_ref[pl.program_id(0), j] = jnp.where(low_half, whole[j], swap_halves(whole[j + 4]))
+    for q in range(2):
+
+        def step(b, sums):
+            sums = list(sums)
+            source = [wide_ref[b, k] for k in range(6)]
+            for p in range(4):
+                m = m_ref[4 * q + p, pl.ds(pl.multiple_of(b * 8, 8), 8), :]
+                t = m + swap_halves(m)
+                for k in range(6):
+                    sums[6 * p + k] = sums[6 * p + k] + source[k] * (m if k < 4 else t)
+            return tuple(sums)
+
+        sums = lax.fori_loop(0, SOURCES // 8, step, (jnp.zeros((8, LANES), f32),) * 24, unroll=True)
+        real, imag = [], []
+        for p in range(4):
+            part = sums[6 * p : 6 * p + 6]
+            turned = [swap_halves(v) for v in part[:4]]
+            real.append([a - b for a, b in zip(part[:4], turned)])
+            total = [a + b for a, b in zip(part[:4], turned)]
+            imag.append(
+                [part[4 + h] - jnp.where(low_half, total[2 * h], total[2 * h + 1]) for h in range(2)]
+            )
+        for j in range(2):
+            a, b = 2 * j, 2 * j + 1
+            parts = [jnp.where(low_half, x, -y) for x, y in zip(real[a], real[b])]
+            for h in range(2):
+                x, y = imag[a][h], imag[b][h]
+                parts.append(jnp.where(low_half, x, swap_halves(y)))
+                parts.append(jnp.where(low_half, swap_halves(x), y))
+            o_ref[pl.program_id(0), 2 * q + j] = fold_rows(parts)
 
 
 def scatter_kernel(slot_ref, x_ref, w_ref, cos_ref, sin_ref, o_ref, plain_ref, turned_ref, child_ref):
@@ -209,8 +266,8 @@
             b = x_ref[2 * block + 1, j]
             first = jnp.where(low_half, a, swap_halves(b))
             second = jnp.where(low_half, swap_halves(a), b)
-            plain_ref[j, :, pl.ds(block * LANES, LANES)] = first
-            plain_ref[j + 4, :, pl.ds(block * LANES, LANES)] = second
+            plain_ref[2 * j, :, pl.ds(block * LANES, LANES)] = first
+            plain_ref[2 * j + 1, :, pl.ds(block * LANES, LANES)] = second
     sign = channel_sign()
     for p in range(8):
         turned_ref[p] = -sign * pltpu.roll(plain_ref[p], 4, 0)
@@ -275,14 +332,18 @@
     group = box_index // 8
 
     theta = theta_matrix()
-    up = jnp.asarray(pair_table(theta))
-    down = jnp.asarray(pair_table(theta.T * (TF / TP)))
+    up = jnp.asarray(parity_table(theta))
+    down = jnp.asarray(parity_table(theta.T * (TF / TP)))
     phi = phi_matrix()
     phi_up = jnp.asarray(split_constant(np.kron(np.eye(2), phi.T)))
     phi_down = jnp.asarray(split_constant(np.kron(np.eye(2), phi) * (PF / PP)))
 
     sent = pl.pallas_call(
-        theta_up_kernel, out_shape=near(16, 4, 8, 256), in_specs=[vmem, vmem], out_specs=vmem
+        theta_up_kernel,
+        out_shape=near(16, 4, 8, 256),
+        in_specs=[vmem, vmem],
+        out_specs=vmem,
+        scratch_shapes=[pltpu.VMEM((4, 8, 2, 8, LANES), f32)],
     )(outgoing, up)
     spread = lax.all_to_all(sent, "dir", split_axis=0, concat_axis=0, tiled=True)
 
@@ -294,20 +355,21 @@
     pad = ((0, 0), (0, SLOTS - length))
     rows = jnp.pad(jnp.where(live, rows, -1), pad, constant_values=-1)
     kinds = jnp.pad(kinds, pad, constant_values=-1)
+    kinds = kinds.reshape(TARGETS // 8, 8, SLOTS).transpose(0, 2, 1)
     table = lax.dynamic_slice_in_dim(translator, chunk * CHUNK, CHUNK, 2)
-    table = table.reshape(table.shape[0], LANES).T
-    table = jnp.pad(table, ((0, 0), (0, KINDS - table.shape[1])))
+    table = table.reshape(table.shape[0], LANES)
+    table = jnp.pad(table, ((0, KINDS - table.shape[0]), (0, 0)))
     matrix = pl.pallas_call(
         matrix_kernel,
         grid=(TARGETS // 8,),
         in_specs=[
             pl.BlockSpec((8, SLOTS), lambda i: (i, 0)),
-            pl.BlockSpec((8, SLOTS), lambda i: (i, 0)),
-            pl.BlockSpec((LANES, KINDS), lambda i: (0, 0)),
+            pl.BlockSpec((1, SLOTS, 8), lambda i: (i, 0, 0)),
+            pl.BlockSpec((KINDS, LANES), lambda i: (0, 0)),
         ],
         out_specs=pl.BlockSpec((8, SOURCES, LANES), lambda i: (i, 0, 0)),
         out_shape=shape(TARGETS, SOURCES, LANES),
-        scratch_shapes=[pltpu.VMEM((256, KINDS), bf16)],
+        scratch_shapes=[pltpu.VMEM((KINDS, 256), bf16), pltpu.VMEM((8 * SLOTS, 256), bf16)],
     )(rows, kinds, table)
     cos_table, sin_table = phase_tables(dir_index)
 
@@ -321,7 +383,7 @@
             pltpu.VMEM((8, 8, 512), f32),
             pltpu.SMEM((64,), jnp.int32),
         ],
-    )(fine_slot, hold(spread), phi_up, cos_table, sin_table, matrix)
+    )(fine_slot, hold(spread), hold(phi_up), cos_table, sin_table, matrix)
     everyone = lax.all_to_all(packed, "box", split_axis=0, concat_axis=0, tiled=True)
     incoming = pl.pallas_call(
         translate_kernel,
@@ -332,7 +394,10 @@
         ],
         out_specs=vmem,
         out_shape=near(8, 4, 8, LANES),
-        scratch_shapes=[pltpu.VMEM((SOURCES, 8, LANES), f32)],
+        scratch_shapes=[
+            pltpu.VMEM((SOURCES * 4, LANES), f32),
+            pltpu.VMEM((SOURCES // 8, 6, 8, LANES), f32),
+        ],
     )(hold(everyone), matrix)
     groups = [[8 * g + k for k in range(8)] for g in range(4)]
     fields = lax.all_to_all(
@@ -348,11 +413,15 @@
             pltpu.VMEM((8, 8, 512), f32),
             pltpu.VMEM((64, 8, 512), f32),
         ],
-    )(fine_slot, hold(fields), phi_down, cos_table, sin_table)
+    )(fine_slot, hold(fields), hold(phi_down), cos_table, sin_table)
     back = lax.all_to_all(lowered, "dir", split_axis=0, concat_axis=0, tiled=True)
     return pl.pallas_call(
-        theta_down_kernel, out_shape=shape(4, 8, TF * PF), in_specs=[vmem, vmem], out_specs=vmem
-    )(hold(back), down)
+        theta_down_kernel,
+        out_shape=shape(4, 8, TF * PF),
+        in_specs=[vmem, vmem],
+        out_specs=vmem,
+        scratch_shapes=[pltpu.VMEM((4, 16, 2, 8, LANES), f32)],
+    )(hold(back), hold(down))
 
 
 def solution(mesh):

time: 138 us -> 128 us (0.928)
  Pallas kernels: 51.2 us -> 34.2 us
  waiting for transfers between devices: 0.01 us -> 10.9 us
  blocking collectives: 67.1 us -> 62.1 us
    pallas_call x1, Pallas kernels: 28.2 us -> 12.8 us  [body(): pl.pallas_call(matrix_kernel, grid=(TARGETS // 8,), in_specs=[pl.BlockSpe...]
    all_to_all x1, waiting for transfers between devices: 0.01 us -> 10.9 us  [body(): lax.all_to_all(sent, 'dir', split_axis=0, concat_axis=0, tiled=True)]
    all_to_all x1, blocking collectives: 40 us -> 34.7 us  [body(): lax.all_to_all(lowered, 'dir', split_axis=0, concat_axis=0, tiled=True)]
    pallas_call x1, Pallas kernels: 3.09 us -> 1.47 us  [body(): pl.pallas_call(theta_down_kernel, out_shape=shape(4, 8, TF * PF), in_spec...]
  transfers between devices with their start and end apart: 1 -> 1, of which waited for: 0 -> 1; matrix products, arithmetic and copies ran while one was open for 3% -> 4% of each run, Pallas kernels for 21% -> 10%
where the time goes in v3:
time: 128 us; the launch traced here: 127 us
  blocking collectives  62.1 us (49%)
  Pallas kernels  34.2 us (27%)
  starting transfers between devices  15.2 us (12%)
  waiting for transfers between devices  10.9 us (9%)
  local copies, waits for them, and re-layouts  3.63 us (3%)
    all_to_all x1, blocking collectives, body(): lax.all_to_all(lowered, 'dir', split_axis=0, concat_axis=0, tiled=True)  34.7 us
    all_to_all x1, blocking collectives, body(): lax.all_to_all(packed, 'box', split_axis=0, concat_axis=0, tiled=True)  18.2 us
    all_to_all x1, starting transfers between devices, body(): lax.all_to_all(sent, 'dir', split_axis=0, concat_axis=0, tiled=True)  15.2 us
    pallas_call x1, Pallas kernels, body(): pl.pallas_call(matrix_kernel, grid=(TARGETS // 8,), in_specs=[pl.BlockSpe...  12.8 us
    pallas_call x1, Pallas kernels, body(): pl.pallas_call(translate_kernel, grid=(TARGETS // 8,), in_specs=[vmem, pl...  12.8 us
    all_to_all x1, waiting for transfers between devices, body(): lax.all_to_all(sent, 'dir', split_axis=0, concat_axis=0, tiled=True)  10.9 us
    all_to_all x1, blocking collectives, body(): lax.all_to_all(incoming, 'box', split_axis=0, concat_axis=0, axis_index_g...  9.2 us
    pallas_call x1, Pallas kernels, body(): pl.pallas_call(theta_up_kernel, out_shape=near(16, 4, 8, 256), in_specs=[...  3.2 us
  transfers between devices with their start and end apart: 1, of which 1 were waited for; matrix products, arithmetic and copies ran while one was open for 4% of the time, Pallas kernels for 10%

profile of v3, /device:TPU:32, one launch (start us, length us, event | category | flops | bytes accessed | tf_op | source)
XLA Modules:
  0.0 127.2 jit_solution(1230917465558204398)
XLA Ops:
  0.0 3.2 %shard_map.100 = f32[16,4,8,256]{3,2,1,0:T(8,128)} custom-call(f32[4,8,2048]{2,1,0:T(8,128)} %x_ref.1, f32[16,32,128]{2,1,0:T(8,128)} %constant.110.clone.c_ref), custom_call_target="tpu_custom_call" | custom-call | tf_op jit(solution)/shard_map/pallas_call | solution.py:341
  3.2 15.2 %all-to-all-start = ((f32[16,4,8,256]{3,2,1,0:T(8,128)}), f32[16,4,8,256]{3,2,1,0:T(8,128)S(1)}, u32[]{:S(2)}, u32[]{:S(2)}) async-start(f32[16,4,8,256]{3,2,1,0:T(8,128)} %shard_map.100), calls=%async_computation | async-start | bytes 1048576 | tf_op jit(solution)/shard_map/all_to_all | solution.py:348
  18.4 0.1 constant_dynamic-slice_fusion.1
  18.6 0.1 copy.18
  18.7 1.3 copy.14
  19.9 0.4 constant_dynamic-slice_fusion
  20.3 0.2 copy.15
  20.5 0.1 copy.16
  20.6 0.1 copy.17
  20.7 0.1 dynamic_slice.12
  20.8 0.1 fusion
  20.9 0.6 pad.11.partner_ref
  21.5 0.7 pad.13.table_ref
  22.2 12.8 %shard_map.101.after_ref.m_ref = f32[64,256,128]{2,1,0:T(8,128)} custom-call(s32[64,192]{1,0:T(8,128)} %pad.11.partner_ref, s32[8,192,8]{2,1,0:T(8,128)} %bitcast.10, f32[384,128]{1,0:T(8,128)} %pad.13.table_ref), custom_call_target="tpu_custom_call" | custom-call | tf_op jit(solution)/shard_map/pallas_call | solution.py:362
  35.1 0.1 add_bitcast_fusion
  35.3 0.8 fusion.1
  36.0 10.9 %all-to-all-done.x_ref = f32[16,4,8,256]{3,2,1,0:T(8,128)S(1)} async-done(((f32[16,4,8,256]{3,2,1,0:T(8,128)}), f32[16,4,8,256]{3,2,1,0:T(8,128)S(1)}, u32[]{:S(2)}, u32[]{:S(2)}) %all-to-all-start) | async-done | bytes 524320 | tf_op jit(solution)/shard_map/all_to_all | solution.py:348
  46.9 1.7 %shard_map.102 = f32[32,4,8,128]{3,2,1,0:T(8,128)S(1)} custom-call(s32[64]{0:T(128)} %slot_ref.3, f32[16,4,8,256]{3,2,1,0:T(8,128)S(1)} %all-to-all-done.x_ref, bf16[2,128,256]{2,1,0:T(8,128)(2,1)S(1)} %copy-done.2, f32[8,512]{1,0:T(8,128)} %get-tuple-element.6.cos_ref, f32[8,512]{1,0:T(8,128)} %get-tuple-element.5.sin_ref, ...), custom_call_target="tpu_custom_call" | custom-call | tf_op jit(solution)/shard_map/pallas_call | solution.py:376
  48.6 18.2 %all_to_all.20.s_ref = f32[32,4,8,128]{3,2,1,0:T(8,128)S(1)} all-to-all(f32[32,4,8,128]{3,2,1,0:T(8,128)S(1)} %shard_map.102), channel_id=1, replica_groups=mesh['box'=32,'dir'=16] {'box'}, dimensions={0} | all-to-all | bytes 1048576 | tf_op jit(solution)/shard_map/all_to_all | solution.py:387
  66.8 12.8 %shard_map.103 = f32[8,4,8,128]{3,2,1,0:T(8,128)S(1)} custom-call(f32[32,4,8,128]{3,2,1,0:T(8,128)S(1)} %all_to_all.20.s_ref, f32[64,256,128]{2,1,0:T(8,128)} %shard_map.101.after_ref.m_ref), custom_call_target="tpu_custom_call" | custom-call | tf_op jit(solution)/shard_map/pallas_call | solution.py:388
  79.6 9.2 %all_to_all.21.x_ref = f32[8,4,8,128]{3,2,1,0:T(8,128)S(1)} all-to-all(f32[8,4,8,128]{3,2,1,0:T(8,128)S(1)} %shard_map.103), channel_id=1, replica_groups={{0,16,32,48,64,80,96,112},{128,144,160,176,192,208,224,240},{256,272,28..., dimensions={0} | all-to-all | bytes 262144 | tf_op jit(solution)/shard_map/all_to_all | solution.py:403
  88.8 2.2 %shard_map.104 = f32[16,4,8,256]{3,2,1,0:T(8,128)S(1)} custom-call(s32[64]{0:T(128)} %slot_ref.3, f32[8,4,8,128]{3,2,1,0:T(8,128)S(1)} %all_to_all.21.x_ref, bf16[2,256,128]{2,1,0:T(8,128)(2,1)S(1)} %copy-done.3, f32[8,512]{1,0:T(8,128)} %get-tuple-element.6.cos_ref, f32[8,512]{1,0:T(8,128)} %get-tuple-element.5.sin_ref), custom_call_target="tpu_custom_call" | custom-call | tf_op jit(solution)/shard_map/pallas_call | solution.py:406
  91.0 34.7 %all_to_all.22.y_ref = f32[16,4,8,256]{3,2,1,0:T(8,128)S(1)} all-to-all(f32[16,4,8,256]{3,2,1,0:T(8,128)S(1)} %shard_map.104), channel_id=1, replica_groups=mesh['box'=32,'dir'=16] {'dir'}, dimensions={0} | all-to-all | bytes 1048576 | tf_op jit(solution)/shard_map/all_to_all | solution.py:417
  125.7 1.5 %shard_map.105 = f32[4,8,2048]{2,1,0:T(8,128)} custom-call(f32[16,4,8,256]{3,2,1,0:T(8,128)S(1)} %all_to_all.22.y_ref, f32[8,64,128]{2,1,0:T(8,128)S(1)} %copy-done.1), custom_call_target="tpu_custom_call" | custom-call | tf_op jit(solution)/shard_map/pallas_call | solution.py:418
  (21 shorter events, 0.2 us)
Async XLA Ops:
  0.0 19.9 %copy-start = (f32[316,2,512]{2,1,0:T(2,128)S(1)}, f32[316,2,512]{2,1,0:T(2,128)}, u32[]{:S(2)}) copy-start(f32[316,2,512]{2,1,0:T(2,128)} %param.12) | copy-start | bytes 3883012
  0.0 18.4 %copy-start.5 = (s32[256,189]{0,1:T(8,128)S(1)}, s32[256,189]{0,1:T(8,128)}, u32[]{:S(2)}) copy-start(s32[256,189]{0,1:T(8,128)} %param.13) | copy-start | bytes 580612
  0.0 18.4 %copy-start.4 = (s32[256,189]{0,1:T(8,128)S(1)}, s32[256,189]{0,1:T(8,128)}, u32[]{:S(2)}) copy-start(s32[256,189]{0,1:T(8,128)} %param.14) | copy-start | bytes 580612
  3.2 43.7 %all-to-all-start = ((f32[16,4,8,256]{3,2,1,0:T(8,128)}), f32[16,4,8,256]{3,2,1,0:T(8,128)S(1)}, u32[]{:S(2)}, u32[]{:S(2)}) async-start(f32[16,4,8,256]{3,2,1,0:T(8,128)} %shard_map.100), calls=%async_computation | async-start | bytes 1048576 | tf_op jit(solution)/shard_map/all_to_all | solution.py:348
  18.7 2.0 %copy-start.6 = (s32[256]{0:T(256)S(1)}, s32[256]{0:T(256)}, u32[]{:S(2)}) copy-start(s32[256]{0:T(256)} %param.15) | copy-start | bytes 3076
  22.2 24.7 %copy-start.2 = (bf16[2,128,256]{2,1,0:T(8,128)(2,1)S(1)}, bf16[2,128,256]{2,1,0:T(8,128)(2,1)}, u32[]{:S(2)}) copy-start(bf16[2,128,256]{2,1,0:T(8,128)(2,1)} %constant.112.clone.w_ref) | copy-start | bytes 393220
  66.8 22.0 %copy-start.3 = (bf16[2,256,128]{2,1,0:T(8,128)(2,1)S(1)}, bf16[2,256,128]{2,1,0:T(8,128)(2,1)}, u32[]{:S(2)}) copy-start(bf16[2,256,128]{2,1,0:T(8,128)(2,1)} %constant.113.clone.w_ref) | copy-start | bytes 393220
  79.6 46.2 %copy-start.1 = (f32[8,64,128]{2,1,0:T(8,128)S(1)}, f32[8,64,128]{2,1,0:T(8,128)}, u32[]{:S(2)}) copy-start(f32[8,64,128]{2,1,0:T(8,128)} %constant.111.clone.c_ref) | copy-start | bytes 786436

commit v4 on v3

--- a/solution.py
+++ b/solution.py
@@ -163,12 +163,13 @@
                 o_ref[group * 8 + 2 * block + 1, j] = odd
 
 
-def matrix_kernel(partner_ref, kind_ref, table_ref, o_ref, both_ref, picked_ref):
+def matrix_kernel(partner_ref, kind_ref, table_ref, cos_ref, sin_ref, o_ref, token_ref, both_ref, picked_ref):
     @pl.when(pl.program_id(0) == 0)
     def _():
         high, low = split(table_ref[...])
         both_ref[:, :LANES] = high
         both_ref[:, LANES:] = low
+        token_ref[...] = jnp.zeros((8, LANES), f32)
 
     lane_kind = lax.broadcasted_iota(jnp.int32, (SLOTS, KINDS), 1)
     row_source = lax.broadcasted_iota(jnp.int32, (SOURCES, SLOTS), 0)
@@ -200,53 +201,54 @@
     return parts[0]
 
 
-def translate_kernel(s_ref, m_ref, o_ref, rows_ref, wide_ref):
+def translate_kernel(s_ref, m_far, o_ref, rows_ref, wide_ref, m_ref, arrived):
     low_half = lax.broadcasted_iota(jnp.int32, (8, LANES), 1) < PF
     top = lax.broadcasted_iota(jnp.int32, (8, LANES), 0) < 4
 
-    @pl.when(pl.program_id(0) == 0)
-    def _():
-        def pair(b, carry):
-            for j in range(4):
-                v = s_ref[b, j]
-                w = swap_halves(pltpu.roll(v, 4, 0))
-                rows_ref[pl.ds(b * 32 + j * 8, 8), :] = jnp.where(low_half == top, v, w)
-            return carry
-
-        lax.fori_loop(0, 32, pair, 0)
-
-        def spread(b, carry):
-            plain = [rows_ref[pl.ds(b * 32 + e, 8, stride=4), :] for e in range(4)]
-            both = [v + swap_halves(v) for v in plain]
-            for e in range(4):
-                wide_ref[b, e] = plain[e]
-            for h in range(2):
-                wide_ref[b, 4 + h] = jnp.where(low_half, both[2 * h], both[2 * h + 1])
-            return carry
-
-        lax.fori_loop(0, 32, spread, 0)
-
-    for q in range(2):
-
-        def step(b, sums):
-            sums = list(sums)
+    def fetch(g):
+        four = pl.ds(g * 4, 4)
+        return pltpu.make_async_copy(m_far.at[four], m_ref.at[four], arrived.at[g])
+
+    for g in range(TARGETS // 4):
+        fetch(g).start()
+
+    def pair(b, carry):
+        for j in range(4):
+            v = s_ref[b, j]
+            w = swap_halves(pltpu.roll(v, 4, 0))
+            rows_ref[pl.ds(b * 32 + j * 8, 8), :] = jnp.where(low_half == top, v, w)
+        return carry
+
+    lax.fori_loop(0, 32, pair, 0, unroll=4)
+
+    def spread(b, carry):
+        plain = [rows_ref[pl.ds(b * 32 + e, 8, stride=4), :] for e in range(4)]
+        both = [v + swap_halves(v) for v in plain]
+        for e in range(4):
+            wide_ref[b, e] = plain[e]
+        for h in range(2):
+            wide_ref[b, 4 + h] = jnp.where(low_half, both[2 * h], both[2 * h + 1])
+        return carry
+
+    lax.fori_loop(0, 32, spread, 0, unroll=4)
+
+    def four_targets(g, carry):
+        fetch(g).wait()
+        sums = [[jnp.zeros((8, LANES), f32) for _ in range(6)] for _ in range(4)]
+        for b in range(SOURCES // 8):
             source = [wide_ref[b, k] for k in range(6)]
             for p in range(4):
-                m = m_ref[4 * q + p, pl.ds(pl.multiple_of(b * 8, 8), 8), :]
+                m = m_ref[g * 4 + p, pl.ds(b * 8, 8), :]
                 t = m + swap_halves(m)
                 for k in range(6):
-                    sums[6 * p + k] = sums[6 * p + k] + source[k] * (m if k < 4 else t)
-            return tuple(sums)
-
-        sums = lax.fori_loop(0, SOURCES // 8, step, (jnp.zeros((8, LANES), f32),) * 24, unroll=True)
+                    sums[p][k] = sums[p][k] + source[k] * (m if k < 4 else t)
         real, imag = [], []
         for p in range(4):
-            part = sums[6 * p : 6 * p + 6]
-            turned = [swap_halves(v) for v in part[:4]]
-            real.append([a - b for a, b in zip(part[:4], turned)])
-            total = [a + b for a, b in zip(part[:4], turned)]
+            turned = [swap_halves(v) for v in sums[p][:4]]
+            real.append([x - y for x, y in zip(sums[p], turned)])
+            total = [x + y for x, y in zip(sums[p], turned)]
             imag.append(
-                [part[4 + h] - jnp.where(low_half, total[2 * h], total[2 * h + 1]) for h in range(2)]
+                [sums[p][4 + h] - jnp.where(low_half, total[2 * h], total[2 * h + 1]) for h in range(2)]
             )
         for j in range(2):
             a, b = 2 * j, 2 * j + 1
@@ -255,7 +257,10 @@
                 x, y = imag[a][h], imag[b][h]
                 parts.append(jnp.where(low_half, x, swap_halves(y)))
                 parts.append(jnp.where(low_half, swap_halves(x), y))
-            o_ref[pl.program_id(0), 2 * q + j] = fold_rows(parts)
+            o_ref[g // 2, (g % 2) * 2 + j] = fold_rows(parts)
+        return carry
+
+    lax.fori_loop(0, TARGETS // 4, four_targets, 0)
 
 
 def scatter_kernel(slot_ref, x_ref, w_ref, cos_ref, sin_ref, o_ref, plain_ref, turned_ref, child_ref):
@@ -321,6 +326,10 @@
     return pltpu.VMEM(dims, f32)
 
 
+def grant(mib):
+    return pltpu.CompilerParams(vmem_limit_bytes=mib << 20)
+
+
 def hold(x):
     return pltpu.with_memory_space_constraint(x, pltpu.VMEM)
 
@@ -344,6 +353,7 @@
         in_specs=[vmem, vmem],
         out_specs=vmem,
         scratch_shapes=[pltpu.VMEM((4, 8, 2, 8, LANES), f32)],
+        compiler_params=grant(8),
     )(outgoing, up)
     spread = lax.all_to_all(sent, "dir", split_axis=0, concat_axis=0, tiled=True)
 
@@ -359,46 +369,49 @@
     table = lax.dynamic_slice_in_dim(translator, chunk * CHUNK, CHUNK, 2)
     table = table.reshape(table.shape[0], LANES)
     table = jnp.pad(table, ((0, KINDS - table.shape[0]), (0, 0)))
-    matrix = pl.pallas_call(
+    cos_table, sin_table = phase_tables(dir_index)
+    matrix, token = pl.pallas_call(
         matrix_kernel,
         grid=(TARGETS // 8,),
         in_specs=[
             pl.BlockSpec((8, SLOTS), lambda i: (i, 0)),
             pl.BlockSpec((1, SLOTS, 8), lambda i: (i, 0, 0)),
             pl.BlockSpec((KINDS, LANES), lambda i: (0, 0)),
+            vmem,
+            vmem,
         ],
-        out_specs=pl.BlockSpec((8, SOURCES, LANES), lambda i: (i, 0, 0)),
-        out_shape=shape(TARGETS, SOURCES, LANES),
+        out_specs=[pl.BlockSpec((8, SOURCES, LANES), lambda i: (i, 0, 0)), vmem],
+        out_shape=[pltpu.HBM((TARGETS, SOURCES, LANES), f32), near(8, LANES)],
         scratch_shapes=[pltpu.VMEM((KINDS, 256), bf16), pltpu.VMEM((8 * SLOTS, 256), bf16)],
-    )(rows, kinds, table)
-    cos_table, sin_table = phase_tables(dir_index)
+        compiler_params=grant(16),
+    )(rows, kinds, table, hold(cos_table), hold(sin_table))
 
     packed = pl.pallas_call(
         gather_kernel,
         out_shape=near(32, 4, 8, LANES),
-        in_specs=[smem, vmem, vmem, vmem, vmem, pl.BlockSpec(memory_space=pl.ANY)],
+        in_specs=[smem, vmem, vmem, vmem, vmem, vmem],
         out_specs=vmem,
         scratch_shapes=[
             pltpu.VMEM((64, 8, 512), f32),
             pltpu.VMEM((8, 8, 512), f32),
             pltpu.SMEM((64,), jnp.int32),
         ],
-    )(fine_slot, hold(spread), hold(phi_up), cos_table, sin_table, matrix)
+        compiler_params=grant(16),
+    )(fine_slot, hold(spread), hold(phi_up), hold(cos_table), hold(sin_table), hold(token))
     everyone = lax.all_to_all(packed, "box", split_axis=0, concat_axis=0, tiled=True)
     incoming = pl.pallas_call(
         translate_kernel,
-        grid=(TARGETS // 8,),
-        in_specs=[
-            vmem,
-            pl.BlockSpec((8, SOURCES, LANES), lambda i: (i, 0, 0)),
-        ],
+        in_specs=[vmem, pl.BlockSpec(memory_space=pltpu.HBM)],
         out_specs=vmem,
         out_shape=near(8, 4, 8, LANES),
         scratch_shapes=[
             pltpu.VMEM((SOURCES * 4, LANES), f32),
             pltpu.VMEM((SOURCES // 8, 6, 8, LANES), f32),
+            pltpu.VMEM((TARGETS, SOURCES, LANES), f32),
+            pltpu.SemaphoreType.DMA((TARGETS // 4,)),
         ],
-    )(hold(everyone), matrix)
+        compiler_params=grant(16),
+    )(hold(everyone), pltpu.with_memory_space_constraint(matrix, pltpu.HBM))
     groups = [[8 * g + k for k in range(8)] for g in range(4)]
     fields = lax.all_to_all(
         incoming, "box", split_axis=0, concat_axis=0, axis_index_groups=groups, tiled=True
@@ -413,7 +426,8 @@
             pltpu.VMEM((8, 8, 512), f32),
             pltpu.VMEM((64, 8, 512), f32),
         ],
-    )(fine_slot, hold(fields), hold(phi_down), cos_table, sin_table)
+        compiler_params=grant(16),
+    )(fine_slot, hold(fields), hold(phi_down), hold(cos_table), hold(sin_table))
     back = lax.all_to_all(lowered, "dir", split_axis=0, concat_axis=0, tiled=True)
     return pl.pallas_call(
         theta_down_kernel,
@@ -421,6 +435,7 @@
         in_specs=[vmem, vmem],
         out_specs=vmem,
         scratch_shapes=[pltpu.VMEM((4, 16, 2, 8, LANES), f32)],
+        compiler_params=grant(8),
     )(hold(back), hold(down))
 
 

time: 128 us -> 122 us (0.953)
  the two profiles are of different devices: /device:TPU:32 before, /device:TPU:2 now
where the time goes in v4:
time: 122 us
  blocking collectives  61.6 us (50%)
  Pallas kernels  25.9 us (21%)
  waiting for transfers between devices  15.3 us (13%)
  starting transfers between devices  15.2 us (12%)
  local copies, waits for them, and re-layouts  3.37 us (3%)
    all_to_all x1, blocking collectives, body(): lax.all_to_all(lowered, 'dir', split_axis=0, concat_axis=0, tiled=True)  35 us
    all_to_all x1, blocking collectives, body(): lax.all_to_all(packed, 'box', split_axis=0, concat_axis=0, tiled=True)  17.2 us
    all_to_all x1, waiting for transfers between devices, body(): lax.all_to_all(sent, 'dir', split_axis=0, concat_axis=0, tiled=True)  15.3 us
    all_to_all x1, starting transfers between devices, body(): lax.all_to_all(sent, 'dir', split_axis=0, concat_axis=0, tiled=True)  15.2 us
    pallas_call x1, Pallas kernels, body(): pl.pallas_call(matrix_kernel, grid=(TARGETS // 8,), in_specs=[pl.BlockSpe...  11.7 us
    all_to_all x1, blocking collectives, body(): lax.all_to_all(incoming, 'box', split_axis=0, concat_axis=0, axis_index_g...  9.3 us
    pallas_call x1, Pallas kernels, body(): pl.pallas_call(translate_kernel, in_specs=[vmem, pl.BlockSpec(memory_spac...  7.08 us
  transfers between devices with their start and end apart: 1, of which 1 were waited for; matrix products, arithmetic and copies ran while one was open for 1% of the time, Pallas kernels for 10%

profile of v4, /device:TPU:2, one launch (start us, length us, event | category | flops | bytes accessed | tf_op | source)
XLA Modules:
  0.0 122.0 jit_solution(784701212677576137)
XLA Ops:
  0.0 1.1 copy-done.1
  1.1 0.9 copy-done.3
  2.0 2.1 %shard_map.100 = f32[16,4,8,256]{3,2,1,0:T(8,128)} custom-call(f32[4,8,2048]{2,1,0:T(8,128)S(1)} %copy-done.1, f32[16,32,128]{2,1,0:T(8,128)S(1)} %copy-done.3), custom_call_target="tpu_custom_call" | custom-call | tf_op jit(solution)/shard_map/pallas_call | solution.py:350
  4.1 15.2 %all-to-all-start = ((f32[16,4,8,256]{3,2,1,0:T(8,128)}), f32[16,4,8,256]{3,2,1,0:T(8,128)S(1)}, u32[]{:S(2)}, u32[]{:S(2)}) async-start(f32[16,4,8,256]{3,2,1,0:T(8,128)} %shard_map.100), calls=%async_computation | async-start | bytes 1048576 | tf_op jit(solution)/shard_map/all_to_all | solution.py:358
  19.4 0.1 constant_dynamic-slice_fusion.1
  19.5 0.1 copy.18
  19.6 0.3 copy.14
  19.9 0.4 constant_dynamic-slice_fusion
  20.3 0.2 copy.15
  20.5 0.1 copy.16
  20.6 0.1 copy.17
  20.7 0.1 dynamic_slice.12
  20.8 0.1 fusion
  21.0 0.1 add_bitcast_fusion
  21.2 0.1 fusion.1
  21.3 11.7 %shard_map.101 = (f32[64,256,128]{2,1,0:T(8,128)}, f32[8,128]{1,0:T(8,128)S(1)}) custom-call(s32[64,192]{1,0:T(8,128)S(1)} %pad.11.partner_ref, s32[8,192,8]{2,1,0:T(8,128)S(1)} %bitcast.10, f32[384,128]{1,0:T(8,128)S(1)} %pad.13.table_ref, f32[8,512]{1,0:T(8,128)S(1)} %get-tuple-element.10.cos_ref, f32[8,512]{1,0:T(8,128)S(1)} %get-tuple-element.9.sin_ref), custom_call_target="tpu_custom_call" | custom-call | tf_op jit(solution)/shard_map/pallas_call | solution.py:373
  33.1 15.3 %all-to-all-done.x_ref = f32[16,4,8,256]{3,2,1,0:T(8,128)S(1)} async-done(((f32[16,4,8,256]{3,2,1,0:T(8,128)}), f32[16,4,8,256]{3,2,1,0:T(8,128)S(1)}, u32[]{:S(2)}, u32[]{:S(2)}) %all-to-all-start) | async-done | bytes 524320 | tf_op jit(solution)/shard_map/all_to_all | solution.py:358
  48.4 1.5 %shard_map.102 = f32[32,4,8,128]{3,2,1,0:T(8,128)S(1)} custom-call(s32[64]{0:T(128)S(1)} %copy-done.6, f32[16,4,8,256]{3,2,1,0:T(8,128)S(1)} %all-to-all-done.x_ref, bf16[2,128,256]{2,1,0:T(8,128)(2,1)S(1)} %copy-done.4, f32[8,512]{1,0:T(8,128)S(1)} %get-tuple-element.10.cos_ref, f32[8,512]{1,0:T(8,128)S(1)} %get-tuple-element.9.sin_ref, ...), custom_call_target="tpu_custom_call" | custom-call | tf_op jit(solution)/shard_map/pallas_call | solution.py:389
  49.8 17.2 %all_to_all.20.s_ref = f32[32,4,8,128]{3,2,1,0:T(8,128)S(1)} all-to-all(f32[32,4,8,128]{3,2,1,0:T(8,128)S(1)} %shard_map.102), channel_id=1, replica_groups=mesh['box'=32,'dir'=16] {'box'}, dimensions={0} | all-to-all | bytes 1048576 | tf_op jit(solution)/shard_map/all_to_all | solution.py:401
  67.1 7.1 %shard_map.103 = f32[8,4,8,128]{3,2,1,0:T(8,128)S(1)} custom-call(f32[32,4,8,128]{3,2,1,0:T(8,128)S(1)} %all_to_all.20.s_ref, f32[64,256,128]{2,1,0:T(8,128)} %get-tuple-element.8.m_far), custom_call_target="tpu_custom_call" | custom-call | tf_op jit(solution)/shard_map/pallas_call | solution.py:402
  74.2 9.3 %all_to_all.21.x_ref = f32[8,4,8,128]{3,2,1,0:T(8,128)S(1)} all-to-all(f32[8,4,8,128]{3,2,1,0:T(8,128)S(1)} %shard_map.103), channel_id=1, replica_groups={{0,16,32,48,64,80,96,112},{128,144,160,176,192,208,224,240},{256,272,28..., dimensions={0} | all-to-all | bytes 262144 | tf_op jit(solution)/shard_map/all_to_all | solution.py:416
  83.5 2.0 %shard_map.104 = f32[16,4,8,256]{3,2,1,0:T(8,128)S(1)} custom-call(s32[64]{0:T(128)S(1)} %copy-done.6, f32[8,4,8,128]{3,2,1,0:T(8,128)S(1)} %all_to_all.21.x_ref, bf16[2,256,128]{2,1,0:T(8,128)(2,1)S(1)} %copy-done.5, f32[8,512]{1,0:T(8,128)S(1)} %get-tuple-element.10.cos_ref, f32[8,512]{1,0:T(8,128)S(1)} %get-tuple-element.9.sin_ref), custom_call_target="tpu_custom_call" | custom-call | tf_op jit(solution)/shard_map/pallas_call | solution.py:419
  85.5 35.0 %all_to_all.22.y_ref = f32[16,4,8,256]{3,2,1,0:T(8,128)S(1)} all-to-all(f32[16,4,8,256]{3,2,1,0:T(8,128)S(1)} %shard_map.104), channel_id=1, replica_groups=mesh['box'=32,'dir'=16] {'dir'}, dimensions={0} | all-to-all | bytes 1048576 | tf_op jit(solution)/shard_map/all_to_all | solution.py:431
  120.5 1.5 %shard_map.105 = f32[4,8,2048]{2,1,0:T(8,128)} custom-call(f32[16,4,8,256]{3,2,1,0:T(8,128)S(1)} %all_to_all.22.y_ref, f32[8,64,128]{2,1,0:T(8,128)S(1)} %copy-done.2), custom_call_target="tpu_custom_call" | custom-call | tf_op jit(solution)/shard_map/pallas_call | solution.py:432
  (27 shorter events, 0.3 us)
Async XLA Ops:
  0.0 19.9 %copy-start = (f32[316,2,512]{2,1,0:T(2,128)S(1)}, f32[316,2,512]{2,1,0:T(2,128)}, u32[]{:S(2)}) copy-start(f32[316,2,512]{2,1,0:T(2,128)} %param.12) | copy-start | bytes 3883012
  0.0 1.1 copy-start.1
  1.1 0.9 copy-start.3
  2.0 17.3 %copy-start.7 = (s32[256,189]{0,1:T(8,128)S(1)}, s32[256,189]{0,1:T(8,128)}, u32[]{:S(2)}) copy-start(s32[256,189]{0,1:T(8,128)} %param.14) | copy-start | bytes 580612
  2.0 17.3 %copy-start.8 = (s32[256,189]{0,1:T(8,128)S(1)}, s32[256,189]{0,1:T(8,128)}, u32[]{:S(2)}) copy-start(s32[256,189]{0,1:T(8,128)} %param.13) | copy-start | bytes 580612
  4.1 44.3 %all-to-all-start = ((f32[16,4,8,256]{3,2,1,0:T(8,128)}), f32[16,4,8,256]{3,2,1,0:T(8,128)S(1)}, u32[]{:S(2)}, u32[]{:S(2)}) async-start(f32[16,4,8,256]{3,2,1,0:T(8,128)} %shard_map.100), calls=%async_computation | async-start | bytes 1048576 | tf_op jit(solution)/shard_map/all_to_all | solution.py:358
  19.6 1.1 copy-start.9
  20.3 28.1 %copy-start.4 = (bf16[2,128,256]{2,1,0:T(8,128)(2,1)S(1)}, bf16[2,128,256]{2,1,0:T(8,128)(2,1)}, u32[]{:S(2)}) copy-start(bf16[2,128,256]{2,1,0:T(8,128)(2,1)} %constant.112.clone.w_ref) | copy-start | bytes 393220
  20.3 28.1 %copy-start.6 = (s32[64]{0:T(128)S(1)}, s32[64]{0:T(128)}, u32[]{:S(2)}) copy-start(s32[64]{0:T(128)} %slot_ref.3) | copy-start | bytes 772
  67.1 16.4 %copy-start.5 = (bf16[2,256,128]{2,1,0:T(8,128)(2,1)S(1)}, bf16[2,256,128]{2,1,0:T(8,128)(2,1)}, u32[]{:S(2)}) copy-start(bf16[2,256,128]{2,1,0:T(8,128)(2,1)} %constant.113.clone.w_ref) | copy-start | bytes 393220
  74.1 46.4 %copy-start.2 = (f32[8,64,128]{2,1,0:T(8,128)S(1)}, f32[8,64,128]{2,1,0:T(8,128)}, u32[]{:S(2)}) copy-start(f32[8,64,128]{2,1,0:T(8,128)} %constant.111.clone.c_ref) | copy-start | bytes 786436

commit v5 on v4

--- a/solution.py
+++ b/solution.py
@@ -55,7 +55,7 @@
 def split_constant(x):
     high = np.asarray(x, np.float32).astype(jnp.bfloat16)
     low = (np.asarray(x, np.float32) - high.astype(np.float32)).astype(jnp.bfloat16)
-    return np.stack([high, low])
+    return high, low
 
 
 def swap_halves(x):
@@ -88,8 +88,23 @@
     return out
 
 
-def theta_up_kernel(x_ref, c_ref, o_ref, parity_ref):
+def theta_up_kernel(x_far, c_far, o_far, x_ref, c_ref, o_ref, parity_ref, x_in, c_in, o_out):
+    def get_x(f):
+        return pltpu.make_async_copy(x_far.at[f], x_ref.at[f], x_in.at[f])
+
+    def get_c(z):
+        two = pl.ds(2 * z, 2)
+        return pltpu.make_async_copy(c_far.at[two], c_ref.at[two], c_in.at[z])
+
+    def put(z):
+        return pltpu.make_async_copy(o_ref.at[z], o_far.at[z], o_out.at[z])
+
     for f in range(4):
+        get_x(f).start()
+    for z in range(8):
+        get_c(z).start()
+    for f in range(4):
+        get_x(f).wait()
         for i in range(8):
             v = x_ref[f, :, pl.ds(i * LANES, LANES)]
             w = swap_halves(x_ref[f, :, pl.ds((15 - i) * LANES, LANES)])
@@ -97,17 +112,26 @@
             parity_ref[f, i, 1] = v - w
 
     def step(z, carry):
+        get_c(z).wait()
         for part in range(2):
             out = theta_step(parity_ref, c_ref, 2 * z + part, 8)
             for f in range(4):
                 o_ref[z, f, :, pl.ds(part * LANES, LANES)] = out[f][0]
                 o_ref[15 - z, f, :, pl.ds((1 - part) * LANES, LANES)] = out[f][1]
+        put(z).start()
+        put(15 - z).start()
         return carry
 
     lax.fori_loop(0, 8, step, 0)
-
-
-def theta_down_kernel(y_ref, c_ref, o_ref, parity_ref):
+    for z in range(16):
+        put(z).wait()
+
+
+def theta_down_kernel(y_ref, c_ref, o_far, o_ref, parity_ref, o_out):
+    def put(j):
+        block = pl.ds(j * LANES, LANES)
+        return pltpu.make_async_copy(o_ref.at[:, :, block], o_far.at[:, :, block], o_out.at[j])
+
     for f in range(4):
         for i in range(16):
             v = y_ref[i // 2, f, :, pl.ds(i % 2 * LANES, LANES)]
@@ -119,6 +143,10 @@
         for f in range(4):
             o_ref[f, :, pl.ds(j * LANES, LANES)] = out[f][0]
             o_ref[f, :, pl.ds((15 - j) * LANES, LANES)] = out[f][1]
+        put(j).start()
+        put(15 - j).start()
+    for j in range(16):
+        put(j).wait()
 
 
 def channel_sign():
@@ -131,12 +159,9 @@
         inv_ref[slot_ref[i] % 64] = i
     for j in range(2):
         high, low = split(x_ref[:, :, :, pl.ds(j * LANES, LANES)].reshape(512, LANES))
-        wh, wl = w_ref[0], w_ref[1]
-        part = (
-            jnp.dot(high, wh, preferred_element_type=f32)
-            + jnp.dot(low, wh, preferred_element_type=f32)
-            + jnp.dot(high, wl, preferred_element_type=f32)
-        )
+        both = jnp.concatenate([high, low], 1)
+        part = jnp.dot(both, w_ref[:256], preferred_element_type=f32)
+        part = part + jnp.dot(high, w_ref[256:], preferred_element_type=f32)
         raised_ref[:, :, pl.ds(j * 256, 256)] = part.reshape(64, 8, 256)
     sign = channel_sign()
 
@@ -289,12 +314,9 @@
     lax.fori_loop(0, 64, step, 0, unroll=4)
     for j in range(2):
         high, low = split(child_ref[:, :, pl.ds(j * 256, 256)].reshape(512, 256))
-        wh, wl = w_ref[0], w_ref[1]
-        part = (
-            jnp.dot(high, wh, preferred_element_type=f32)
-            + jnp.dot(low, wh, preferred_element_type=f32)
-            + jnp.dot(high, wl, preferred_element_type=f32)
-        )
+        part = jnp.dot(high, w_ref[...], preferred_element_type=f32)
+        part = part[:, :LANES] + part[:, LANES:]
+        part = part + jnp.dot(low, w_ref[:, :LANES], preferred_element_type=f32)
         o_ref[:, :, :, pl.ds(j * LANES, LANES)] = part.reshape(16, 4, 8, LANES)
 
 
@@ -316,6 +338,7 @@
 
 vmem = pl.BlockSpec(memory_space=pltpu.VMEM)
 smem = pl.BlockSpec(memory_space=pltpu.SMEM)
+hbm = pl.BlockSpec(memory_space=pltpu.HBM)
 
 
 def shape(*dims):
@@ -328,6 +351,10 @@
 
 def grant(mib):
     return pltpu.CompilerParams(vmem_limit_bytes=mib << 20)
+
+
+def far(x):
+    return pltpu.with_memory_space_constraint(x, pltpu.HBM)
 
 
 def hold(x):
@@ -344,17 +371,27 @@
     up = jnp.asarray(parity_table(theta))
     down = jnp.asarray(parity_table(theta.T * (TF / TP)))
     phi = phi_matrix()
-    phi_up = jnp.asarray(split_constant(np.kron(np.eye(2), phi.T)))
-    phi_down = jnp.asarray(split_constant(np.kron(np.eye(2), phi) * (PF / PP)))
+    high, low = split_constant(np.kron(np.eye(2), phi.T))
+    phi_up = jnp.asarray(np.concatenate([high, high, low], 0))
+    high, low = split_constant(np.kron(np.eye(2), phi) * (PF / PP))
+    phi_down = jnp.asarray(np.concatenate([high, low], 1))
 
     sent = pl.pallas_call(
         theta_up_kernel,
-        out_shape=near(16, 4, 8, 256),
-        in_specs=[vmem, vmem],
-        out_specs=vmem,
-        scratch_shapes=[pltpu.VMEM((4, 8, 2, 8, LANES), f32)],
+        out_shape=pltpu.HBM((16, 4, 8, 256), f32),
+        in_specs=[hbm, hbm],
+        out_specs=hbm,
+        scratch_shapes=[
+            pltpu.VMEM((4, 8, TF * PF), f32),
+            pltpu.VMEM((16, 32, LANES), f32),
+            pltpu.VMEM((16, 4, 8, 256), f32),
+            pltpu.VMEM((4, 8, 2, 8, LANES), f32),
+            pltpu.SemaphoreType.DMA((4,)),
+            pltpu.SemaphoreType.DMA((8,)),
+            pltpu.SemaphoreType.DMA((16,)),
+        ],
         compiler_params=grant(8),
-    )(outgoing, up)
+    )(far(outgoing), far(up))
     spread = lax.all_to_all(sent, "dir", split_axis=0, concat_axis=0, tiled=True)
 
     rows = lax.dynamic_slice_in_dim(list_partner, group * TARGETS, TARGETS, 0)
@@ -401,7 +438,7 @@
     everyone = lax.all_to_all(packed, "box", split_axis=0, concat_axis=0, tiled=True)
     incoming = pl.pallas_call(
         translate_kernel,
-        in_specs=[vmem, pl.BlockSpec(memory_space=pltpu.HBM)],
+        in_specs=[vmem, hbm],
         out_specs=vmem,
         out_shape=near(8, 4, 8, LANES),
         scratch_shapes=[
@@ -411,7 +448,7 @@
             pltpu.SemaphoreType.DMA((TARGETS // 4,)),
         ],
         compiler_params=grant(16),
-    )(hold(everyone), pltpu.with_memory_space_constraint(matrix, pltpu.HBM))
+    )(hold(everyone), far(matrix))
     groups = [[8 * g + k for k in range(8)] for g in range(4)]
     fields = lax.all_to_all(
         incoming, "box", split_axis=0, concat_axis=0, axis_index_groups=groups, tiled=True
@@ -433,8 +470,12 @@
         theta_down_kernel,
         out_shape=shape(4, 8, TF * PF),
         in_specs=[vmem, vmem],
-        out_specs=vmem,
-        scratch_shapes=[pltpu.VMEM((4, 16, 2, 8, LANES), f32)],
+        out_specs=hbm,
+        scratch_shapes=[
+            pltpu.VMEM((4, 8, TF * PF), f32),
+            pltpu.VMEM((4, 16, 2, 8, LANES), f32),
+            pltpu.SemaphoreType.DMA((16,)),
+        ],
         compiler_params=grant(8),
     )(hold(back), hold(down))
 

time: 122 us -> 121 us (level)
  local copies, waits for them, and re-layouts: 3.37 us -> 1.36 us
    unnamed x22 -> x18, local copies, waits for them, and re-layouts: 2.21 us -> 0.21 us
    pallas_call x2, Pallas kernels: 9.17 us -> 10.5 us  [the longest x1 7.08 us: body(): pl.pallas_call(translate_kernel, in_specs=[vmem, hbm], out_specs=vmem, ou...]
where the time goes in v5:
time: 121 us
  blocking collectives  61.5 us (51%)
  Pallas kernels  27 us (22%)
  waiting for transfers between devices  15.3 us (13%)
  starting transfers between devices  15.2 us (13%)
  local copies, waits for them, and re-layouts  1.36 us (1%)
    all_to_all x1, blocking collectives, body(): lax.all_to_all(lowered, 'dir', split_axis=0, concat_axis=0, tiled=True)  35 us
    all_to_all x1, blocking collectives, body(): lax.all_to_all(packed, 'box', split_axis=0, concat_axis=0, tiled=True)  17.2 us
    all_to_all x1, waiting for transfers between devices, body(): lax.all_to_all(sent, 'dir', split_axis=0, concat_axis=0, tiled=True)  15.3 us
    all_to_all x1, starting transfers between devices, body(): lax.all_to_all(sent, 'dir', split_axis=0, concat_axis=0, tiled=True)  15.2 us
    pallas_call x1, Pallas kernels, body(): pl.pallas_call(matrix_kernel, grid=(TARGETS // 8,), in_specs=[pl.BlockSpe...  11.8 us
    all_to_all x1, blocking collectives, body(): lax.all_to_all(incoming, 'box', split_axis=0, concat_axis=0, axis_index_g...  9.3 us
    pallas_call x1, Pallas kernels, body(): pl.pallas_call(translate_kernel, in_specs=[vmem, hbm], out_specs=vmem, ou...  7.08 us
    pallas_call x1, Pallas kernels, body(): pl.pallas_call(theta_up_kernel, out_shape=pltpu.HBM((16, 4, 8, 256), f32)...  3.39 us
  transfers between devices with their start and end apart: 1, of which 1 were waited for; matrix products, arithmetic and copies ran while one was open for 1% of the time, Pallas kernels for 10%

profile of v5, /device:TPU:2, one launch (start us, length us, event | category | flops | bytes accessed | tf_op | source)
XLA Modules:
  0.0 121.1 jit_solution(4606094941012757616)
XLA Ops:
  0.0 3.4 %shard_map.100 = f32[16,4,8,256]{3,2,1,0:T(8,128)} custom-call(f32[4,8,2048]{2,1,0:T(8,128)} %x_far.1, f32[16,32,128]{2,1,0:T(8,128)} %constant.110.clone.c_far), custom_call_target="tpu_custom_call" | custom-call | tf_op jit(solution)/shard_map/pallas_call | solution.py:379
  3.4 15.2 %all-to-all-start = ((f32[16,4,8,256]{3,2,1,0:T(8,128)}), f32[16,4,8,256]{3,2,1,0:T(8,128)S(1)}, u32[]{:S(2)}, u32[]{:S(2)}) async-start(f32[16,4,8,256]{3,2,1,0:T(8,128)} %shard_map.100), calls=%async_computation | async-start | bytes 1048576 | tf_op jit(solution)/shard_map/all_to_all | solution.py:395
  18.7 0.1 constant_dynamic-slice_fusion.1
  18.8 0.1 copy.18
  18.9 0.3 copy.14
  19.2 0.4 constant_dynamic-slice_fusion
  19.6 0.2 copy.15
  19.8 0.1 copy.16
  19.9 0.1 copy.17
  20.0 0.1 dynamic_slice.12
  20.1 0.1 fusion
  20.3 0.1 add_bitcast_fusion
  20.4 0.1 multiply_bitcast_fusion.1
  20.5 0.1 fusion.1
  20.6 11.8 %shard_map.101 = (f32[64,256,128]{2,1,0:T(8,128)}, f32[8,128]{1,0:T(8,128)S(1)}) custom-call(s32[64,192]{1,0:T(8,128)S(1)} %pad.11.partner_ref, s32[8,192,8]{2,1,0:T(8,128)S(1)} %bitcast.10, f32[384,128]{1,0:T(8,128)S(1)} %pad.13.table_ref, f32[8,512]{1,0:T(8,128)S(1)} %get-tuple-element.10.cos_ref, f32[8,512]{1,0:T(8,128)S(1)} %get-tuple-element.9.sin_ref), custom_call_target="tpu_custom_call" | custom-call | tf_op jit(solution)/shard_map/pallas_call | solution.py:410
  32.4 15.3 %all-to-all-done.x_ref = f32[16,4,8,256]{3,2,1,0:T(8,128)S(1)} async-done(((f32[16,4,8,256]{3,2,1,0:T(8,128)}), f32[16,4,8,256]{3,2,1,0:T(8,128)S(1)}, u32[]{:S(2)}, u32[]{:S(2)}) %all-to-all-start) | async-done | bytes 524320 | tf_op jit(solution)/shard_map/all_to_all | solution.py:395
  47.7 1.3 %shard_map.102 = f32[32,4,8,128]{3,2,1,0:T(8,128)S(1)} custom-call(s32[64]{0:T(128)S(1)} %copy-done.4, f32[16,4,8,256]{3,2,1,0:T(8,128)S(1)} %all-to-all-done.x_ref, bf16[384,256]{1,0:T(8,128)(2,1)S(1)} %copy-done.2, f32[8,512]{1,0:T(8,128)S(1)} %get-tuple-element.10.cos_ref, f32[8,512]{1,0:T(8,128)S(1)} %get-tuple-element.9.sin_ref, ...), custom_call_target="tpu_custom_call" | custom-call | tf_op jit(solution)/shard_map/pallas_call | solution.py:426
  49.0 17.2 %all_to_all.20.s_ref = f32[32,4,8,128]{3,2,1,0:T(8,128)S(1)} all-to-all(f32[32,4,8,128]{3,2,1,0:T(8,128)S(1)} %shard_map.102), channel_id=1, replica_groups=mesh['box'=32,'dir'=16] {'box'}, dimensions={0} | all-to-all | bytes 1048576 | tf_op jit(solution)/shard_map/all_to_all | solution.py:438
  66.2 7.1 %shard_map.103 = f32[8,4,8,128]{3,2,1,0:T(8,128)S(1)} custom-call(f32[32,4,8,128]{3,2,1,0:T(8,128)S(1)} %all_to_all.20.s_ref, f32[64,256,128]{2,1,0:T(8,128)} %get-tuple-element.8.m_far), custom_call_target="tpu_custom_call" | custom-call | tf_op jit(solution)/shard_map/pallas_call | solution.py:439
  73.3 0.0 copy-start.1
  73.3 9.3 %all_to_all.21.x_ref = f32[8,4,8,128]{3,2,1,0:T(8,128)S(1)} all-to-all(f32[8,4,8,128]{3,2,1,0:T(8,128)S(1)} %shard_map.103), channel_id=1, replica_groups={{0,16,32,48,64,80,96,112},{128,144,160,176,192,208,224,240},{256,272,28..., dimensions={0} | all-to-all | bytes 262144 | tf_op jit(solution)/shard_map/all_to_all | solution.py:453
  82.7 1.9 %shard_map.104 = f32[16,4,8,256]{3,2,1,0:T(8,128)S(1)} custom-call(s32[64]{0:T(128)S(1)} %copy-done.4, f32[8,4,8,128]{3,2,1,0:T(8,128)S(1)} %all_to_all.21.x_ref, bf16[256,256]{1,0:T(8,128)(2,1)S(1)} %copy-done.3, f32[8,512]{1,0:T(8,128)S(1)} %get-tuple-element.10.cos_ref, f32[8,512]{1,0:T(8,128)S(1)} %get-tuple-element.9.sin_ref), custom_call_target="tpu_custom_call" | custom-call | tf_op jit(solution)/shard_map/pallas_call | solution.py:456
  84.6 35.0 %all_to_all.22.y_ref = f32[16,4,8,256]{3,2,1,0:T(8,128)S(1)} all-to-all(f32[16,4,8,256]{3,2,1,0:T(8,128)S(1)} %shard_map.104), channel_id=1, replica_groups=mesh['box'=32,'dir'=16] {'dir'}, dimensions={0} | all-to-all | bytes 1048576 | tf_op jit(solution)/shard_map/all_to_all | solution.py:468
  119.6 1.6 %shard_map.105 = f32[4,8,2048]{2,1,0:T(8,128)} custom-call(f32[16,4,8,256]{3,2,1,0:T(8,128)S(1)} %all_to_all.22.y_ref, f32[8,64,128]{2,1,0:T(8,128)S(1)} %copy-done.1), custom_call_target="tpu_custom_call" | custom-call | tf_op jit(solution)/shard_map/pallas_call | solution.py:469
  (23 shorter events, 0.2 us)
Async XLA Ops:
  0.0 19.2 %copy-start = (f32[316,2,512]{2,1,0:T(2,128)S(1)}, f32[316,2,512]{2,1,0:T(2,128)}, u32[]{:S(2)}) copy-start(f32[316,2,512]{2,1,0:T(2,128)} %param.12) | copy-start | bytes 3883012
  0.0 18.6 %copy-start.6 = (s32[256,189]{0,1:T(8,128)S(1)}, s32[256,189]{0,1:T(8,128)}, u32[]{:S(2)}) copy-start(s32[256,189]{0,1:T(8,128)} %param.13) | copy-start | bytes 580612
  0.0 18.7 %copy-start.5 = (s32[256,189]{0,1:T(8,128)S(1)}, s32[256,189]{0,1:T(8,128)}, u32[]{:S(2)}) copy-start(s32[256,189]{0,1:T(8,128)} %param.14) | copy-start | bytes 580612
  3.4 44.3 %all-to-all-start = ((f32[16,4,8,256]{3,2,1,0:T(8,128)}), f32[16,4,8,256]{3,2,1,0:T(8,128)S(1)}, u32[]{:S(2)}, u32[]{:S(2)}) async-start(f32[16,4,8,256]{3,2,1,0:T(8,128)} %shard_map.100), calls=%async_computation | async-start | bytes 1048576 | tf_op jit(solution)/shard_map/all_to_all | solution.py:395
  18.9 1.1 copy-start.7
  19.6 28.1 %copy-start.2 = (bf16[384,256]{1,0:T(8,128)(2,1)S(1)}, bf16[384,256]{1,0:T(8,128)(2,1)}, u32[]{:S(2)}) copy-start(bf16[384,256]{1,0:T(8,128)(2,1)} %constant.112.clone.w_ref) | copy-start | bytes 589828
  19.6 28.1 %copy-start.4 = (s32[64]{0:T(128)S(1)}, s32[64]{0:T(128)}, u32[]{:S(2)}) copy-start(s32[64]{0:T(128)} %slot_ref.3) | copy-start | bytes 772
  66.2 16.4 %copy-start.3 = (bf16[256,256]{1,0:T(8,128)(2,1)S(1)}, bf16[256,256]{1,0:T(8,128)(2,1)}, u32[]{:S(2)}) copy-start(bf16[256,256]{1,0:T(8,128)(2,1)} %constant.113.clone.w_ref) | copy-start | bytes 393220
  73.3 46.2 %copy-start.1 = (f32[8,64,128]{2,1,0:T(8,128)S(1)}, f32[8,64,128]{2,1,0:T(8,128)}, u32[]{:S(2)}) copy-start(f32[8,64,128]{2,1,0:T(8,128)} %constant.111.clone.c_ref) | copy-start | bytes 786436

commit v6 on v5

--- a/solution.py
+++ b/solution.py
@@ -71,21 +71,25 @@
 
 def theta_step(parity_ref, c_ref, j, count):
     zero = jnp.zeros((8, LANES), f32)
-    sums = [[zero] * 4 for _ in range(4)]
+    sums = [[[zero] * 4 for _ in range(4)] for _ in range(2)]
     for i in range(count):
         for odd in range(2):
             base = odd * 2 * count + 2 * i
-            cs = c_ref[j, pl.ds(base, 1), :]
-            cx = c_ref[j, pl.ds(base + 1, 1), :]
+            scales = [
+                [c_ref[j + part, pl.ds(base + k, 1), :] for k in range(2)] for part in range(2)
+            ]
             for f in range(4):
                 v = parity_ref[f, i, odd]
-                sums[2 * odd][f] = sums[2 * odd][f] + cs * v
-                sums[2 * odd + 1][f] = sums[2 * odd + 1][f] + cx * v
+                for part in range(2):
+                    for k in range(2):
+                        old = sums[part][2 * odd + k][f]
+                        sums[part][2 * odd + k][f] = old + scales[part][k] * v
     out = []
-    for f in range(4):
-        es, ex, os, ox = (sums[k][f] for k in range(4))
-        out.append(((es + os) + swap_halves(ex + ox), swap_halves(es - os) + (ex - ox)))
-    return out
+    for part in range(2):
+        for f in range(4):
+            es, ex, os, ox = (sums[part][k][f] for k in range(4))
+            out.append(((es + os) + swap_halves(ex + ox), swap_halves(es - os) + (ex - ox)))
+    return out[:4], out[4:]
 
 
 def theta_up_kernel(x_far, c_far, o_far, x_ref, c_ref, o_ref, parity_ref, x_in, c_in, o_out):
@@ -113,8 +117,8 @@
 
     def step(z, carry):
         get_c(z).wait()
-        for part in range(2):
-            out = theta_step(parity_ref, c_ref, 2 * z + part, 8)
+        both = theta_step(parity_ref, c_ref, 2 * z, 8)
+        for part, out in enumerate(both):
             for f in range(4):
                 o_ref[z, f, :, pl.ds(part * LANES, LANES)] = out[f][0]
                 o_ref[15 - z, f, :, pl.ds((1 - part) * LANES, LANES)] = out[f][1]
@@ -129,7 +133,7 @@
 
 def theta_down_kernel(y_ref, c_ref, o_far, o_ref, parity_ref, o_out):
     def put(j):
-        block = pl.ds(j * LANES, LANES)
+        block = pl.ds(pl.multiple_of(j * LANES, LANES), LANES)
         return pltpu.make_async_copy(o_ref.at[:, :, block], o_far.at[:, :, block], o_out.at[j])
 
     for f in range(4):
@@ -138,13 +142,20 @@
             w = swap_halves(y_ref[15 - i // 2, f, :, pl.ds((1 - i % 2) * LANES, LANES)])
             parity_ref[f, i, 0] = v + w
             parity_ref[f, i, 1] = v - w
-    for j in range(8):
-        out = theta_step(parity_ref, c_ref, j, 16)
-        for f in range(4):
-            o_ref[f, :, pl.ds(j * LANES, LANES)] = out[f][0]
-            o_ref[f, :, pl.ds((15 - j) * LANES, LANES)] = out[f][1]
-        put(j).start()
-        put(15 - j).start()
+
+    def step(q, carry):
+        both = theta_step(parity_ref, c_ref, 2 * q, 16)
+        for part, out in enumerate(both):
+            j = 2 * q + part
+            for f in range(4):
+                o_ref[f, :, pl.ds(pl.multiple_of(j * LANES, LANES), LANES)] = out[f][0]
+                o_ref[f, :, pl.ds(pl.multiple_of((15 - j) * LANES, LANES), LANES)] = out[f][1]
+            put(j).start()
+            put(15 - j).start()
+        return carry
+
+    for q in range(4):
+        step(q, 0)
     for j in range(16):
         put(j).wait()
 
@@ -154,9 +165,7 @@
     return jnp.where(row < 4, 1.0, -1.0).astype(f32)
 
 
-def gather_kernel(slot_ref, x_ref, w_ref, cos_ref, sin_ref, after_ref, o_ref, raised_ref, parent_ref, inv_ref):
-    for i in range(64):
-        inv_ref[slot_ref[i] % 64] = i
+def gather_kernel(inv_ref, x_ref, w_ref, cos_ref, sin_ref, after_ref, o_ref, raised_ref, parent_ref):
     for j in range(2):
         high, low = split(x_ref[:, :, :, pl.ds(j * LANES, LANES)].reshape(512, LANES))
         both = jnp.concatenate([high, low], 1)
@@ -175,7 +184,7 @@
         parent_ref[p] = plain + sign * pltpu.roll(turned, 4, 0)
         return carry
 
-    lax.fori_loop(0, 8, step, 0)
+    lax.fori_loop(0, 8, step, 0, unroll=4)
     low_half = lax.broadcasted_iota(jnp.int32, (8, LANES), 1) < PF
     for j in range(4):
         for block in range(4):
@@ -288,7 +297,7 @@
     lax.fori_loop(0, TARGETS // 4, four_targets, 0)
 
 
-def scatter_kernel(slot_ref, x_ref, w_ref, cos_ref, sin_ref, o_ref, plain_ref, turned_ref, child_ref):
+def scatter_kernel(inv_ref, x_ref, w_ref, cos_ref, sin_ref, o_ref, plain_ref, child_ref):
     low_half = lax.broadcasted_iota(jnp.int32, (8, LANES), 1) < PF
     for block in range(4):
         for j in range(4):
@@ -299,19 +308,17 @@
             plain_ref[2 * j, :, pl.ds(block * LANES, LANES)] = first
             plain_ref[2 * j + 1, :, pl.ds(block * LANES, LANES)] = second
     sign = channel_sign()
-    for p in range(8):
-        turned_ref[p] = -sign * pltpu.roll(plain_ref[p], 4, 0)
-
-    def step(f, carry):
-        s = slot_ref[f] % 64
-        p = s // 8
-        o = s % 8
-        child_ref[f] = (
-            plain_ref[p] * cos_ref[pl.ds(o, 1), :] + turned_ref[p] * sin_ref[pl.ds(o, 1), :]
-        )
-        return carry
-
-    lax.fori_loop(0, 64, step, 0, unroll=4)
+
+    def step(p, carry):
+        plain = plain_ref[p]
+        turned = -sign * pltpu.roll(plain, 4, 0)
+        for o in range(8):
+            child_ref[inv_ref[p * 8 + o]] = (
+                plain * cos_ref[pl.ds(o, 1), :] + turned * sin_ref[pl.ds(o, 1), :]
+            )
+        return carry
+
+    lax.fori_loop(0, 8, step, 0, unroll=4)
     for j in range(2):
         high, low = split(child_ref[:, :, pl.ds(j * 256, 256)].reshape(512, 256))
         part = jnp.dot(high, w_ref[...], preferred_element_type=f32)
@@ -407,6 +414,9 @@
     table = table.reshape(table.shape[0], LANES)
     table = jnp.pad(table, ((0, KINDS - table.shape[0]), (0, 0)))
     cos_table, sin_table = phase_tables(dir_index)
+    place = jnp.arange(64, dtype=jnp.int32)
+    found = fine_slot[None, :] % 64 == place[:, None]
+    inverse = jnp.sum(jnp.where(found, place[None, :], 0), 1)
     matrix, token = pl.pallas_call(
         matrix_kernel,
         grid=(TARGETS // 8,),
@@ -431,10 +441,9 @@
         scratch_shapes=[
             pltpu.VMEM((64, 8, 512), f32),
             pltpu.VMEM((8, 8, 512), f32),
-            pltpu.SMEM((64,), jnp.int32),
         ],
         compiler_params=grant(16),
-    )(fine_slot, hold(spread), hold(phi_up), hold(cos_table), hold(sin_table), hold(token))
+    )(inverse, hold(spread), hold(phi_up), hold(cos_table), hold(sin_table), hold(token))
     everyone = lax.all_to_all(packed, "box", split_axis=0, concat_axis=0, tiled=True)
     incoming = pl.pallas_call(
         translate_kernel,
@@ -460,11 +469,10 @@
         out_specs=vmem,
         scratch_shapes=[
             pltpu.VMEM((8, 8, 512), f32),
-            pltpu.VMEM((8, 8, 512), f32),
             pltpu.VMEM((64, 8, 512), f32),
         ],
         compiler_params=grant(16),
-    )(fine_slot, hold(fields), hold(phi_down), hold(cos_table), hold(sin_table))
+    )(inverse, hold(fields), hold(phi_down), hold(cos_table), hold(sin_table))
     back = lax.all_to_all(lowered, "dir", split_axis=0, concat_axis=0, tiled=True)
     return pl.pallas_call(
         theta_down_kernel,

time: 121 us -> 121 us (level)
  transfers between devices with their start and end apart: 1 -> 1, of which waited for: 1 -> 1; matrix products, arithmetic and copies ran while one was open for 1% -> 2% of each run, Pallas kernels for 10% -> 10%
where the time goes in v6:
time: 121 us; the launch traced here: 120 us
  blocking collectives  61.6 us (51%)
  Pallas kernels  26.2 us (22%)
  starting transfers between devices  15.2 us (13%)
  waiting for transfers between devices  15.2 us (13%)
  local copies, waits for them, and re-layouts  1.36 us (1%)
    all_to_all x1, blocking collectives, body(): lax.all_to_all(lowered, 'dir', split_axis=0, concat_axis=0, tiled=True)  35 us
    all_to_all x1, blocking collectives, body(): lax.all_to_all(packed, 'box', split_axis=0, concat_axis=0, tiled=True)  17.2 us
    all_to_all x1, starting transfers between devices, body(): lax.all_to_all(sent, 'dir', split_axis=0, concat_axis=0, tiled=True)  15.2 us
    all_to_all x1, waiting for transfers between devices, body(): lax.all_to_all(sent, 'dir', split_axis=0, concat_axis=0, tiled=True)  15.2 us
    pallas_call x1, Pallas kernels, body(): pl.pallas_call(matrix_kernel, grid=(TARGETS // 8,), in_specs=[pl.BlockSpe...  11.7 us
    all_to_all x1, blocking collectives, body(): lax.all_to_all(incoming, 'box', split_axis=0, concat_axis=0, axis_index_g...  9.3 us
    pallas_call x1, Pallas kernels, body(): pl.pallas_call(translate_kernel, in_specs=[vmem, hbm], out_specs=vmem, ou...  7.08 us
    pallas_call x1, Pallas kernels, body(): pl.pallas_call(theta_up_kernel, out_shape=pltpu.HBM((16, 4, 8, 256), f32)...  3.39 us
  transfers between devices with their start and end apart: 1, of which 1 were waited for; matrix products, arithmetic and copies ran while one was open for 2% of the time, Pallas kernels for 10%

profile of v6, /device:TPU:2, one launch (start us, length us, event | category | flops | bytes accessed | tf_op | source)
XLA Modules:
  0.0 120.4 jit_solution(5757516166828962354)
XLA Ops:
  0.0 3.4 %shard_map.100 = f32[16,4,8,256]{3,2,1,0:T(8,128)} custom-call(f32[4,8,2048]{2,1,0:T(8,128)} %x_far.1, f32[16,32,128]{2,1,0:T(8,128)} %constant.122.clone.c_far), custom_call_target="tpu_custom_call" | custom-call | tf_op jit(solution)/shard_map/pallas_call | solution.py:386
  3.4 15.2 %all-to-all-start = ((f32[16,4,8,256]{3,2,1,0:T(8,128)}), f32[16,4,8,256]{3,2,1,0:T(8,128)S(1)}, u32[]{:S(2)}, u32[]{:S(2)}) async-start(f32[16,4,8,256]{3,2,1,0:T(8,128)} %shard_map.100), calls=%async_computation | async-start | bytes 1048576 | tf_op jit(solution)/shard_map/all_to_all | solution.py:402
  18.7 0.1 constant_dynamic-slice_fusion
  18.8 0.1 copy.23
  18.9 0.3 copy.19
  19.2 0.4 constant_dynamic-slice_fusion.2
  19.6 0.2 copy.20
  19.8 0.1 copy.21
  19.9 0.1 copy.22
  20.0 0.1 dynamic_slice.12
  20.1 0.1 fusion
  20.3 0.1 add_bitcast_fusion
  20.4 0.1 multiply_bitcast_fusion.1
  20.5 0.1 fusion.1
  20.6 11.7 %shard_map.101 = (f32[64,256,128]{2,1,0:T(8,128)}, f32[8,128]{1,0:T(8,128)S(1)}) custom-call(s32[64,192]{1,0:T(8,128)S(1)} %pad.11.partner_ref, s32[8,192,8]{2,1,0:T(8,128)S(1)} %bitcast.10, f32[384,128]{1,0:T(8,128)S(1)} %pad.13.table_ref, f32[8,512]{1,0:T(8,128)S(1)} %get-tuple-element.10.cos_ref, f32[8,512]{1,0:T(8,128)S(1)} %get-tuple-element.9.sin_ref), custom_call_target="tpu_custom_call" | custom-call | tf_op jit(solution)/shard_map/pallas_call | solution.py:420
  32.4 0.1 select_reduce_fusion.inv_ref
  32.5 15.2 %all-to-all-done.x_ref = f32[16,4,8,256]{3,2,1,0:T(8,128)S(1)} async-done(((f32[16,4,8,256]{3,2,1,0:T(8,128)}), f32[16,4,8,256]{3,2,1,0:T(8,128)S(1)}, u32[]{:S(2)}, u32[]{:S(2)}) %all-to-all-start) | async-done | bytes 524320 | tf_op jit(solution)/shard_map/all_to_all | solution.py:402
  47.7 1.2 %shard_map.102 = f32[32,4,8,128]{3,2,1,0:T(8,128)S(1)} custom-call(s32[64]{0:T(128)S(1)} %select_reduce_fusion.inv_ref, f32[16,4,8,256]{3,2,1,0:T(8,128)S(1)} %all-to-all-done.x_ref, bf16[384,256]{1,0:T(8,128)(2,1)S(1)} %copy-done.2, f32[8,512]{1,0:T(8,128)S(1)} %get-tuple-element.10.cos_ref, f32[8,512]{1,0:T(8,128)S(1)} %get-tuple-element.9.sin_ref, ...), custom_call_target="tpu_custom_call" | custom-call | tf_op jit(solution)/shard_map/pallas_call | solution.py:436
  48.9 17.2 %all_to_all.20.s_ref = f32[32,4,8,128]{3,2,1,0:T(8,128)S(1)} all-to-all(f32[32,4,8,128]{3,2,1,0:T(8,128)S(1)} %shard_map.102), channel_id=1, replica_groups=mesh['box'=32,'dir'=16] {'box'}, dimensions={0} | all-to-all | bytes 1048576 | tf_op jit(solution)/shard_map/all_to_all | solution.py:447
  66.2 7.1 %shard_map.103 = f32[8,4,8,128]{3,2,1,0:T(8,128)S(1)} custom-call(f32[32,4,8,128]{3,2,1,0:T(8,128)S(1)} %all_to_all.20.s_ref, f32[64,256,128]{2,1,0:T(8,128)} %get-tuple-element.8.m_far), custom_call_target="tpu_custom_call" | custom-call | tf_op jit(solution)/shard_map/pallas_call | solution.py:448
  73.3 9.3 %all_to_all.21.x_ref = f32[8,4,8,128]{3,2,1,0:T(8,128)S(1)} all-to-all(f32[8,4,8,128]{3,2,1,0:T(8,128)S(1)} %shard_map.103), channel_id=1, replica_groups={{0,16,32,48,64,80,96,112},{128,144,160,176,192,208,224,240},{256,272,28..., dimensions={0} | all-to-all | bytes 262144 | tf_op jit(solution)/shard_map/all_to_all | solution.py:462
  82.6 1.3 %shard_map.104 = f32[16,4,8,256]{3,2,1,0:T(8,128)S(1)} custom-call(s32[64]{0:T(128)S(1)} %select_reduce_fusion.inv_ref, f32[8,4,8,128]{3,2,1,0:T(8,128)S(1)} %all_to_all.21.x_ref, bf16[256,256]{1,0:T(8,128)(2,1)S(1)} %copy-done.3, f32[8,512]{1,0:T(8,128)S(1)} %get-tuple-element.10.cos_ref, f32[8,512]{1,0:T(8,128)S(1)} %get-tuple-element.9.sin_ref), custom_call_target="tpu_custom_call" | custom-call | tf_op jit(solution)/shard_map/pallas_call | solution.py:465
  83.8 35.0 %all_to_all.22.y_ref = f32[16,4,8,256]{3,2,1,0:T(8,128)S(1)} all-to-all(f32[16,4,8,256]{3,2,1,0:T(8,128)S(1)} %shard_map.104), channel_id=1, replica_groups=mesh['box'=32,'dir'=16] {'dir'}, dimensions={0} | all-to-all | bytes 1048576 | tf_op jit(solution)/shard_map/all_to_all | solution.py:476
  118.9 1.5 %shard_map.105 = f32[4,8,2048]{2,1,0:T(8,128)} custom-call(f32[16,4,8,256]{3,2,1,0:T(8,128)S(1)} %all_to_all.22.y_ref, f32[8,64,128]{2,1,0:T(8,128)S(1)} %copy-done.1), custom_call_target="tpu_custom_call" | custom-call | tf_op jit(solution)/shard_map/pallas_call | solution.py:477
  (25 shorter events, 0.2 us)
Async XLA Ops:
  0.0 19.2 %copy-start = (f32[316,2,512]{2,1,0:T(2,128)S(1)}, f32[316,2,512]{2,1,0:T(2,128)}, u32[]{:S(2)}) copy-start(f32[316,2,512]{2,1,0:T(2,128)} %param.12) | copy-start | bytes 3883012
  0.0 18.6 %copy-start.5 = (s32[256,189]{0,1:T(8,128)S(1)}, s32[256,189]{0,1:T(8,128)}, u32[]{:S(2)}) copy-start(s32[256,189]{0,1:T(8,128)} %param.13) | copy-start | bytes 580612
  0.0 18.6 %copy-start.4 = (s32[256,189]{0,1:T(8,128)S(1)}, s32[256,189]{0,1:T(8,128)}, u32[]{:S(2)}) copy-start(s32[256,189]{0,1:T(8,128)} %param.14) | copy-start | bytes 580612
  3.4 44.3 %all-to-all-start = ((f32[16,4,8,256]{3,2,1,0:T(8,128)}), f32[16,4,8,256]{3,2,1,0:T(8,128)S(1)}, u32[]{:S(2)}, u32[]{:S(2)}) async-start(f32[16,4,8,256]{3,2,1,0:T(8,128)} %shard_map.100), calls=%async_computation | async-start | bytes 1048576 | tf_op jit(solution)/shard_map/all_to_all | solution.py:402
  18.9 1.1 copy-start.6
  19.6 12.8 %copy-start.7 = (s32[64]{0:T(128)S(1)}, s32[64]{0:T(128)}, u32[]{:S(2)}) copy-start(s32[64]{0:T(128)} %param.11) | copy-start | bytes 772
  19.6 28.1 %copy-start.2 = (bf16[384,256]{1,0:T(8,128)(2,1)S(1)}, bf16[384,256]{1,0:T(8,128)(2,1)}, u32[]{:S(2)}) copy-start(bf16[384,256]{1,0:T(8,128)(2,1)} %constant.124.clone.w_ref) | copy-start | bytes 589828
  66.2 16.4 %copy-start.3 = (bf16[256,256]{1,0:T(8,128)(2,1)S(1)}, bf16[256,256]{1,0:T(8,128)(2,1)}, u32[]{:S(2)}) copy-start(bf16[256,256]{1,0:T(8,128)(2,1)} %constant.125.clone.w_ref) | copy-start | bytes 393220
  73.2 45.6 %copy-start.1 = (f32[8,64,128]{2,1,0:T(8,128)S(1)}, f32[8,64,128]{2,1,0:T(8,128)}, u32[]{:S(2)}) copy-start(f32[8,64,128]{2,1,0:T(8,128)} %constant.123.clone.c_ref) | copy-start | bytes 786436

commit v7 on v6

--- a/solution.py
+++ b/solution.py
@@ -186,15 +186,19 @@
 
     lax.fori_loop(0, 8, step, 0, unroll=4)
     low_half = lax.broadcasted_iota(jnp.int32, (8, LANES), 1) < PF
+    top = lax.broadcasted_iota(jnp.int32, (8, LANES), 0) < 4
     for j in range(4):
         for block in range(4):
             a = parent_ref[2 * j, :, pl.ds(block * LANES, LANES)]
             b = parent_ref[2 * j + 1, :, pl.ds(block * LANES, LANES)]
-            even = jnp.where(low_half, a, swap_halves(b))
-            odd = jnp.where(low_half, swap_halves(a), b)
+            real = jnp.where(top, a, pltpu.roll(b, 4, 0))
+            imag = jnp.where(top, pltpu.roll(a, 4, 0), b)
+            even = jnp.where(low_half, real, swap_halves(imag))
+            odd = jnp.where(low_half, swap_halves(real), imag)
             for group in range(4):
-                o_ref[group * 8 + 2 * block, j] = even
-                o_ref[group * 8 + 2 * block + 1, j] = odd
+                dest = group * 8 + 2 * block
+                o_ref[pl.ds(dest * 32 + j * 8, 8), :] = even
+                o_ref[pl.ds(dest * 32 + 32 + j * 8, 8), :] = odd
 
 
 def matrix_kernel(partner_ref, kind_ref, table_ref, cos_ref, sin_ref, o_ref, token_ref, both_ref, picked_ref):
@@ -235,9 +239,8 @@
     return parts[0]
 
 
-def translate_kernel(s_ref, m_far, o_ref, rows_ref, wide_ref, m_ref, arrived):
+def translate_kernel(s_ref, m_far, o_ref, wide_ref, m_ref, arrived):
     low_half = lax.broadcasted_iota(jnp.int32, (8, LANES), 1) < PF
-    top = lax.broadcasted_iota(jnp.int32, (8, LANES), 0) < 4
 
     def fetch(g):
         four = pl.ds(g * 4, 4)
@@ -246,17 +249,8 @@
     for g in range(TARGETS // 4):
         fetch(g).start()
 
-    def pair(b, carry):
-        for j in range(4):
-            v = s_ref[b, j]
-            w = swap_halves(pltpu.roll(v, 4, 0))
-            rows_ref[pl.ds(b * 32 + j * 8, 8), :] = jnp.where(low_half == top, v, w)
-        return carry
-
-    lax.fori_loop(0, 32, pair, 0, unroll=4)
-
     def spread(b, carry):
-        plain = [rows_ref[pl.ds(b * 32 + e, 8, stride=4), :] for e in range(4)]
+        plain = [s_ref[pl.ds(b * 32 + e, 8, stride=4), :] for e in range(4)]
         both = [v + swap_halves(v) for v in plain]
         for e in range(4):
             wide_ref[b, e] = plain[e]
@@ -266,8 +260,7 @@
 
     lax.fori_loop(0, 32, spread, 0, unroll=4)
 
-    def four_targets(g, carry):
-        fetch(g).wait()
+    def four_targets(g):
         sums = [[jnp.zeros((8, LANES), f32) for _ in range(6)] for _ in range(4)]
         for b in range(SOURCES // 8):
             source = [wide_ref[b, k] for k in range(6)]
@@ -292,9 +285,15 @@
                 parts.append(jnp.where(low_half, x, swap_halves(y)))
                 parts.append(jnp.where(low_half, swap_halves(x), y))
             o_ref[g // 2, (g % 2) * 2 + j] = fold_rows(parts)
-        return carry
-
-    lax.fori_loop(0, TARGETS // 4, four_targets, 0)
+
+    def step(q, carry):
+        fetch(2 * q).wait()
+        fetch(2 * q + 1).wait()
+        four_targets(2 * q)
+        four_targets(2 * q + 1)
+        return carry
+
+    lax.fori_loop(0, TARGETS // 8, step, 0)
 
 
 def scatter_kernel(inv_ref, x_ref, w_ref, cos_ref, sin_ref, o_ref, plain_ref, child_ref):
@@ -435,7 +434,7 @@
 
     packed = pl.pallas_call(
         gather_kernel,
-        out_shape=near(32, 4, 8, LANES),
+        out_shape=near(32 * 32, LANES),
         in_specs=[smem, vmem, vmem, vmem, vmem, vmem],
         out_specs=vmem,
         scratch_shapes=[
@@ -451,7 +450,6 @@
         out_specs=vmem,
         out_shape=near(8, 4, 8, LANES),
         scratch_shapes=[
-            pltpu.VMEM((SOURCES * 4, LANES), f32),
             pltpu.VMEM((SOURCES // 8, 6, 8, LANES), f32),
             pltpu.VMEM((TARGETS, SOURCES, LANES), f32),
             pltpu.SemaphoreType.DMA((TARGETS // 4,)),

time: 121 us -> 120 us (level)
  no operation moved by 1% of the time
where the time goes in v7:
time: 120 us; the launch traced here: 119 us
  blocking collectives  61.6 us (51%)
  Pallas kernels  25.2 us (21%)
  starting transfers between devices  15.2 us (13%)
  waiting for transfers between devices  15.2 us (13%)
  local copies, waits for them, and re-layouts  1.36 us (1%)
    all_to_all x1, blocking collectives, body(): lax.all_to_all(lowered, 'dir', split_axis=0, concat_axis=0, tiled=True)  35 us
    all_to_all x1, blocking collectives, body(): lax.all_to_all(packed, 'box', split_axis=0, concat_axis=0, tiled=True)  17.2 us
    all_to_all x1, starting transfers between devices, body(): lax.all_to_all(sent, 'dir', split_axis=0, concat_axis=0, tiled=True)  15.2 us
    all_to_all x1, waiting for transfers between devices, body(): lax.all_to_all(sent, 'dir', split_axis=0, concat_axis=0, tiled=True)  15.2 us
    pallas_call x1, Pallas kernels, body(): pl.pallas_call(matrix_kernel, grid=(TARGETS // 8,), in_specs=[pl.BlockSpe...  11.7 us
    all_to_all x1, blocking collectives, body(): lax.all_to_all(incoming, 'box', split_axis=0, concat_axis=0, axis_index_g...  9.3 us
    pallas_call x1, Pallas kernels, body(): pl.pallas_call(translate_kernel, in_specs=[vmem, hbm], out_specs=vmem, ou...  6.07 us
    pallas_call x1, Pallas kernels, body(): pl.pallas_call(theta_up_kernel, out_shape=pltpu.HBM((16, 4, 8, 256), f32)...  3.39 us
  transfers between devices with their start and end apart: 1, of which 1 were waited for; matrix products, arithmetic and copies ran while one was open for 2% of the time, Pallas kernels for 10%

profile of v7, /device:TPU:2, one launch (start us, length us, event | category | flops | bytes accessed | tf_op | source)
XLA Modules:
  0.0 119.4 jit_solution(9452293616039439314)
XLA Ops:
  0.0 3.4 %shard_map.100 = f32[16,4,8,256]{3,2,1,0:T(8,128)} custom-call(f32[4,8,2048]{2,1,0:T(8,128)} %x_far.1, f32[16,32,128]{2,1,0:T(8,128)} %constant.122.clone.c_far), custom_call_target="tpu_custom_call" | custom-call | tf_op jit(solution)/shard_map/pallas_call | solution.py:385
  3.4 15.2 %all-to-all-start = ((f32[16,4,8,256]{3,2,1,0:T(8,128)}), f32[16,4,8,256]{3,2,1,0:T(8,128)S(1)}, u32[]{:S(2)}, u32[]{:S(2)}) async-start(f32[16,4,8,256]{3,2,1,0:T(8,128)} %shard_map.100), calls=%async_computation | async-start | bytes 1048576 | tf_op jit(solution)/shard_map/all_to_all | solution.py:401
  18.7 0.1 constant_dynamic-slice_fusion
  18.8 0.1 copy.23
  18.9 0.3 copy.19
  19.2 0.4 constant_dynamic-slice_fusion.2
  19.6 0.2 copy.20
  19.8 0.1 copy.21
  19.9 0.1 copy.22
  20.0 0.1 dynamic_slice.12
  20.1 0.1 fusion
  20.3 0.1 add_bitcast_fusion
  20.4 0.1 multiply_bitcast_fusion.1
  20.5 0.1 fusion.1
  20.6 11.7 %shard_map.101 = (f32[64,256,128]{2,1,0:T(8,128)}, f32[8,128]{1,0:T(8,128)S(1)}) custom-call(s32[64,192]{1,0:T(8,128)S(1)} %pad.11.partner_ref, s32[8,192,8]{2,1,0:T(8,128)S(1)} %bitcast.12, f32[384,128]{1,0:T(8,128)S(1)} %pad.13.table_ref, f32[8,512]{1,0:T(8,128)S(1)} %get-tuple-element.10.cos_ref, f32[8,512]{1,0:T(8,128)S(1)} %get-tuple-element.9.sin_ref), custom_call_target="tpu_custom_call" | custom-call | tf_op jit(solution)/shard_map/pallas_call | solution.py:419
  32.4 0.1 select_reduce_fusion.inv_ref
  32.5 15.2 %all-to-all-done.x_ref = f32[16,4,8,256]{3,2,1,0:T(8,128)S(1)} async-done(((f32[16,4,8,256]{3,2,1,0:T(8,128)}), f32[16,4,8,256]{3,2,1,0:T(8,128)S(1)}, u32[]{:S(2)}, u32[]{:S(2)}) %all-to-all-start) | async-done | bytes 524320 | tf_op jit(solution)/shard_map/all_to_all | solution.py:401
  47.7 1.2 %shard_map.102 = f32[1024,128]{1,0:T(8,128)S(1)} custom-call(s32[64]{0:T(128)S(1)} %select_reduce_fusion.inv_ref, f32[16,4,8,256]{3,2,1,0:T(8,128)S(1)} %all-to-all-done.x_ref, bf16[384,256]{1,0:T(8,128)(2,1)S(1)} %copy-done.2, f32[8,512]{1,0:T(8,128)S(1)} %get-tuple-element.10.cos_ref, f32[8,512]{1,0:T(8,128)S(1)} %get-tuple-element.9.sin_ref, ...), custom_call_target="tpu_custom_call" | custom-call | tf_op jit(solution)/shard_map/pallas_call | solution.py:435
  48.9 17.2 %all_to_all.26 = f32[32,32,128]{2,1,0:T(8,128)S(1)} all-to-all(f32[32,32,128]{2,1,0:T(8,128)S(1)} %bitcast.13), channel_id=1, replica_groups=mesh['box'=32,'dir'=16] {'box'}, dimensions={0} | all-to-all | bytes 1048576 | tf_op jit(solution)/shard_map/all_to_all | solution.py:446
  66.2 6.1 %shard_map.103 = f32[8,4,8,128]{3,2,1,0:T(8,128)S(1)} custom-call(f32[1024,128]{1,0:T(8,128)S(1)} %bitcast.14, f32[64,256,128]{2,1,0:T(8,128)} %get-tuple-element.8.m_far), custom_call_target="tpu_custom_call" | custom-call | tf_op jit(solution)/shard_map/pallas_call | solution.py:447
  72.2 9.3 %all_to_all.27.x_ref = f32[8,4,8,128]{3,2,1,0:T(8,128)S(1)} all-to-all(f32[8,4,8,128]{3,2,1,0:T(8,128)S(1)} %shard_map.103), channel_id=1, replica_groups={{0,16,32,48,64,80,96,112},{128,144,160,176,192,208,224,240},{256,272,28..., dimensions={0} | all-to-all | bytes 262144 | tf_op jit(solution)/shard_map/all_to_all | solution.py:460
  81.6 1.3 %shard_map.104 = f32[16,4,8,256]{3,2,1,0:T(8,128)S(1)} custom-call(s32[64]{0:T(128)S(1)} %select_reduce_fusion.inv_ref, f32[8,4,8,128]{3,2,1,0:T(8,128)S(1)} %all_to_all.27.x_ref, bf16[256,256]{1,0:T(8,128)(2,1)S(1)} %copy-done.3, f32[8,512]{1,0:T(8,128)S(1)} %get-tuple-element.10.cos_ref, f32[8,512]{1,0:T(8,128)S(1)} %get-tuple-element.9.sin_ref), custom_call_target="tpu_custom_call" | custom-call | tf_op jit(solution)/shard_map/pallas_call | solution.py:463
  82.8 35.0 %all_to_all.28.y_ref = f32[16,4,8,256]{3,2,1,0:T(8,128)S(1)} all-to-all(f32[16,4,8,256]{3,2,1,0:T(8,128)S(1)} %shard_map.104), channel_id=1, replica_groups=mesh['box'=32,'dir'=16] {'dir'}, dimensions={0} | all-to-all | bytes 1048576 | tf_op jit(solution)/shard_map/all_to_all | solution.py:474
  117.9 1.5 %shard_map.105 = f32[4,8,2048]{2,1,0:T(8,128)} custom-call(f32[16,4,8,256]{3,2,1,0:T(8,128)S(1)} %all_to_all.28.y_ref, f32[8,64,128]{2,1,0:T(8,128)S(1)} %copy-done.1), custom_call_target="tpu_custom_call" | custom-call | tf_op jit(solution)/shard_map/pallas_call | solution.py:475
  (25 shorter events, 0.2 us)
Async XLA Ops:
  0.0 19.2 %copy-start = (f32[316,2,512]{2,1,0:T(2,128)S(1)}, f32[316,2,512]{2,1,0:T(2,128)}, u32[]{:S(2)}) copy-start(f32[316,2,512]{2,1,0:T(2,128)} %param.12) | copy-start | bytes 3883012
  0.0 18.6 %copy-start.5 = (s32[256,189]{0,1:T(8,128)S(1)}, s32[256,189]{0,1:T(8,128)}, u32[]{:S(2)}) copy-start(s32[256,189]{0,1:T(8,128)} %param.13) | copy-start | bytes 580612
  0.0 18.6 %copy-start.4 = (s32[256,189]{0,1:T(8,128)S(1)}, s32[256,189]{0,1:T(8,128)}, u32[]{:S(2)}) copy-start(s32[256,189]{0,1:T(8,128)} %param.14) | copy-start | bytes 580612
  3.4 44.3 %all-to-all-start = ((f32[16,4,8,256]{3,2,1,0:T(8,128)}), f32[16,4,8,256]{3,2,1,0:T(8,128)S(1)}, u32[]{:S(2)}, u32[]{:S(2)}) async-start(f32[16,4,8,256]{3,2,1,0:T(8,128)} %shard_map.100), calls=%async_computation | async-start | bytes 1048576 | tf_op jit(solution)/shard_map/all_to_all | solution.py:401
  18.9 1.1 copy-start.6
  19.6 12.8 %copy-start.7 = (s32[64]{0:T(128)S(1)}, s32[64]{0:T(128)}, u32[]{:S(2)}) copy-start(s32[64]{0:T(128)} %param.11) | copy-start | bytes 772
  19.6 28.1 %copy-start.2 = (bf16[384,256]{1,0:T(8,128)(2,1)S(1)}, bf16[384,256]{1,0:T(8,128)(2,1)}, u32[]{:S(2)}) copy-start(bf16[384,256]{1,0:T(8,128)(2,1)} %constant.124.clone.w_ref) | copy-start | bytes 589828
  66.2 15.4 %copy-start.3 = (bf16[256,256]{1,0:T(8,128)(2,1)S(1)}, bf16[256,256]{1,0:T(8,128)(2,1)}, u32[]{:S(2)}) copy-start(bf16[256,256]{1,0:T(8,128)(2,1)} %constant.125.clone.w_ref) | copy-start | bytes 393220
  72.2 45.6 %copy-start.1 = (f32[8,64,128]{2,1,0:T(8,128)S(1)}, f32[8,64,128]{2,1,0:T(8,128)}, u32[]{:S(2)}) copy-start(f32[8,64,128]{2,1,0:T(8,128)} %constant.123.clone.c_ref) | copy-start | bytes 786436

commit v8 on v7

--- a/solution.py
+++ b/solution.py
@@ -13,10 +13,10 @@
 PP = 128
 LANES = 128
 SLOTS = 192
-KINDS = 384
-TARGETS = 64
+KINDS = 256
+TARGETS = 128
 SOURCES = 256
-CHUNK = 64
+CHUNK = 32
 
 wave_shift = 5.0
 f32 = jnp.float32
@@ -67,6 +67,25 @@
     top = matrix[: n_out // 2]
     near, far = top[:, : n_in // 2], top[:, ::-1][:, : n_in // 2]
     return np.concatenate([pair_table((near + far) / 2), pair_table((near - far) / 2)], 1)
+
+
+def lane_quarter():
+    return lax.broadcasted_iota(jnp.int32, (8, LANES), 1) // 32
+
+
+def transpose_quarters(x):
+    low_half = lane_quarter() < 2
+    even = lane_quarter() % 2 == 0
+    half = [
+        (jnp.where(low_half, a, swap_halves(b)), jnp.where(low_half, swap_halves(a), b))
+        for a, b in ((x[0], x[2]), (x[1], x[3]))
+    ]
+    out = []
+    for k in range(2):
+        a, b = half[0][k], half[1][k]
+        out.append(jnp.where(even, a, pltpu.roll(b, 32, 1)))
+        out.append(jnp.where(even, pltpu.roll(a, 96, 1), b))
+    return out
 
 
 def theta_step(parity_ref, c_ref, j, count):
@@ -185,45 +204,61 @@
         return carry
 
     lax.fori_loop(0, 8, step, 0, unroll=4)
-    low_half = lax.broadcasted_iota(jnp.int32, (8, LANES), 1) < PF
     top = lax.broadcasted_iota(jnp.int32, (8, LANES), 0) < 4
-    for j in range(4):
+    for k in range(2):
         for block in range(4):
-            a = parent_ref[2 * j, :, pl.ds(block * LANES, LANES)]
-            b = parent_ref[2 * j + 1, :, pl.ds(block * LANES, LANES)]
-            real = jnp.where(top, a, pltpu.roll(b, 4, 0))
-            imag = jnp.where(top, pltpu.roll(a, 4, 0), b)
-            even = jnp.where(low_half, real, swap_halves(imag))
-            odd = jnp.where(low_half, swap_halves(real), imag)
-            for group in range(4):
-                dest = group * 8 + 2 * block
-                o_ref[pl.ds(dest * 32 + j * 8, 8), :] = even
-                o_ref[pl.ds(dest * 32 + 32 + j * 8, 8), :] = odd
-
-
-def matrix_kernel(partner_ref, kind_ref, table_ref, cos_ref, sin_ref, o_ref, token_ref, both_ref, picked_ref):
+            lanes = pl.ds(block * LANES, LANES)
+            a, b, c, d = (parent_ref[4 * k + i, :, lanes] for i in range(4))
+            quarters = transpose_quarters(
+                [
+                    jnp.where(top, a, pltpu.roll(c, 4, 0)),
+                    jnp.where(top, b, pltpu.roll(d, 4, 0)),
+                    jnp.where(top, pltpu.roll(a, 4, 0), c),
+                    jnp.where(top, pltpu.roll(b, 4, 0), d),
+                ]
+            )
+            for q in range(4):
+                for group in range(2):
+                    dest = group * 16 + 4 * block + q
+                    o_ref[pl.ds(dest * 16 + k * 8, 8), :] = quarters[q]
+
+
+def matrix_kernel(
+    partner_ref, kind_ref, table_ref, cos_ref, sin_ref, o_ref, token_ref, both_ref, picked_ref
+):
     @pl.when(pl.program_id(0) == 0)
     def _():
-        high, low = split(table_ref[...])
-        both_ref[:, :LANES] = high
-        both_ref[:, LANES:] = low
+        low_half = lax.broadcasted_iota(jnp.int32, (KINDS, LANES), 1) < PF
+        high, low = (v.astype(f32) for v in split(table_ref[...]))
+        both_ref[:, :LANES] = jnp.where(low_half, high, swap_halves(low)).astype(bf16)
+        both_ref[:, LANES:] = jnp.where(low_half, swap_halves(high), low).astype(bf16)
         token_ref[...] = jnp.zeros((8, LANES), f32)
 
     lane_kind = lax.broadcasted_iota(jnp.int32, (SLOTS, KINDS), 1)
-    row_source = lax.broadcasted_iota(jnp.int32, (SOURCES, SLOTS), 0)
-    pick_kind = jnp.concatenate(
-        [
-            jnp.where(lane_kind == kind_ref[0, :, p : p + 1], 1.0, 0.0).astype(bf16)
-            for p in range(8)
-        ],
-        0,
+    row = lax.broadcasted_iota(jnp.int32, (SOURCES, SLOTS), 0)
+    row_source = jnp.where(row < LANES, 2 * row, 2 * row - SOURCES + 1)
+    pick_kind = []
+    for p in range(8):
+        kind = kind_ref[0, :, p : p + 1] % KINDS
+        pick_kind.append(jnp.where(lane_kind == kind, 1.0, 0.0).astype(bf16))
+    picked = jnp.dot(
+        jnp.concatenate(pick_kind, 0), both_ref[...], preferred_element_type=f32
     )
-    picked_ref[...] = jnp.dot(pick_kind, both_ref[...], preferred_element_type=f32).astype(bf16)
+    for p in range(8):
+        mine = picked[p * SLOTS : (p + 1) * SLOTS]
+        upper = kind_ref[0, :, p : p + 1] >= KINDS
+        chosen = jnp.where(upper, mine[:, LANES:], mine[:, :LANES])
+        picked_ref[pl.ds(p * SLOTS, SLOTS), :] = chosen.astype(bf16)
+    quarter = lax.broadcasted_iota(jnp.int32, (LANES, LANES), 1) // 32
     for p in range(8):
         pick_source = jnp.where(row_source == partner_ref[pl.ds(p, 1), :], 1.0, 0.0).astype(bf16)
         rows = picked_ref[pl.ds(p * SLOTS, SLOTS), :]
-        both = jnp.dot(pick_source, rows, preferred_element_type=f32)
-        o_ref[p] = both[:, :LANES] + both[:, LANES:]
+        sums = jnp.dot(pick_source, rows, preferred_element_type=f32)
+        sums = sums + swap_halves(sums)
+        a, b = sums[:LANES], sums[LANES:]
+        outer = jnp.where(quarter == 0, a, b)
+        inner = jnp.where(quarter == 0, b, a)
+        o_ref[p] = jnp.where((quarter == 0) | (quarter == 3), outer, pltpu.roll(inner, 32, 1))
 
 
 def fold_rows(parts):
@@ -240,13 +275,15 @@
 
 
 def translate_kernel(s_ref, m_far, o_ref, wide_ref, m_ref, arrived):
-    low_half = lax.broadcasted_iota(jnp.int32, (8, LANES), 1) < PF
+    low_half = lane_quarter() < 2
+    row = lax.broadcasted_iota(jnp.int32, (8, LANES), 0)
+    top = row < 4
 
     def fetch(g):
-        four = pl.ds(g * 4, 4)
-        return pltpu.make_async_copy(m_far.at[four], m_ref.at[four], arrived.at[g])
-
-    for g in range(TARGETS // 4):
+        eight = pl.ds(g * 8, 8)
+        return pltpu.make_async_copy(m_far.at[eight], m_ref.at[eight], arrived.at[g])
+
+    for g in range(TARGETS // 8):
         fetch(g).start()
 
     def spread(b, carry):
@@ -255,57 +292,59 @@
         for e in range(4):
             wide_ref[b, e] = plain[e]
         for h in range(2):
-            wide_ref[b, 4 + h] = jnp.where(low_half, both[2 * h], both[2 * h + 1])
+            wide_ref[b, 4 + h] = jnp.where(low_half, both[h], both[h + 2])
         return carry
 
-    lax.fori_loop(0, 32, spread, 0, unroll=4)
+    lax.fori_loop(0, 16, spread, 0, unroll=4)
+
+    def add_pair(v):
+        return v + pltpu.roll(v, 96, 1)
 
     def four_targets(g):
         sums = [[jnp.zeros((8, LANES), f32) for _ in range(6)] for _ in range(4)]
-        for b in range(SOURCES // 8):
+        for b in range(16):
             source = [wide_ref[b, k] for k in range(6)]
             for p in range(4):
                 m = m_ref[g * 4 + p, pl.ds(b * 8, 8), :]
                 t = m + swap_halves(m)
                 for k in range(6):
                     sums[p][k] = sums[p][k] + source[k] * (m if k < 4 else t)
-        real, imag = [], []
-        for p in range(4):
-            turned = [swap_halves(v) for v in sums[p][:4]]
-            real.append([x - y for x, y in zip(sums[p], turned)])
-            total = [x + y for x, y in zip(sums[p], turned)]
-            imag.append(
-                [sums[p][4 + h] - jnp.where(low_half, total[2 * h], total[2 * h + 1]) for h in range(2)]
-            )
-        for j in range(2):
-            a, b = 2 * j, 2 * j + 1
-            parts = [jnp.where(low_half, x, -y) for x, y in zip(real[a], real[b])]
-            for h in range(2):
-                x, y = imag[a][h], imag[b][h]
-                parts.append(jnp.where(low_half, x, swap_halves(y)))
-                parts.append(jnp.where(low_half, swap_halves(x), y))
-            o_ref[g // 2, (g % 2) * 2 + j] = fold_rows(parts)
+        plain = [fold_rows(sums[0][:4] + sums[1][:4]), fold_rows(sums[2][:4] + sums[3][:4])]
+        mixed = fold_rows(sums[0][4:] + sums[2][4:] + sums[1][4:] + sums[3][4:])
+        turned = swap_halves(mixed)
+        first = (row & 2) == 0
+        third = [
+            jnp.where(first, mixed, pltpu.roll(turned, 2, 0)),
+            jnp.where(first, pltpu.roll(mixed, 6, 0), turned),
+        ]
+        whole = []
+        for k in range(2):
+            other = swap_halves(plain[k])
+            real = add_pair(plain[k] - other)
+            imag = add_pair(third[k] - (plain[k] + other))
+            whole.append(jnp.where(top, real, pltpu.roll(imag, 4, 0)))
+            whole.append(jnp.where(top, pltpu.roll(real, 4, 0), imag))
+        out = whole[0]
+        for k in range(1, 4):
+            out = jnp.where(lane_quarter() == k, pltpu.roll(whole[k], 32 * k, 1), out)
+        o_ref[g // 2, g % 2] = out
 
     def step(q, carry):
         fetch(2 * q).wait()
         fetch(2 * q + 1).wait()
-        four_targets(2 * q)
-        four_targets(2 * q + 1)
+        for k in range(4):
+            four_targets(4 * q + k)
         return carry
 
-    lax.fori_loop(0, TARGETS // 8, step, 0)
+    lax.fori_loop(0, TARGETS // 16, step, 0)
 
 
 def scatter_kernel(inv_ref, x_ref, w_ref, cos_ref, sin_ref, o_ref, plain_ref, child_ref):
-    low_half = lax.broadcasted_iota(jnp.int32, (8, LANES), 1) < PF
     for block in range(4):
-        for j in range(4):
-            a = x_ref[2 * block, j]
-            b = x_ref[2 * block + 1, j]
-            first = jnp.where(low_half, a, swap_halves(b))
-            second = jnp.where(low_half, swap_halves(a), b)
-            plain_ref[2 * j, :, pl.ds(block * LANES, LANES)] = first
-            plain_ref[2 * j + 1, :, pl.ds(block * LANES, LANES)] = second
+        for k in range(2):
+            quarters = transpose_quarters([x_ref[4 * block + q, k] for q in range(4)])
+            for i in range(4):
+                plain_ref[4 * k + i, :, pl.ds(block * LANES, LANES)] = quarters[i]
     sign = channel_sign()
 
     def step(p, carry):
@@ -370,8 +409,8 @@
 def body(outgoing, fine_slot, translator, list_partner, list_kind, list_count):
     box_index = lax.axis_index("box")
     dir_index = lax.axis_index("dir")
-    chunk = box_index % 8
-    group = box_index // 8
+    chunk = box_index % 16
+    group = box_index // 16
 
     theta = theta_matrix()
     up = jnp.asarray(parity_table(theta))
@@ -410,8 +449,9 @@
     kinds = jnp.pad(kinds, pad, constant_values=-1)
     kinds = kinds.reshape(TARGETS // 8, 8, SLOTS).transpose(0, 2, 1)
     table = lax.dynamic_slice_in_dim(translator, chunk * CHUNK, CHUNK, 2)
-    table = table.reshape(table.shape[0], LANES)
-    table = jnp.pad(table, ((0, KINDS - table.shape[0]), (0, 0)))
+    table = table.reshape(table.shape[0], 2 * CHUNK)
+    table = jnp.pad(table, ((0, 2 * KINDS - table.shape[0]), (0, 0)))
+    table = jnp.concatenate([table[:KINDS], table[KINDS:]], 1)
     cos_table, sin_table = phase_tables(dir_index)
     place = jnp.arange(64, dtype=jnp.int32)
     found = fine_slot[None, :] % 64 == place[:, None]
@@ -426,15 +466,15 @@
             vmem,
             vmem,
         ],
-        out_specs=[pl.BlockSpec((8, SOURCES, LANES), lambda i: (i, 0, 0)), vmem],
-        out_shape=[pltpu.HBM((TARGETS, SOURCES, LANES), f32), near(8, LANES)],
-        scratch_shapes=[pltpu.VMEM((KINDS, 256), bf16), pltpu.VMEM((8 * SLOTS, 256), bf16)],
+        out_specs=[pl.BlockSpec((8, LANES, LANES), lambda i: (i, 0, 0)), vmem],
+        out_shape=[pltpu.HBM((TARGETS, LANES, LANES), f32), near(8, LANES)],
+        scratch_shapes=[pltpu.VMEM((KINDS, 256), bf16), pltpu.VMEM((8 * SLOTS, LANES), bf16)],
         compiler_params=grant(16),
     )(rows, kinds, table, hold(cos_table), hold(sin_table))
 
     packed = pl.pallas_call(
         gather_kernel,
-        out_shape=near(32 * 32, LANES),
+        out_shape=near(32 * 16, LANES),
         in_specs=[smem, vmem, vmem, vmem, vmem, vmem],
         out_specs=vmem,
         scratch_shapes=[
@@ -448,15 +488,15 @@
         translate_kernel,
         in_specs=[vmem, hbm],
         out_specs=vmem,
-        out_shape=near(8, 4, 8, LANES),
+        out_shape=near(16, 2, 8, LANES),
         scratch_shapes=[
-            pltpu.VMEM((SOURCES // 8, 6, 8, LANES), f32),
-            pltpu.VMEM((TARGETS, SOURCES, LANES), f32),
-            pltpu.SemaphoreType.DMA((TARGETS // 4,)),
+            pltpu.VMEM((16, 6, 8, LANES), f32),
+            pltpu.VMEM((TARGETS, LANES, LANES), f32),
+            pltpu.SemaphoreType.DMA((TARGETS // 8,)),
         ],
         compiler_params=grant(16),
     )(hold(everyone), far(matrix))
-    groups = [[8 * g + k for k in range(8)] for g in range(4)]
+    groups = [[16 * g + k for k in range(16)] for g in range(2)]
     fields = lax.all_to_all(
         incoming, "box", split_axis=0, concat_axis=0, axis_index_groups=groups, tiled=True
     )

time: 120 us -> 128 us (1.067)
  the two profiles are of different devices: /device:TPU:2 before, /device:TPU:32 now
where the time goes in v8:
time: 128 us; the launch traced here: 127 us
  blocking collectives  65.8 us (51%)
  Pallas kernels  34.1 us (27%)
  starting transfers between devices  15.2 us (12%)
  local copies, waits for them, and re-layouts  9.76 us (8%)
  other arithmetic  2.27 us (2%)
    all_to_all x1, blocking collectives, body(): lax.all_to_all(lowered, 'dir', split_axis=0, concat_axis=0, tiled=True)  40.3 us
    pallas_call x1, Pallas kernels, body(): pl.pallas_call(matrix_kernel, grid=(TARGETS // 8,), in_specs=[pl.BlockSpe...  19.3 us
    all_to_all x1, blocking collectives, body(): lax.all_to_all(packed, 'box', split_axis=0, concat_axis=0, tiled=True)  16 us
    all_to_all x1, starting transfers between devices, body(): lax.all_to_all(sent, 'dir', split_axis=0, concat_axis=0, tiled=True)  15.2 us
    all_to_all x1, blocking collectives, body(): lax.all_to_all(incoming, 'box', split_axis=0, concat_axis=0, axis_index_g...  9.4 us
    pallas_call x1, Pallas kernels, body(): pl.pallas_call(translate_kernel, in_specs=[vmem, hbm], out_specs=vmem, ou...  7.26 us
    unnamed x19, local copies, waits for them, and re-layouts  4.41 us
    pallas_call x1, Pallas kernels, body(): pl.pallas_call(theta_up_kernel, out_shape=pltpu.HBM((16, 4, 8, 256), f32)...  3.39 us
  transfers between devices with their start and end apart: 1, of which 0 were waited for; matrix products, arithmetic and copies ran while one was open for 8% of the time, Pallas kernels for 15%

profile of v8, /device:TPU:32, one launch (start us, length us, event | category | flops | bytes accessed | tf_op | source)
XLA Modules:
  0.0 127.3 jit_solution(8185079004850008484)
XLA Ops:
  0.0 3.4 %shard_map.100 = f32[16,4,8,256]{3,2,1,0:T(8,128)} custom-call(f32[4,8,2048]{2,1,0:T(8,128)} %x_far.1, f32[16,32,128]{2,1,0:T(8,128)} %constant.126.clone.c_far), custom_call_target="tpu_custom_call" | custom-call | tf_op jit(solution)/shard_map/pallas_call | solution.py:424
  3.4 15.2 %all-to-all-start = ((f32[16,4,8,256]{3,2,1,0:T(8,128)}), f32[16,4,8,256]{3,2,1,0:T(8,128)S(1)}, u32[]{:S(2)}, u32[]{:S(2)}) async-start(f32[16,4,8,256]{3,2,1,0:T(8,128)} %shard_map.100), calls=%async_computation | async-start | bytes 1048576 | tf_op jit(solution)/shard_map/all_to_all | solution.py:440
  18.6 0.7 constant_dynamic-slice_fusion
  19.4 0.5 copy.20
  19.9 1.1 constant_dynamic-slice_fusion.2
  21.1 1.1 copy.26
  22.2 0.8 copy.22
  23.0 0.7 copy.23
  23.7 1.0 copy.24
  24.7 0.8 dynamic_slice.12
  25.7 0.8 pad_slice_fusion
  26.5 1.0 pad_maximum_fusion.table_ref
  27.8 19.3 %shard_map.101 = (f32[128,128,128]{2,1,0:T(8,128)}, f32[8,128]{1,0:T(8,128)S(1)}) custom-call(s32[128,192]{1,0:T(8,128)S(1)} %pad.11.partner_ref, s32[16,192,8]{2,1,0:T(8,128)S(1)} %bitcast.13, f32[256,128]{1,0:T(8,128)S(1)} %pad_maximum_fusion.table_ref, f32[8,512]{1,0:T(8,128)S(1)} %get-tuple-element.10.cos_ref, f32[8,512]{1,0:T(8,128)S(1)} %get-tuple-element.9.sin_ref), custom_call_target="tpu_custom_call" | custom-call | tf_op jit(solution)/shard_map/pallas_call | solution.py:459
  47.1 0.6 copy-done.4
  47.7 0.7 and_select_fusion.4
  48.5 0.9 copy-done.2
  49.4 0.7 copy-done.5
  50.1 1.3 %shard_map.102 = f32[512,128]{1,0:T(8,128)S(1)} custom-call(s32[64]{0:T(128)S(1)} %select_reduce_fusion.inv_ref, f32[16,4,8,256]{3,2,1,0:T(8,128)S(1)} %all-to-all-done.x_ref, bf16[384,256]{1,0:T(8,128)(2,1)S(1)} %copy-done.2, f32[8,512]{1,0:T(8,128)S(1)} %get-tuple-element.10.cos_ref, f32[8,512]{1,0:T(8,128)S(1)} %get-tuple-element.9.sin_ref, ...), custom_call_target="tpu_custom_call" | custom-call | tf_op jit(solution)/shard_map/pallas_call | solution.py:475
  51.4 16.0 %all_to_all.26 = f32[32,16,128]{2,1,0:T(8,128)S(1)} all-to-all(f32[32,16,128]{2,1,0:T(8,128)S(1)} %bitcast.14), channel_id=1, replica_groups=mesh['box'=32,'dir'=16] {'box'}, dimensions={0} | all-to-all | bytes 524288 | tf_op jit(solution)/shard_map/all_to_all | solution.py:486
  67.4 7.3 %shard_map.103 = f32[16,2,8,128]{3,2,1,0:T(8,128)S(1)} custom-call(f32[512,128]{1,0:T(8,128)S(1)} %bitcast.15, f32[128,128,128]{2,1,0:T(8,128)} %get-tuple-element.8.m_far), custom_call_target="tpu_custom_call" | custom-call | tf_op jit(solution)/shard_map/pallas_call | solution.py:487
  74.7 9.4 %all_to_all.27.x_ref = f32[16,2,8,128]{3,2,1,0:T(8,128)S(1)} all-to-all(f32[16,2,8,128]{3,2,1,0:T(8,128)S(1)} %shard_map.103), channel_id=1, replica_groups={{0,16,32,48,64,80,96,112,128,144,160,176,192,208,224,240},{256,272,288,..., dimensions={0} | all-to-all | bytes 262144 | tf_op jit(solution)/shard_map/all_to_all | solution.py:500
  84.1 1.3 %shard_map.104 = f32[16,4,8,256]{3,2,1,0:T(8,128)S(1)} custom-call(s32[64]{0:T(128)S(1)} %select_reduce_fusion.inv_ref, f32[16,2,8,128]{3,2,1,0:T(8,128)S(1)} %all_to_all.27.x_ref, bf16[256,256]{1,0:T(8,128)(2,1)S(1)} %copy-done.3, f32[8,512]{1,0:T(8,128)S(1)} %get-tuple-element.10.cos_ref, f32[8,512]{1,0:T(8,128)S(1)} %get-tuple-element.9.sin_ref), custom_call_target="tpu_custom_call" | custom-call | tf_op jit(solution)/shard_map/pallas_call | solution.py:503
  85.5 40.3 %all_to_all.28.y_ref = f32[16,4,8,256]{3,2,1,0:T(8,128)S(1)} all-to-all(f32[16,4,8,256]{3,2,1,0:T(8,128)S(1)} %shard_map.104), channel_id=1, replica_groups=mesh['box'=32,'dir'=16] {'dir'}, dimensions={0} | all-to-all | bytes 1048576 | tf_op jit(solution)/shard_map/all_to_all | solution.py:514
  125.8 1.5 %shard_map.105 = f32[4,8,2048]{2,1,0:T(8,128)} custom-call(f32[16,4,8,256]{3,2,1,0:T(8,128)S(1)} %all_to_all.28.y_ref, f32[8,64,128]{2,1,0:T(8,128)S(1)} %copy-done.1), custom_call_target="tpu_custom_call" | custom-call | tf_op jit(solution)/shard_map/pallas_call | solution.py:515
  (28 shorter events, 0.8 us)
Async XLA Ops:
  0.0 19.9 %copy-start = (f32[316,2,512]{2,1,0:T(2,128)S(1)}, f32[316,2,512]{2,1,0:T(2,128)}, u32[]{:S(2)}) copy-start(f32[316,2,512]{2,1,0:T(2,128)} %param.12) | copy-start | bytes 3883012
  0.0 18.6 %copy-start.7 = (s32[256,189]{0,1:T(8,128)S(1)}, s32[256,189]{0,1:T(8,128)}, u32[]{:S(2)}) copy-start(s32[256,189]{0,1:T(8,128)} %param.13) | copy-start | bytes 580612
  0.0 18.6 %copy-start.6 = (s32[256,189]{0,1:T(8,128)S(1)}, s32[256,189]{0,1:T(8,128)}, u32[]{:S(2)}) copy-start(s32[256,189]{0,1:T(8,128)} %param.14) | copy-start | bytes 580612
  3.4 45.1 %all-to-all-start = ((f32[16,4,8,256]{3,2,1,0:T(8,128)}), f32[16,4,8,256]{3,2,1,0:T(8,128)S(1)}, u32[]{:S(2)}, u32[]{:S(2)}) async-start(f32[16,4,8,256]{3,2,1,0:T(8,128)} %shard_map.100), calls=%async_computation | async-start | bytes 1048576 | tf_op jit(solution)/shard_map/all_to_all | solution.py:440
  47.1 0.6 copy-start.4
  48.5 0.9 copy-start.2
  49.4 0.7 copy-start.5
  67.4 16.7 %copy-start.3 = (bf16[256,256]{1,0:T(8,128)(2,1)S(1)}, bf16[256,256]{1,0:T(8,128)(2,1)}, u32[]{:S(2)}) copy-start(bf16[256,256]{1,0:T(8,128)(2,1)} %constant.129.clone.w_ref) | copy-start | bytes 393220
  74.7 51.1 %copy-start.1 = (f32[8,64,128]{2,1,0:T(8,128)S(1)}, f32[8,64,128]{2,1,0:T(8,128)}, u32[]{:S(2)}) copy-start(f32[8,64,128]{2,1,0:T(8,128)} %constant.127.clone.c_ref) | copy-start | bytes 786436

commit v9 on v8

--- a/solution.py
+++ b/solution.py
@@ -224,12 +224,37 @@
 
 
 def matrix_kernel(
-    partner_ref, kind_ref, table_ref, cos_ref, sin_ref, o_ref, token_ref, both_ref, picked_ref
+    partner_ref,
+    kind_ref,
+    place_ref,
+    whole_far,
+    cos_ref,
+    sin_ref,
+    o_ref,
+    token_ref,
+    both_ref,
+    picked_ref,
+    whole_ref,
+    table_ref,
+    arrived,
 ):
     @pl.when(pl.program_id(0) == 0)
     def _():
+        chunk = place_ref[64]
+        lanes = pl.ds(pl.multiple_of(chunk // 4 * LANES, LANES), LANES)
+        copy = pltpu.make_async_copy(whole_far.at[:, :, lanes], whole_ref, arrived)
+        copy.start()
+        table_ref[...] = jnp.zeros((2 * KINDS, LANES), f32)
+        copy.wait()
+        count = whole_ref.shape[0]
+        turn = chunk % 4 * 32
+        real = pltpu.roll(whole_ref[:, 0, :], (LANES - turn) % LANES, 1)
+        imag = pltpu.roll(whole_ref[:, 1, :], (LANES + 32 - turn) % LANES, 1)
+        lane = lax.broadcasted_iota(jnp.int32, (count, LANES), 1)
+        table_ref[pl.ds(0, count), :] = jnp.where(lane < 32, real, imag)
         low_half = lax.broadcasted_iota(jnp.int32, (KINDS, LANES), 1) < PF
-        high, low = (v.astype(f32) for v in split(table_ref[...]))
+        table = jnp.where(low_half, table_ref[:KINDS], swap_halves(table_ref[KINDS:]))
+        high, low = (v.astype(f32) for v in split(table))
         both_ref[:, :LANES] = jnp.where(low_half, high, swap_halves(low)).astype(bf16)
         both_ref[:, LANES:] = jnp.where(low_half, swap_halves(high), low).astype(bf16)
         token_ref[...] = jnp.zeros((8, LANES), f32)
@@ -448,29 +473,33 @@
     rows = jnp.pad(jnp.where(live, rows, -1), pad, constant_values=-1)
     kinds = jnp.pad(kinds, pad, constant_values=-1)
     kinds = kinds.reshape(TARGETS // 8, 8, SLOTS).transpose(0, 2, 1)
-    table = lax.dynamic_slice_in_dim(translator, chunk * CHUNK, CHUNK, 2)
-    table = table.reshape(table.shape[0], 2 * CHUNK)
-    table = jnp.pad(table, ((0, 2 * KINDS - table.shape[0]), (0, 0)))
-    table = jnp.concatenate([table[:KINDS], table[KINDS:]], 1)
     cos_table, sin_table = phase_tables(dir_index)
     place = jnp.arange(64, dtype=jnp.int32)
     found = fine_slot[None, :] % 64 == place[:, None]
     inverse = jnp.sum(jnp.where(found, place[None, :], 0), 1)
+    inverse = jnp.concatenate([inverse, jnp.full((8,), chunk, jnp.int32)])
     matrix, token = pl.pallas_call(
         matrix_kernel,
         grid=(TARGETS // 8,),
         in_specs=[
             pl.BlockSpec((8, SLOTS), lambda i: (i, 0)),
             pl.BlockSpec((1, SLOTS, 8), lambda i: (i, 0, 0)),
-            pl.BlockSpec((KINDS, LANES), lambda i: (0, 0)),
+            smem,
+            hbm,
             vmem,
             vmem,
         ],
         out_specs=[pl.BlockSpec((8, LANES, LANES), lambda i: (i, 0, 0)), vmem],
         out_shape=[pltpu.HBM((TARGETS, LANES, LANES), f32), near(8, LANES)],
-        scratch_shapes=[pltpu.VMEM((KINDS, 256), bf16), pltpu.VMEM((8 * SLOTS, LANES), bf16)],
+        scratch_shapes=[
+            pltpu.VMEM((KINDS, 256), bf16),
+            pltpu.VMEM((8 * SLOTS, LANES), bf16),
+            pltpu.VMEM((translator.shape[0], 2, LANES), f32),
+            pltpu.VMEM((2 * KINDS, LANES), f32),
+            pltpu.SemaphoreType.DMA,
+        ],
         compiler_params=grant(16),
-    )(rows, kinds, table, hold(cos_table), hold(sin_table))
+    )(rows, kinds, inverse, far(translator), hold(cos_table), hold(sin_table))
 
     packed = pl.pallas_call(
         gather_kernel,

time: 128 us -> 120 us (0.938)
  local copies, waits for them, and re-layouts: 9.76 us -> 0.84 us
  waiting for transfers between devices: 0.01 us -> 5.52 us
  blocking collectives: 65.8 us -> 60.6 us
  Pallas kernels: 34.1 us -> 36.1 us
  other arithmetic: 2.27 us -> 0.61 us
    all_to_all x1, waiting for transfers between devices: 0.01 us -> 5.52 us  [body(): lax.all_to_all(sent, 'dir', split_axis=0, concat_axis=0, tiled=True)]
    all_to_all x1, blocking collectives: 40.3 us -> 35.2 us  [body(): lax.all_to_all(lowered, 'dir', split_axis=0, concat_axis=0, tiled=True)]
    unnamed x19 -> x16, local copies, waits for them, and re-layouts: 4.41 us -> 0.23 us
    pallas_call x1, Pallas kernels: 19.3 us -> 21.4 us  [body(): pl.pallas_call(matrix_kernel, grid=(TARGETS // 8,), in_specs=[pl.BlockSpe...]
    dynamic_slice x2 -> x1, local copies, waits for them, and re-layouts: 1.78 us -> 0.02 us  [body(): rows = lax.dynamic_slice_in_dim(list_partner, group * TARGETS, TARGETS, 0)]
    slice x3 -> x0, local copies, waits for them, and re-layouts: 1.53 us -> none  [body(): table = jnp.concatenate([table[:KINDS], table[KINDS:]], 1)]
  transfers between devices with their start and end apart: 1 -> 1, of which waited for: 0 -> 1; matrix products, arithmetic and copies ran while one was open for 8% -> 1% of each run, Pallas kernels for 15% -> 18%
where the time goes in v9:
time: 120 us; the launch traced here: 119 us
  blocking collectives  60.6 us (50%)
  Pallas kernels  36.1 us (30%)
  starting transfers between devices  15.2 us (13%)
  waiting for transfers between devices  5.52 us (5%)
    all_to_all x1, blocking collectives, body(): lax.all_to_all(lowered, 'dir', split_axis=0, concat_axis=0, tiled=True)  35.2 us
    pallas_call x1, Pallas kernels, body(): pl.pallas_call(matrix_kernel, grid=(TARGETS // 8,), in_specs=[pl.BlockSpe...  21.4 us
    all_to_all x1, blocking collectives, body(): lax.all_to_all(packed, 'box', split_axis=0, concat_axis=0, tiled=True)  16 us
    all_to_all x1, starting transfers between devices, body(): lax.all_to_all(sent, 'dir', split_axis=0, concat_axis=0, tiled=True)  15.2 us
    all_to_all x1, blocking collectives, body(): lax.all_to_all(incoming, 'box', split_axis=0, concat_axis=0, axis_index_g...  9.4 us
    pallas_call x1, Pallas kernels, body(): pl.pallas_call(translate_kernel, in_specs=[vmem, hbm], out_specs=vmem, ou...  7.26 us
    all_to_all x1, waiting for transfers between devices, body(): lax.all_to_all(sent, 'dir', split_axis=0, concat_axis=0, tiled=True)  5.52 us
    pallas_call x1, Pallas kernels, body(): pl.pallas_call(theta_up_kernel, out_shape=pltpu.HBM((16, 4, 8, 256), f32)...  3.29 us
  transfers between devices with their start and end apart: 1, of which 1 were waited for; matrix products, arithmetic and copies ran while one was open for 1% of the time, Pallas kernels for 18%

profile of v9, /device:TPU:32, one launch (start us, length us, event | category | flops | bytes accessed | tf_op | source)
XLA Modules:
  0.0 119.2 jit_solution(413479152725514749)
XLA Ops:
  0.0 3.3 %shard_map.100 = f32[16,4,8,256]{3,2,1,0:T(8,128)} custom-call(f32[4,8,2048]{2,1,0:T(8,128)} %x_far.1, f32[16,32,128]{2,1,0:T(8,128)} %constant.121.clone.c_far), custom_call_target="tpu_custom_call" | custom-call | tf_op jit(solution)/shard_map/pallas_call | solution.py:449
  3.3 15.2 %all-to-all-start = ((f32[16,4,8,256]{3,2,1,0:T(8,128)}), f32[16,4,8,256]{3,2,1,0:T(8,128)S(1)}, u32[]{:S(2)}, u32[]{:S(2)}) async-start(f32[16,4,8,256]{3,2,1,0:T(8,128)} %shard_map.100), calls=%async_computation | async-start | bytes 1048576 | tf_op jit(solution)/shard_map/all_to_all | solution.py:465
  18.6 0.0 copy-start.6
  18.6 0.1 copy.19
  18.7 0.5 copy.17
  19.2 0.1 copy.18
  19.4 0.1 dynamic_slice.9
  19.4 0.1 fusion
  19.5 0.0 copy-start.1
  19.6 0.1 select_reduce_fusion
  19.8 0.1 add_bitcast_fusion
  19.9 0.1 multiply_bitcast_fusion.1
  20.0 0.1 fusion.1
  20.1 21.4 %shard_map.101 = (f32[128,128,128]{2,1,0:T(8,128)}, f32[8,128]{1,0:T(8,128)S(1)}) custom-call(s32[128,192]{1,0:T(8,128)S(1)} %pad.8.partner_ref, s32[16,192,8]{2,1,0:T(8,128)S(1)} %bitcast.11, s32[72]{0:T(128)S(1)} %concatenate.3.place_ref.inv_ref, f32[316,2,512]{2,1,0:T(2,128)} %whole_far.1, f32[8,512]{1,0:T(8,128)S(1)} %get-tuple-element.10.cos_ref, ...), custom_call_target="tpu_custom_call" | custom-call | tf_op jit(solution)/shard_map/pallas_call | solution.py:481
  41.5 5.5 %all-to-all-done.x_ref = f32[16,4,8,256]{3,2,1,0:T(8,128)S(1)} async-done(((f32[16,4,8,256]{3,2,1,0:T(8,128)}), f32[16,4,8,256]{3,2,1,0:T(8,128)S(1)}, u32[]{:S(2)}, u32[]{:S(2)}) %all-to-all-start) | async-done | bytes 524320 | tf_op jit(solution)/shard_map/all_to_all | solution.py:465
  47.0 1.3 %shard_map.102 = f32[512,128]{1,0:T(8,128)S(1)} custom-call(s32[72]{0:T(128)S(1)} %concatenate.3.place_ref.inv_ref, f32[16,4,8,256]{3,2,1,0:T(8,128)S(1)} %all-to-all-done.x_ref, bf16[384,256]{1,0:T(8,128)(2,1)S(1)} %copy-done.1, f32[8,512]{1,0:T(8,128)S(1)} %get-tuple-element.10.cos_ref, f32[8,512]{1,0:T(8,128)S(1)} %get-tuple-element.9.sin_ref, ...), custom_call_target="tpu_custom_call" | custom-call | tf_op jit(solution)/shard_map/pallas_call | solution.py:504
  48.4 16.0 %all_to_all.26 = f32[32,16,128]{2,1,0:T(8,128)S(1)} all-to-all(f32[32,16,128]{2,1,0:T(8,128)S(1)} %bitcast.12), channel_id=1, replica_groups=mesh['box'=32,'dir'=16] {'box'}, dimensions={0} | all-to-all | bytes 524288 | tf_op jit(solution)/shard_map/all_to_all | solution.py:515
  64.4 7.3 %shard_map.103 = f32[16,2,8,128]{3,2,1,0:T(8,128)S(1)} custom-call(f32[512,128]{1,0:T(8,128)S(1)} %bitcast.13, f32[128,128,128]{2,1,0:T(8,128)} %get-tuple-element.8.m_far), custom_call_target="tpu_custom_call" | custom-call | tf_op jit(solution)/shard_map/pallas_call | solution.py:516
  71.7 0.0 copy-start
  71.7 9.4 %all_to_all.27.x_ref = f32[16,2,8,128]{3,2,1,0:T(8,128)S(1)} all-to-all(f32[16,2,8,128]{3,2,1,0:T(8,128)S(1)} %shard_map.103), channel_id=1, replica_groups={{0,16,32,48,64,80,96,112,128,144,160,176,192,208,224,240},{256,272,288,..., dimensions={0} | all-to-all | bytes 262144 | tf_op jit(solution)/shard_map/all_to_all | solution.py:529
  81.1 0.0 copy-done.2
  81.1 1.3 %shard_map.104 = f32[16,4,8,256]{3,2,1,0:T(8,128)S(1)} custom-call(s32[72]{0:T(128)S(1)} %concatenate.3.place_ref.inv_ref, f32[16,2,8,128]{3,2,1,0:T(8,128)S(1)} %all_to_all.27.x_ref, bf16[256,256]{1,0:T(8,128)(2,1)S(1)} %copy-done.2, f32[8,512]{1,0:T(8,128)S(1)} %get-tuple-element.10.cos_ref, f32[8,512]{1,0:T(8,128)S(1)} %get-tuple-element.9.sin_ref), custom_call_target="tpu_custom_call" | custom-call | tf_op jit(solution)/shard_map/pallas_call | solution.py:532
  82.4 35.2 %all_to_all.28.y_ref = f32[16,4,8,256]{3,2,1,0:T(8,128)S(1)} all-to-all(f32[16,4,8,256]{3,2,1,0:T(8,128)S(1)} %shard_map.104), channel_id=1, replica_groups=mesh['box'=32,'dir'=16] {'dir'}, dimensions={0} | all-to-all | bytes 1048576 | tf_op jit(solution)/shard_map/all_to_all | solution.py:543
  117.6 1.5 %shard_map.105 = f32[4,8,2048]{2,1,0:T(8,128)} custom-call(f32[16,4,8,256]{3,2,1,0:T(8,128)S(1)} %all_to_all.28.y_ref, f32[8,64,128]{2,1,0:T(8,128)S(1)} %copy-done), custom_call_target="tpu_custom_call" | custom-call | tf_op jit(solution)/shard_map/pallas_call | solution.py:544
  (20 shorter events, 0.2 us)
Async XLA Ops:
  0.0 18.6 %copy-start.3 = (s32[256,189]{0,1:T(8,128)S(1)}, s32[256,189]{0,1:T(8,128)}, u32[]{:S(2)}) copy-start(s32[256,189]{0,1:T(8,128)} %param.13) | copy-start | bytes 580612
  0.0 18.6 %copy-start.4 = (s32[256,189]{0,1:T(8,128)S(1)}, s32[256,189]{0,1:T(8,128)}, u32[]{:S(2)}) copy-start(s32[256,189]{0,1:T(8,128)} %param.14) | copy-start | bytes 580612
  3.3 43.7 %all-to-all-start = ((f32[16,4,8,256]{3,2,1,0:T(8,128)}), f32[16,4,8,256]{3,2,1,0:T(8,128)S(1)}, u32[]{:S(2)}, u32[]{:S(2)}) async-start(f32[16,4,8,256]{3,2,1,0:T(8,128)} %shard_map.100), calls=%async_computation | async-start | bytes 1048576 | tf_op jit(solution)/shard_map/all_to_all | solution.py:465
  18.5 0.8 copy-start.5
  18.6 1.0 copy-start.6
  19.5 27.5 %copy-start.1 = (bf16[384,256]{1,0:T(8,128)(2,1)S(1)}, bf16[384,256]{1,0:T(8,128)(2,1)}, u32[]{:S(2)}) copy-start(bf16[384,256]{1,0:T(8,128)(2,1)} %constant.123.clone.w_ref) | copy-start | bytes 589828
  64.4 16.7 %copy-start.2 = (bf16[256,256]{1,0:T(8,128)(2,1)S(1)}, bf16[256,256]{1,0:T(8,128)(2,1)}, u32[]{:S(2)}) copy-start(bf16[256,256]{1,0:T(8,128)(2,1)} %constant.124.clone.w_ref) | copy-start | bytes 393220
  71.7 46.0 %copy-start = (f32[8,64,128]{2,1,0:T(8,128)S(1)}, f32[8,64,128]{2,1,0:T(8,128)}, u32[]{:S(2)}) copy-start(f32[8,64,128]{2,1,0:T(8,128)} %constant.122.clone.c_ref) | copy-start | bytes 786436

commit v10 on v9

--- a/solution.py
+++ b/solution.py
@@ -299,7 +299,7 @@
     return parts[0]
 
 
-def translate_kernel(s_ref, m_far, o_ref, wide_ref, m_ref, arrived):
+def translate_kernel(s_ref, m_far, o_ref, wide_ref, m_ref, sums_ref, arrived):
     low_half = lane_quarter() < 2
     row = lax.broadcasted_iota(jnp.int32, (8, LANES), 0)
     top = row < 4
@@ -334,6 +334,12 @@
                 t = m + swap_halves(m)
                 for k in range(6):
                     sums[p][k] = sums[p][k] + source[k] * (m if k < 4 else t)
+        for p in range(4):
+            for k in range(6):
+                sums_ref[g, p, k] = sums[p][k]
+
+    def finish(g):
+        sums = [[sums_ref[g, p, k] for k in range(6)] for p in range(4)]
         plain = [fold_rows(sums[0][:4] + sums[1][:4]), fold_rows(sums[2][:4] + sums[3][:4])]
         mixed = fold_rows(sums[0][4:] + sums[2][4:] + sums[1][4:] + sums[3][4:])
         turned = swap_halves(mixed)
@@ -355,13 +361,19 @@
         o_ref[g // 2, g % 2] = out
 
     def step(q, carry):
-        fetch(2 * q).wait()
-        fetch(2 * q + 1).wait()
-        for k in range(4):
-            four_targets(4 * q + k)
-        return carry
-
-    lax.fori_loop(0, TARGETS // 16, step, 0)
+        fetch(q).wait()
+        for k in range(2):
+            four_targets(2 * q + k)
+        return carry
+
+    lax.fori_loop(0, TARGETS // 8, step, 0)
+
+    def last(q, carry):
+        for k in range(16):
+            finish(16 * q + k)
+        return carry
+
+    lax.fori_loop(0, TARGETS // 64, last, 0)
 
 
 def scatter_kernel(inv_ref, x_ref, w_ref, cos_ref, sin_ref, o_ref, plain_ref, child_ref):
@@ -521,6 +533,7 @@
         scratch_shapes=[
             pltpu.VMEM((16, 6, 8, LANES), f32),
             pltpu.VMEM((TARGETS, LANES, LANES), f32),
+            pltpu.VMEM((TARGETS // 4, 4, 6, 8, LANES), f32),
             pltpu.SemaphoreType.DMA((TARGETS // 8,)),
         ],
         compiler_params=grant(16),

time: 120 us -> 118 us (0.983)
  Pallas kernels: 36.1 us -> 34.5 us
    pallas_call x1, Pallas kernels: 7.26 us -> 5.66 us  [body(): pl.pallas_call(translate_kernel, in_specs=[vmem, hbm], out_specs=vmem, ou...]
where the time goes in v10:
time: 118 us
  blocking collectives  60.6 us (51%)
  Pallas kernels  34.5 us (29%)
  starting transfers between devices  15.2 us (13%)
  waiting for transfers between devices  5.52 us (5%)
    all_to_all x1, blocking collectives, body(): lax.all_to_all(lowered, 'dir', split_axis=0, concat_axis=0, tiled=True)  35.2 us
    pallas_call x1, Pallas kernels, body(): pl.pallas_call(matrix_kernel, grid=(TARGETS // 8,), in_specs=[pl.BlockSpe...  21.4 us
    all_to_all x1, blocking collectives, body(): lax.all_to_all(packed, 'box', split_axis=0, concat_axis=0, tiled=True)  16 us
    all_to_all x1, starting transfers between devices, body(): lax.all_to_all(sent, 'dir', split_axis=0, concat_axis=0, tiled=True)  15.2 us
    all_to_all x1, blocking collectives, body(): lax.all_to_all(incoming, 'box', split_axis=0, concat_axis=0, axis_index_g...  9.4 us
    pallas_call x1, Pallas kernels, body(): pl.pallas_call(translate_kernel, in_specs=[vmem, hbm], out_specs=vmem, ou...  5.66 us
    all_to_all x1, waiting for transfers between devices, body(): lax.all_to_all(sent, 'dir', split_axis=0, concat_axis=0, tiled=True)  5.52 us
    pallas_call x1, Pallas kernels, body(): pl.pallas_call(theta_up_kernel, out_shape=pltpu.HBM((16, 4, 8, 256), f32)...  3.29 us
  transfers between devices with their start and end apart: 1, of which 1 were waited for; matrix products, arithmetic and copies ran while one was open for 1% of the time, Pallas kernels for 18%

profile of v10, /device:TPU:32, one launch (start us, length us, event | category | flops | bytes accessed | tf_op | source)
XLA Modules:
  0.0 117.6 jit_solution(12120364323586740918)
XLA Ops:
  0.0 3.3 %shard_map.100 = f32[16,4,8,256]{3,2,1,0:T(8,128)} custom-call(f32[4,8,2048]{2,1,0:T(8,128)} %x_far.1, f32[16,32,128]{2,1,0:T(8,128)} %constant.121.clone.c_far), custom_call_target="tpu_custom_call" | custom-call | tf_op jit(solution)/shard_map/pallas_call | solution.py:461
  3.3 15.2 %all-to-all-start = ((f32[16,4,8,256]{3,2,1,0:T(8,128)}), f32[16,4,8,256]{3,2,1,0:T(8,128)S(1)}, u32[]{:S(2)}, u32[]{:S(2)}) async-start(f32[16,4,8,256]{3,2,1,0:T(8,128)} %shard_map.100), calls=%async_computation | async-start | bytes 1048576 | tf_op jit(solution)/shard_map/all_to_all | solution.py:477
  18.6 0.0 copy-start.6
  18.6 0.1 copy.19
  18.7 0.5 copy.17
  19.2 0.1 copy.18
  19.4 0.1 dynamic_slice.9
  19.4 0.1 fusion
  19.5 0.0 copy-start.1
  19.6 0.1 select_reduce_fusion
  19.8 0.1 add_bitcast_fusion
  19.9 0.1 multiply_bitcast_fusion.1
  20.0 0.1 fusion.1
  20.1 21.4 %shard_map.101 = (f32[128,128,128]{2,1,0:T(8,128)}, f32[8,128]{1,0:T(8,128)S(1)}) custom-call(s32[128,192]{1,0:T(8,128)S(1)} %pad.8.partner_ref, s32[16,192,8]{2,1,0:T(8,128)S(1)} %bitcast.11, s32[72]{0:T(128)S(1)} %concatenate.3.place_ref.inv_ref, f32[316,2,512]{2,1,0:T(2,128)} %whole_far.1, f32[8,512]{1,0:T(8,128)S(1)} %get-tuple-element.10.cos_ref, ...), custom_call_target="tpu_custom_call" | custom-call | tf_op jit(solution)/shard_map/pallas_call | solution.py:493
  41.5 5.5 %all-to-all-done.x_ref = f32[16,4,8,256]{3,2,1,0:T(8,128)S(1)} async-done(((f32[16,4,8,256]{3,2,1,0:T(8,128)}), f32[16,4,8,256]{3,2,1,0:T(8,128)S(1)}, u32[]{:S(2)}, u32[]{:S(2)}) %all-to-all-start) | async-done | bytes 524320 | tf_op jit(solution)/shard_map/all_to_all | solution.py:477
  47.0 1.3 %shard_map.102 = f32[512,128]{1,0:T(8,128)S(1)} custom-call(s32[72]{0:T(128)S(1)} %concatenate.3.place_ref.inv_ref, f32[16,4,8,256]{3,2,1,0:T(8,128)S(1)} %all-to-all-done.x_ref, bf16[384,256]{1,0:T(8,128)(2,1)S(1)} %copy-done.1, f32[8,512]{1,0:T(8,128)S(1)} %get-tuple-element.10.cos_ref, f32[8,512]{1,0:T(8,128)S(1)} %get-tuple-element.9.sin_ref, ...), custom_call_target="tpu_custom_call" | custom-call | tf_op jit(solution)/shard_map/pallas_call | solution.py:516
  48.4 16.0 %all_to_all.26 = f32[32,16,128]{2,1,0:T(8,128)S(1)} all-to-all(f32[32,16,128]{2,1,0:T(8,128)S(1)} %bitcast.12), channel_id=1, replica_groups=mesh['box'=32,'dir'=16] {'box'}, dimensions={0} | all-to-all | bytes 524288 | tf_op jit(solution)/shard_map/all_to_all | solution.py:527
  64.4 5.7 %shard_map.103 = f32[16,2,8,128]{3,2,1,0:T(8,128)S(1)} custom-call(f32[512,128]{1,0:T(8,128)S(1)} %bitcast.13, f32[128,128,128]{2,1,0:T(8,128)} %get-tuple-element.8.m_far), custom_call_target="tpu_custom_call" | custom-call | tf_op jit(solution)/shard_map/pallas_call | solution.py:528
  70.1 0.0 copy-start
  70.1 9.4 %all_to_all.27.x_ref = f32[16,2,8,128]{3,2,1,0:T(8,128)S(1)} all-to-all(f32[16,2,8,128]{3,2,1,0:T(8,128)S(1)} %shard_map.103), channel_id=1, replica_groups={{0,16,32,48,64,80,96,112,128,144,160,176,192,208,224,240},{256,272,288,..., dimensions={0} | all-to-all | bytes 262144 | tf_op jit(solution)/shard_map/all_to_all | solution.py:542
  79.5 0.0 copy-done.2
  79.5 1.3 %shard_map.104 = f32[16,4,8,256]{3,2,1,0:T(8,128)S(1)} custom-call(s32[72]{0:T(128)S(1)} %concatenate.3.place_ref.inv_ref, f32[16,2,8,128]{3,2,1,0:T(8,128)S(1)} %all_to_all.27.x_ref, bf16[256,256]{1,0:T(8,128)(2,1)S(1)} %copy-done.2, f32[8,512]{1,0:T(8,128)S(1)} %get-tuple-element.10.cos_ref, f32[8,512]{1,0:T(8,128)S(1)} %get-tuple-element.9.sin_ref), custom_call_target="tpu_custom_call" | custom-call | tf_op jit(solution)/shard_map/pallas_call | solution.py:545
  80.8 35.2 %all_to_all.28.y_ref = f32[16,4,8,256]{3,2,1,0:T(8,128)S(1)} all-to-all(f32[16,4,8,256]{3,2,1,0:T(8,128)S(1)} %shard_map.104), channel_id=1, replica_groups=mesh['box'=32,'dir'=16] {'dir'}, dimensions={0} | all-to-all | bytes 1048576 | tf_op jit(solution)/shard_map/all_to_all | solution.py:556
  116.0 1.5 %shard_map.105 = f32[4,8,2048]{2,1,0:T(8,128)} custom-call(f32[16,4,8,256]{3,2,1,0:T(8,128)S(1)} %all_to_all.28.y_ref, f32[8,64,128]{2,1,0:T(8,128)S(1)} %copy-done), custom_call_target="tpu_custom_call" | custom-call | tf_op jit(solution)/shard_map/pallas_call | solution.py:557
  (20 shorter events, 0.2 us)
Async XLA Ops:
  0.0 18.6 %copy-start.3 = (s32[256,189]{0,1:T(8,128)S(1)}, s32[256,189]{0,1:T(8,128)}, u32[]{:S(2)}) copy-start(s32[256,189]{0,1:T(8,128)} %param.13) | copy-start | bytes 580612
  0.0 18.6 %copy-start.4 = (s32[256,189]{0,1:T(8,128)S(1)}, s32[256,189]{0,1:T(8,128)}, u32[]{:S(2)}) copy-start(s32[256,189]{0,1:T(8,128)} %param.14) | copy-start | bytes 580612
  3.3 43.7 %all-to-all-start = ((f32[16,4,8,256]{3,2,1,0:T(8,128)}), f32[16,4,8,256]{3,2,1,0:T(8,128)S(1)}, u32[]{:S(2)}, u32[]{:S(2)}) async-start(f32[16,4,8,256]{3,2,1,0:T(8,128)} %shard_map.100), calls=%async_computation | async-start | bytes 1048576 | tf_op jit(solution)/shard_map/all_to_all | solution.py:477
  18.5 0.8 copy-start.5
  18.6 1.0 copy-start.6
  19.5 27.5 %copy-start.1 = (bf16[384,256]{1,0:T(8,128)(2,1)S(1)}, bf16[384,256]{1,0:T(8,128)(2,1)}, u32[]{:S(2)}) copy-start(bf16[384,256]{1,0:T(8,128)(2,1)} %constant.123.clone.w_ref) | copy-start | bytes 589828
  64.4 15.1 %copy-start.2 = (bf16[256,256]{1,0:T(8,128)(2,1)S(1)}, bf16[256,256]{1,0:T(8,128)(2,1)}, u32[]{:S(2)}) copy-start(bf16[256,256]{1,0:T(8,128)(2,1)} %constant.124.clone.w_ref) | copy-start | bytes 393220
  70.1 46.0 %copy-start = (f32[8,64,128]{2,1,0:T(8,128)S(1)}, f32[8,64,128]{2,1,0:T(8,128)}, u32[]{:S(2)}) copy-start(f32[8,64,128]{2,1,0:T(8,128)} %constant.122.clone.c_ref) | copy-start | bytes 786436

commit v11 on v10

--- a/solution.py
+++ b/solution.py
@@ -14,6 +14,7 @@
 LANES = 128
 SLOTS = 192
 KINDS = 256
+TABLE_ROWS = 320
 TARGETS = 128
 SOURCES = 256
 CHUNK = 32
@@ -203,7 +204,7 @@
         parent_ref[p] = plain + sign * pltpu.roll(turned, 4, 0)
         return carry
 
-    lax.fori_loop(0, 8, step, 0, unroll=4)
+    lax.fori_loop(0, 8, step, 0, unroll=True)
     top = lax.broadcasted_iota(jnp.int32, (8, LANES), 0) < 4
     for k in range(2):
         for block in range(4):
@@ -242,11 +243,15 @@
     def _():
         chunk = place_ref[64]
         lanes = pl.ds(pl.multiple_of(chunk // 4 * LANES, LANES), LANES)
-        copy = pltpu.make_async_copy(whole_far.at[:, :, lanes], whole_ref, arrived)
+        kinds = whole_far.shape[0]
+        count = whole_ref.shape[0]
+        copy = pltpu.make_async_copy(
+            whole_far.at[:, :, lanes], whole_ref.at[pl.ds(0, kinds)], arrived
+        )
         copy.start()
+        whole_ref[pl.ds(kinds, count - kinds)] = jnp.zeros((count - kinds, 2, LANES), f32)
         table_ref[...] = jnp.zeros((2 * KINDS, LANES), f32)
         copy.wait()
-        count = whole_ref.shape[0]
         turn = chunk % 4 * 32
         real = pltpu.roll(whole_ref[:, 0, :], (LANES - turn) % LANES, 1)
         imag = pltpu.roll(whole_ref[:, 1, :], (LANES + 32 - turn) % LANES, 1)
@@ -393,7 +398,7 @@
             )
         return carry
 
-    lax.fori_loop(0, 8, step, 0, unroll=4)
+    lax.fori_loop(0, 8, step, 0, unroll=True)
     for j in range(2):
         high, low = split(child_ref[:, :, pl.ds(j * 256, 256)].reshape(512, 256))
         part = jnp.dot(high, w_ref[...], preferred_element_type=f32)
@@ -506,7 +511,7 @@
         scratch_shapes=[
             pltpu.VMEM((KINDS, 256), bf16),
             pltpu.VMEM((8 * SLOTS, LANES), bf16),
-            pltpu.VMEM((translator.shape[0], 2, LANES), f32),
+            pltpu.VMEM((TABLE_ROWS, 2, LANES), f32),
             pltpu.VMEM((2 * KINDS, LANES), f32),
             pltpu.SemaphoreType.DMA,
         ],

time: 118 us -> 118 us (level)
  no operation moved by 1% of the time
where the time goes in v11:
time: 118 us; the launch traced here: 117 us
  blocking collectives  60.6 us (51%)
  Pallas kernels  34.3 us (29%)
  starting transfers between devices  15.2 us (13%)
  waiting for transfers between devices  5.55 us (5%)
    all_to_all x1, blocking collectives, body(): lax.all_to_all(lowered, 'dir', split_axis=0, concat_axis=0, tiled=True)  35.2 us
    pallas_call x1, Pallas kernels, body(): pl.pallas_call(matrix_kernel, grid=(TARGETS // 8,), in_specs=[pl.BlockSpe...  21.3 us
    all_to_all x1, blocking collectives, body(): lax.all_to_all(packed, 'box', split_axis=0, concat_axis=0, tiled=True)  16 us
    all_to_all x1, starting transfers between devices, body(): lax.all_to_all(sent, 'dir', split_axis=0, concat_axis=0, tiled=True)  15.2 us
    all_to_all x1, blocking collectives, body(): lax.all_to_all(incoming, 'box', split_axis=0, concat_axis=0, axis_index_g...  9.4 us
    pallas_call x1, Pallas kernels, body(): pl.pallas_call(translate_kernel, in_specs=[vmem, hbm], out_specs=vmem, ou...  5.66 us
    all_to_all x1, waiting for transfers between devices, body(): lax.all_to_all(sent, 'dir', split_axis=0, concat_axis=0, tiled=True)  5.55 us
    pallas_call x1, Pallas kernels, body(): pl.pallas_call(theta_up_kernel, out_shape=pltpu.HBM((16, 4, 8, 256), f32)...  3.29 us
  transfers between devices with their start and end apart: 1, of which 1 were waited for; matrix products, arithmetic and copies ran while one was open for 1% of the time, Pallas kernels for 18%

profile of v11, /device:TPU:32, one launch (start us, length us, event | category | flops | bytes accessed | tf_op | source)
XLA Modules:
  0.0 117.4 jit_solution(2743476374454659454)
XLA Ops:
  0.0 3.3 %shard_map.100 = f32[16,4,8,256]{3,2,1,0:T(8,128)} custom-call(f32[4,8,2048]{2,1,0:T(8,128)} %x_far.1, f32[16,32,128]{2,1,0:T(8,128)} %constant.121.clone.c_far), custom_call_target="tpu_custom_call" | custom-call | tf_op jit(solution)/shard_map/pallas_call | solution.py:466
  3.3 15.2 %all-to-all-start = ((f32[16,4,8,256]{3,2,1,0:T(8,128)}), f32[16,4,8,256]{3,2,1,0:T(8,128)S(1)}, u32[]{:S(2)}, u32[]{:S(2)}) async-start(f32[16,4,8,256]{3,2,1,0:T(8,128)} %shard_map.100), calls=%async_computation | async-start | bytes 1048576 | tf_op jit(solution)/shard_map/all_to_all | solution.py:482
  18.6 0.0 copy-start.6
  18.6 0.1 copy.19
  18.7 0.5 copy.17
  19.2 0.1 copy.18
  19.4 0.1 dynamic_slice.9
  19.4 0.1 fusion
  19.5 0.0 copy-start.1
  19.6 0.1 select_reduce_fusion
  19.8 0.1 add_bitcast_fusion
  19.9 0.1 multiply_bitcast_fusion.1
  20.0 0.1 fusion.1
  20.1 21.3 %shard_map.101 = (f32[128,128,128]{2,1,0:T(8,128)}, f32[8,128]{1,0:T(8,128)S(1)}) custom-call(s32[128,192]{1,0:T(8,128)S(1)} %pad.8.partner_ref, s32[16,192,8]{2,1,0:T(8,128)S(1)} %bitcast.11, s32[72]{0:T(128)S(1)} %concatenate.3.place_ref.inv_ref, f32[316,2,512]{2,1,0:T(2,128)} %whole_far.1, f32[8,512]{1,0:T(8,128)S(1)} %get-tuple-element.10.cos_ref, ...), custom_call_target="tpu_custom_call" | custom-call | tf_op jit(solution)/shard_map/pallas_call | solution.py:498
  41.5 5.5 %all-to-all-done.x_ref = f32[16,4,8,256]{3,2,1,0:T(8,128)S(1)} async-done(((f32[16,4,8,256]{3,2,1,0:T(8,128)}), f32[16,4,8,256]{3,2,1,0:T(8,128)S(1)}, u32[]{:S(2)}, u32[]{:S(2)}) %all-to-all-start) | async-done | bytes 524320 | tf_op jit(solution)/shard_map/all_to_all | solution.py:482
  47.0 1.2 %shard_map.102 = f32[512,128]{1,0:T(8,128)S(1)} custom-call(s32[72]{0:T(128)S(1)} %concatenate.3.place_ref.inv_ref, f32[16,4,8,256]{3,2,1,0:T(8,128)S(1)} %all-to-all-done.x_ref, bf16[384,256]{1,0:T(8,128)(2,1)S(1)} %copy-done.1, f32[8,512]{1,0:T(8,128)S(1)} %get-tuple-element.10.cos_ref, f32[8,512]{1,0:T(8,128)S(1)} %get-tuple-element.9.sin_ref, ...), custom_call_target="tpu_custom_call" | custom-call | tf_op jit(solution)/shard_map/pallas_call | solution.py:521
  48.3 16.0 %all_to_all.26 = f32[32,16,128]{2,1,0:T(8,128)S(1)} all-to-all(f32[32,16,128]{2,1,0:T(8,128)S(1)} %bitcast.12), channel_id=1, replica_groups=mesh['box'=32,'dir'=16] {'box'}, dimensions={0} | all-to-all | bytes 524288 | tf_op jit(solution)/shard_map/all_to_all | solution.py:532
  64.3 5.7 %shard_map.103 = f32[16,2,8,128]{3,2,1,0:T(8,128)S(1)} custom-call(f32[512,128]{1,0:T(8,128)S(1)} %bitcast.13, f32[128,128,128]{2,1,0:T(8,128)} %get-tuple-element.8.m_far), custom_call_target="tpu_custom_call" | custom-call | tf_op jit(solution)/shard_map/pallas_call | solution.py:533
  70.0 0.0 copy-start
  70.0 9.4 %all_to_all.27.x_ref = f32[16,2,8,128]{3,2,1,0:T(8,128)S(1)} all-to-all(f32[16,2,8,128]{3,2,1,0:T(8,128)S(1)} %shard_map.103), channel_id=1, replica_groups={{0,16,32,48,64,80,96,112,128,144,160,176,192,208,224,240},{256,272,288,..., dimensions={0} | all-to-all | bytes 262144 | tf_op jit(solution)/shard_map/all_to_all | solution.py:547
  79.4 0.0 copy-done.2
  79.4 1.3 %shard_map.104 = f32[16,4,8,256]{3,2,1,0:T(8,128)S(1)} custom-call(s32[72]{0:T(128)S(1)} %concatenate.3.place_ref.inv_ref, f32[16,2,8,128]{3,2,1,0:T(8,128)S(1)} %all_to_all.27.x_ref, bf16[256,256]{1,0:T(8,128)(2,1)S(1)} %copy-done.2, f32[8,512]{1,0:T(8,128)S(1)} %get-tuple-element.10.cos_ref, f32[8,512]{1,0:T(8,128)S(1)} %get-tuple-element.9.sin_ref), custom_call_target="tpu_custom_call" | custom-call | tf_op jit(solution)/shard_map/pallas_call | solution.py:550
  80.7 35.2 %all_to_all.28.y_ref = f32[16,4,8,256]{3,2,1,0:T(8,128)S(1)} all-to-all(f32[16,4,8,256]{3,2,1,0:T(8,128)S(1)} %shard_map.104), channel_id=1, replica_groups=mesh['box'=32,'dir'=16] {'dir'}, dimensions={0} | all-to-all | bytes 1048576 | tf_op jit(solution)/shard_map/all_to_all | solution.py:561
  115.9 1.5 %shard_map.105 = f32[4,8,2048]{2,1,0:T(8,128)} custom-call(f32[16,4,8,256]{3,2,1,0:T(8,128)S(1)} %all_to_all.28.y_ref, f32[8,64,128]{2,1,0:T(8,128)S(1)} %copy-done), custom_call_target="tpu_custom_call" | custom-call | tf_op jit(solution)/shard_map/pallas_call | solution.py:562
  (20 shorter events, 0.2 us)
Async XLA Ops:
  0.0 18.6 %copy-start.3 = (s32[256,189]{0,1:T(8,128)S(1)}, s32[256,189]{0,1:T(8,128)}, u32[]{:S(2)}) copy-start(s32[256,189]{0,1:T(8,128)} %param.13) | copy-start | bytes 580612
  0.0 18.6 %copy-start.4 = (s32[256,189]{0,1:T(8,128)S(1)}, s32[256,189]{0,1:T(8,128)}, u32[]{:S(2)}) copy-start(s32[256,189]{0,1:T(8,128)} %param.14) | copy-start | bytes 580612
  3.3 43.7 %all-to-all-start = ((f32[16,4,8,256]{3,2,1,0:T(8,128)}), f32[16,4,8,256]{3,2,1,0:T(8,128)S(1)}, u32[]{:S(2)}, u32[]{:S(2)}) async-start(f32[16,4,8,256]{3,2,1,0:T(8,128)} %shard_map.100), calls=%async_computation | async-start | bytes 1048576 | tf_op jit(solution)/shard_map/all_to_all | solution.py:482
  18.5 0.8 copy-start.5
  18.6 1.0 copy-start.6
  19.5 27.5 %copy-start.1 = (bf16[384,256]{1,0:T(8,128)(2,1)S(1)}, bf16[384,256]{1,0:T(8,128)(2,1)}, u32[]{:S(2)}) copy-start(bf16[384,256]{1,0:T(8,128)(2,1)} %constant.123.clone.w_ref) | copy-start | bytes 589828
  64.3 15.1 %copy-start.2 = (bf16[256,256]{1,0:T(8,128)(2,1)S(1)}, bf16[256,256]{1,0:T(8,128)(2,1)}, u32[]{:S(2)}) copy-start(bf16[256,256]{1,0:T(8,128)(2,1)} %constant.124.clone.w_ref) | copy-start | bytes 393220
  70.0 45.9 %copy-start = (f32[8,64,128]{2,1,0:T(8,128)S(1)}, f32[8,64,128]{2,1,0:T(8,128)}, u32[]{:S(2)}) copy-start(f32[8,64,128]{2,1,0:T(8,128)} %constant.122.clone.c_ref) | copy-start | bytes 786436

commit v12 on v11

--- a/solution.py
+++ b/solution.py
@@ -325,7 +325,7 @@
             wide_ref[b, 4 + h] = jnp.where(low_half, both[h], both[h + 2])
         return carry
 
-    lax.fori_loop(0, 16, spread, 0, unroll=4)
+    lax.fori_loop(0, 16, spread, 0, unroll=True)
 
     def add_pair(v):
         return v + pltpu.roll(v, 96, 1)

time: 118 us -> 118 us (level)
  no operation moved by 1% of the time
where the time goes in v12:
time: 118 us; the launch traced here: 117 us
  blocking collectives  60.6 us (51%)
  Pallas kernels  34.3 us (29%)
  starting transfers between devices  15.2 us (13%)
  waiting for transfers between devices  5.55 us (5%)
    all_to_all x1, blocking collectives, body(): lax.all_to_all(lowered, 'dir', split_axis=0, concat_axis=0, tiled=True)  35.2 us
    pallas_call x1, Pallas kernels, body(): pl.pallas_call(matrix_kernel, grid=(TARGETS // 8,), in_specs=[pl.BlockSpe...  21.3 us
    all_to_all x1, blocking collectives, body(): lax.all_to_all(packed, 'box', split_axis=0, concat_axis=0, tiled=True)  16 us
    all_to_all x1, starting transfers between devices, body(): lax.all_to_all(sent, 'dir', split_axis=0, concat_axis=0, tiled=True)  15.2 us
    all_to_all x1, blocking collectives, body(): lax.all_to_all(incoming, 'box', split_axis=0, concat_axis=0, axis_index_g...  9.4 us
    pallas_call x1, Pallas kernels, body(): pl.pallas_call(translate_kernel, in_specs=[vmem, hbm], out_specs=vmem, ou...  5.66 us
    all_to_all x1, waiting for transfers between devices, body(): lax.all_to_all(sent, 'dir', split_axis=0, concat_axis=0, tiled=True)  5.55 us
    pallas_call x1, Pallas kernels, body(): pl.pallas_call(theta_up_kernel, out_shape=pltpu.HBM((16, 4, 8, 256), f32)...  3.29 us
  transfers between devices with their start and end apart: 1, of which 1 were waited for; matrix products, arithmetic and copies ran while one was open for 1% of the time, Pallas kernels for 18%

profile of v12, /device:TPU:32, one launch (start us, length us, event | category | flops | bytes accessed | tf_op | source)
XLA Modules:
  0.0 117.4 jit_solution(5275886054467407813)
XLA Ops:
  0.0 3.3 %shard_map.100 = f32[16,4,8,256]{3,2,1,0:T(8,128)} custom-call(f32[4,8,2048]{2,1,0:T(8,128)} %x_far.1, f32[16,32,128]{2,1,0:T(8,128)} %constant.121.clone.c_far), custom_call_target="tpu_custom_call" | custom-call | tf_op jit(solution)/shard_map/pallas_call | solution.py:466
  3.3 15.2 %all-to-all-start = ((f32[16,4,8,256]{3,2,1,0:T(8,128)}), f32[16,4,8,256]{3,2,1,0:T(8,128)S(1)}, u32[]{:S(2)}, u32[]{:S(2)}) async-start(f32[16,4,8,256]{3,2,1,0:T(8,128)} %shard_map.100), calls=%async_computation | async-start | bytes 1048576 | tf_op jit(solution)/shard_map/all_to_all | solution.py:482
  18.6 0.0 copy-done.3
  18.6 0.0 copy-start.6
  18.6 0.1 copy.19
  18.7 0.5 copy.17
  19.2 0.1 copy.18
  19.4 0.1 dynamic_slice.9
  19.4 0.1 fusion
  19.5 0.0 copy-start.1
  19.6 0.1 select_reduce_fusion
  19.8 0.1 add_bitcast_fusion
  19.9 0.1 multiply_bitcast_fusion.1
  20.0 0.1 fusion.1
  20.1 21.3 %shard_map.101 = (f32[128,128,128]{2,1,0:T(8,128)}, f32[8,128]{1,0:T(8,128)S(1)}) custom-call(s32[128,192]{1,0:T(8,128)S(1)} %pad.8.partner_ref, s32[16,192,8]{2,1,0:T(8,128)S(1)} %bitcast.11, s32[72]{0:T(128)S(1)} %concatenate.3.place_ref.inv_ref, f32[316,2,512]{2,1,0:T(2,128)} %whole_far.1, f32[8,512]{1,0:T(8,128)S(1)} %get-tuple-element.10.cos_ref, ...), custom_call_target="tpu_custom_call" | custom-call | tf_op jit(solution)/shard_map/pallas_call | solution.py:498
  41.5 5.5 %all-to-all-done.x_ref = f32[16,4,8,256]{3,2,1,0:T(8,128)S(1)} async-done(((f32[16,4,8,256]{3,2,1,0:T(8,128)}), f32[16,4,8,256]{3,2,1,0:T(8,128)S(1)}, u32[]{:S(2)}, u32[]{:S(2)}) %all-to-all-start) | async-done | bytes 524320 | tf_op jit(solution)/shard_map/all_to_all | solution.py:482
  47.0 1.2 %shard_map.102 = f32[512,128]{1,0:T(8,128)S(1)} custom-call(s32[72]{0:T(128)S(1)} %concatenate.3.place_ref.inv_ref, f32[16,4,8,256]{3,2,1,0:T(8,128)S(1)} %all-to-all-done.x_ref, bf16[384,256]{1,0:T(8,128)(2,1)S(1)} %copy-done.1, f32[8,512]{1,0:T(8,128)S(1)} %get-tuple-element.10.cos_ref, f32[8,512]{1,0:T(8,128)S(1)} %get-tuple-element.9.sin_ref, ...), custom_call_target="tpu_custom_call" | custom-call | tf_op jit(solution)/shard_map/pallas_call | solution.py:521
  48.3 16.0 %all_to_all.26 = f32[32,16,128]{2,1,0:T(8,128)S(1)} all-to-all(f32[32,16,128]{2,1,0:T(8,128)S(1)} %bitcast.12), channel_id=1, replica_groups=mesh['box'=32,'dir'=16] {'box'}, dimensions={0} | all-to-all | bytes 524288 | tf_op jit(solution)/shard_map/all_to_all | solution.py:532
  64.3 5.7 %shard_map.103 = f32[16,2,8,128]{3,2,1,0:T(8,128)S(1)} custom-call(f32[512,128]{1,0:T(8,128)S(1)} %bitcast.13, f32[128,128,128]{2,1,0:T(8,128)} %get-tuple-element.8.m_far), custom_call_target="tpu_custom_call" | custom-call | tf_op jit(solution)/shard_map/pallas_call | solution.py:533
  70.0 0.0 copy-start
  70.0 9.4 %all_to_all.27.x_ref = f32[16,2,8,128]{3,2,1,0:T(8,128)S(1)} all-to-all(f32[16,2,8,128]{3,2,1,0:T(8,128)S(1)} %shard_map.103), channel_id=1, replica_groups={{0,16,32,48,64,80,96,112,128,144,160,176,192,208,224,240},{256,272,288,..., dimensions={0} | all-to-all | bytes 262144 | tf_op jit(solution)/shard_map/all_to_all | solution.py:547
  79.4 1.3 %shard_map.104 = f32[16,4,8,256]{3,2,1,0:T(8,128)S(1)} custom-call(s32[72]{0:T(128)S(1)} %concatenate.3.place_ref.inv_ref, f32[16,2,8,128]{3,2,1,0:T(8,128)S(1)} %all_to_all.27.x_ref, bf16[256,256]{1,0:T(8,128)(2,1)S(1)} %copy-done.2, f32[8,512]{1,0:T(8,128)S(1)} %get-tuple-element.10.cos_ref, f32[8,512]{1,0:T(8,128)S(1)} %get-tuple-element.9.sin_ref), custom_call_target="tpu_custom_call" | custom-call | tf_op jit(solution)/shard_map/pallas_call | solution.py:550
  80.7 35.2 %all_to_all.28.y_ref = f32[16,4,8,256]{3,2,1,0:T(8,128)S(1)} all-to-all(f32[16,4,8,256]{3,2,1,0:T(8,128)S(1)} %shard_map.104), channel_id=1, replica_groups=mesh['box'=32,'dir'=16] {'dir'}, dimensions={0} | all-to-all | bytes 1048576 | tf_op jit(solution)/shard_map/all_to_all | solution.py:561
  115.9 1.5 %shard_map.105 = f32[4,8,2048]{2,1,0:T(8,128)} custom-call(f32[16,4,8,256]{3,2,1,0:T(8,128)S(1)} %all_to_all.28.y_ref, f32[8,64,128]{2,1,0:T(8,128)S(1)} %copy-done), custom_call_target="tpu_custom_call" | custom-call | tf_op jit(solution)/shard_map/pallas_call | solution.py:562
  (20 shorter events, 0.2 us)
Async XLA Ops:
  0.0 18.6 %copy-start.3 = (s32[256,189]{0,1:T(8,128)S(1)}, s32[256,189]{0,1:T(8,128)}, u32[]{:S(2)}) copy-start(s32[256,189]{0,1:T(8,128)} %param.13) | copy-start | bytes 580612
  0.0 18.6 %copy-start.4 = (s32[256,189]{0,1:T(8,128)S(1)}, s32[256,189]{0,1:T(8,128)}, u32[]{:S(2)}) copy-start(s32[256,189]{0,1:T(8,128)} %param.14) | copy-start | bytes 580612
  3.3 43.7 %all-to-all-start = ((f32[16,4,8,256]{3,2,1,0:T(8,128)}), f32[16,4,8,256]{3,2,1,0:T(8,128)S(1)}, u32[]{:S(2)}, u32[]{:S(2)}) async-start(f32[16,4,8,256]{3,2,1,0:T(8,128)} %shard_map.100), calls=%async_computation | async-start | bytes 1048576 | tf_op jit(solution)/shard_map/all_to_all | solution.py:482
  18.5 0.8 copy-start.5
  18.6 1.0 copy-start.6
  19.5 27.5 %copy-start.1 = (bf16[384,256]{1,0:T(8,128)(2,1)S(1)}, bf16[384,256]{1,0:T(8,128)(2,1)}, u32[]{:S(2)}) copy-start(bf16[384,256]{1,0:T(8,128)(2,1)} %constant.123.clone.w_ref) | copy-start | bytes 589828
  64.3 15.1 %copy-start.2 = (bf16[256,256]{1,0:T(8,128)(2,1)S(1)}, bf16[256,256]{1,0:T(8,128)(2,1)}, u32[]{:S(2)}) copy-start(bf16[256,256]{1,0:T(8,128)(2,1)} %constant.124.clone.w_ref) | copy-start | bytes 393220
  70.0 45.9 %copy-start = (f32[8,64,128]{2,1,0:T(8,128)S(1)}, f32[8,64,128]{2,1,0:T(8,128)}, u32[]{:S(2)}) copy-start(f32[8,64,128]{2,1,0:T(8,128)} %constant.122.clone.c_ref) | copy-start | bytes 786436
